TPU v7x, 32 devices: a whole 2x2x4 slice. The times are simulated.
32 devices in a mesh: seq: 2 (over y), group: 8 (over z, x), replica: 2 (over core).
Axes of the slice: x: 2, y: 2, z: 4, core: 2. Of those that a mesh axis runs over, the one named last changes fastest.
Arguments:
- tokens: bfloat16 [16, 1024, 1024], P(('group', 'replica'), 'seq'), may hold values from -6 to 6
- ffn_in: bfloat16 [2, 1024, 4096], P(None, 'group'), may hold values from -0.1875 to 0.1875
- ffn_out: bfloat16 [2, 4096, 1024], P(None, 'group'), may hold values from -0.09375 to 0.09375
- qkv: bfloat16 [3, 1024, 1024], P(None, 'group'), may hold values from -0.1875 to 0.1875
- attn_out: bfloat16 [1024, 1024], P('group'), may hold values from -1.5 to 1.5
- conv_in: bfloat16 [1024, 2048], P('group'), may hold values from -0.1875 to 0.1875
- conv_out: bfloat16 [1024, 1024], P('group'), may hold values from -0.1875 to 0.1875
- depthwise: bfloat16 [31, 1024], P(None, 'group'), may hold values from -1 to 1
- gains: bfloat16 [6, 1024], P(None, 'group'), may hold values from 0.5 to 1.5
- rel_table: bfloat16 [73, 64], replicated, may hold values from -6 to 6
- cotangent: bfloat16 [16, 1024, 1024], P(('group', 'replica'), 'seq'), may hold values from -6 to 6
Outputs:
- output: bfloat16 [16, 1024, 1024], P(('group', 'replica'), 'seq')
- input_grad: bfloat16 [16, 1024, 1024], P(('group', 'replica'), 'seq')
- grad_ffn_in: float32 [2, 1024, 4096], P(None, 'group')
- grad_ffn_out: float32 [2, 4096, 1024], P(None, 'group')
- grad_qkv: float32 [3, 1024, 1024], P(None, 'group')
- grad_attn_out: float32 [1024, 1024], P('group')
- grad_conv_in: float32 [1024, 2048], P('group')
- grad_conv_out: float32 [1024, 1024], P('group')
- grad_depthwise: float32 [31, 1024], P(None, 'group')
- grad_gains: float32 [6, 1024], P(None, 'group')
- grad_rel_table: float32 [73, 64], replicated
- stats: float32 [5], replicated
All inputs are finite; a program needn't handle non-finite values.
Results may differ from a plain program's by a relative error of at most 0.023.
Values may be sent and summed in bfloat16 or wider, within the bound.
A program may use at most 320 MiB of HBM per device.

v0:
```python
import jax
import jax.numpy as jnp
from jax import lax
from jax.sharding import PartitionSpec as P

HEADS = 16
HEAD_DIM = 64
KERNEL = 31
LEFT = 64
RIGHT = 8
WIN = 73
CLIP_LEN = 1024


EPSILON = 1e-05
NEGATIVE = -1e30


def from_behind(value, axis, steps):
    count = lax.axis_size(axis)
    initial, last = (max(0, -steps), min(count, count - steps))
    return lax.ppermute(value, axis, [(source, source + steps) for source in range(initial, last)])


def norm_forward(values, gain):
    centered = values - jnp.mean(values, -1, keepdims=True)
    inverse = lax.rsqrt(jnp.mean(centered * centered, -1, keepdims=True) + EPSILON)
    normal = centered * inverse
    return (normal * gain, normal, inverse)


def norm_backward(grad_out, normal, inverse, gain):
    grad_normal = grad_out * gain
    grad_in = inverse * (
        grad_normal
        - jnp.mean(grad_normal, -1, keepdims=True)
        - normal * jnp.mean(grad_normal * normal, -1, keepdims=True)
    )
    grad_gain = jnp.sum(grad_out * normal, 0)
    return (grad_in, grad_gain)


def matmul(left, right):
    return jnp.dot(left, right, preferred_element_type=jnp.float32)


def matmul_left_t(left, right):
    return lax.dot_general(
        left, right, (((0,), (0,)), ((), ())), preferred_element_type=jnp.float32
    )


def matmul_right_t(left, right):
    return lax.dot_general(
        left, right, (((1,), (1,)), ((), ())), preferred_element_type=jnp.float32
    )


def swish_grad(values):
    logistic = jax.nn.sigmoid(values)
    return logistic + values * logistic * (1.0 - logistic)


def skew(relative, span):
    rows = relative.shape[-2]
    lead = relative.shape[:-2]
    padded = jnp.pad(relative, [(0, 0)] * len(lead) + [(0, 0), (0, span + 1 - relative.shape[-1])])
    flat = padded.reshape(lead + (rows * (span + 1),))[..., : rows * span]
    return flat.reshape(lead + (rows, span))


def unskew(grid, width):
    rows, span = (grid.shape[-2], grid.shape[-1])
    lead = grid.shape[:-2]
    flat = grid.reshape(lead + (rows * span,))
    flat = jnp.pad(flat, [(0, 0)] * len(lead) + [(0, rows)])
    return flat.reshape(lead + (rows, span + 1))[..., :width]


def window_mask(rows, first):
    span = LEFT + rows + RIGHT
    row_ids = lax.broadcasted_iota(jnp.int32, (rows, span), 0)
    col_ids = lax.broadcasted_iota(jnp.int32, (rows, span), 1)
    offset = col_ids - row_ids
    place = first + col_ids - LEFT
    return (offset >= 0) & (offset < WIN) & (place >= 0) & (place < CLIP_LEN)


def attend_scores(query, keys, table, mask):
    scale = HEAD_DIM ** (-0.5)
    direct = jnp.einsum("cshd,cuhd->chsu", query, keys, preferred_element_type=jnp.float32)
    relative = jnp.einsum("cshd,wd->chsw", query, table, preferred_element_type=jnp.float32)
    raw = (direct + skew(relative, keys.shape[1])) * scale
    return jnp.where(mask, raw, NEGATIVE)


def feed_forward(resid, gain, w_in, w_out):
    normed, normal, inverse = norm_forward(resid, gain)
    entry = normed.astype(jnp.bfloat16)
    hidden_pre = matmul(entry, w_in)
    hidden = (hidden_pre * jax.nn.sigmoid(hidden_pre)).astype(jnp.bfloat16)
    return (matmul(hidden, w_out), (normal, inverse, entry, hidden_pre, hidden))


def feed_back(grad_branch, kept, gain, w_in, w_out):
    normal, inverse, entry, hidden_pre, hidden = kept
    grad_low = grad_branch.astype(jnp.bfloat16)
    grad_w_out = matmul_left_t(hidden, grad_low)
    grad_hidden = (matmul_right_t(grad_low, w_out) * swish_grad(hidden_pre)).astype(jnp.bfloat16)
    grad_w_in = matmul_left_t(entry, grad_hidden)
    grad_in, grad_gain = norm_backward(matmul_right_t(grad_hidden, w_in), normal, inverse, gain)
    return (grad_in, grad_gain, grad_w_in, grad_w_out)


def attention_forward(resid, gain, qkv, attn_out, table, shape):
    clips, rows, width = shape
    span = LEFT + rows + RIGHT
    normed, normal, inverse = norm_forward(resid, gain)
    entry = normed.astype(jnp.bfloat16)
    projected = jnp.einsum("rd,tde->tre", entry, qkv, preferred_element_type=jnp.float32).astype(
        jnp.bfloat16
    )
    query = projected[0].reshape(clips, rows, HEADS, HEAD_DIM)
    key_value = projected[1:].reshape(2, clips, rows, width)
    before = from_behind(key_value[:, :, rows - LEFT :], "seq", 1)
    after = from_behind(key_value[:, :, :RIGHT], "seq", -1)
    extended = jnp.concatenate([before, key_value, after], 2)
    keys = extended[0].reshape(clips, span, HEADS, HEAD_DIM)
    values = extended[1].reshape(clips, span, HEADS, HEAD_DIM)
    mask = window_mask(rows, lax.axis_index("seq") * rows)
    raw = attend_scores(query, keys, table, mask)
    peak = jnp.max(raw, -1, keepdims=True)
    expo = jnp.exp(raw - peak)
    total = jnp.sum(expo, -1, keepdims=True)
    probs = (expo / total).astype(jnp.bfloat16)
    mixed = jnp.einsum("chsu,cuhd->cshd", probs, values, preferred_element_type=jnp.float32)
    mixed = mixed.astype(jnp.bfloat16).reshape(clips * rows, width)
    logsum = peak + jnp.log(total)
    return (
        matmul(mixed, attn_out),
        (normal, inverse, entry, query, keys, values, mask, logsum, mixed),
    )


def attention_back(grad_branch, kept, gain, qkv, attn_out, table, shape):
    clips, rows, width = shape
    span = LEFT + rows + RIGHT
    scale = HEAD_DIM ** (-0.5)
    normal, inverse, entry, query, keys, values, mask, logsum, mixed = kept
    grad_low = grad_branch.astype(jnp.bfloat16)
    grad_attn_out = matmul_left_t(mixed, grad_low)
    grad_mixed = (
        matmul_right_t(grad_low, attn_out)
        .astype(jnp.bfloat16)
        .reshape(clips, rows, HEADS, HEAD_DIM)
    )
    raw = attend_scores(query, keys, table, mask)
    probs = jnp.exp(raw - logsum)
    grad_values = jnp.einsum(
        "chsu,cshd->cuhd",
        probs.astype(jnp.bfloat16),
        grad_mixed,
        preferred_element_type=jnp.float32,
    )
    grad_probs = jnp.einsum(
        "cshd,cuhd->chsu", grad_mixed, values, preferred_element_type=jnp.float32
    )
    grad_raw = (probs * (grad_probs - jnp.sum(probs * grad_probs, -1, keepdims=True))).astype(
        jnp.bfloat16
    )
    grad_query = jnp.einsum("chsu,cuhd->cshd", grad_raw, keys, preferred_element_type=jnp.float32)
    grad_keys = jnp.einsum("chsu,cshd->cuhd", grad_raw, query, preferred_element_type=jnp.float32)
    grad_rel = unskew(grad_raw, WIN)
    grad_query = (
        grad_query
        + jnp.einsum("chsw,wd->cshd", grad_rel, table, preferred_element_type=jnp.float32)
    ) * scale
    grad_table = (
        jnp.einsum("chsw,cshd->wd", grad_rel, query, preferred_element_type=jnp.float32) * scale
    )
    grad_kv = jnp.stack([grad_keys * scale, grad_values]).reshape(2, clips, span, width)
    from_later = from_behind(grad_kv[:, :, :LEFT].astype(jnp.bfloat16), "seq", -1).astype(
        jnp.float32
    )
    from_earlier = from_behind(grad_kv[:, :, LEFT + rows :].astype(jnp.bfloat16), "seq", 1).astype(
        jnp.float32
    )
    own_kv = grad_kv[:, :, LEFT : LEFT + rows]
    own_kv = own_kv.at[:, :, rows - LEFT :].add(from_later).at[:, :, :RIGHT].add(from_earlier)
    stacked = jnp.concatenate(
        [grad_query.reshape(1, clips * rows, width), own_kv.reshape(2, clips * rows, width)], 0
    ).astype(jnp.bfloat16)
    grad_qkv = jnp.einsum("rd,tre->tde", entry, stacked, preferred_element_type=jnp.float32)
    grad_entry = jnp.einsum("tre,tde->rd", stacked, qkv, preferred_element_type=jnp.float32)
    grad_in, grad_gain = norm_backward(grad_entry, normal, inverse, gain)
    return (grad_in, grad_gain, grad_qkv, grad_attn_out, grad_table)


def conv_forward(resid, gain_in, gain_mid, conv_in, depthwise, conv_out, shape):
    clips, rows, width = shape
    normed, normal, inverse = norm_forward(resid, gain_in)
    entry = normed.astype(jnp.bfloat16)
    joined = matmul(entry, conv_in)
    opened = jax.nn.sigmoid(joined[:, width:])
    glu = (joined[:, :width] * opened).astype(jnp.bfloat16).reshape(clips, rows, width)
    before = from_behind(glu[:, rows - (KERNEL - 1) :], "seq", 1)
    padded = jnp.concatenate([before, glu], 1).astype(jnp.float32)
    taps = depthwise.astype(jnp.float32)
    summed = jnp.zeros((clips, rows, width), jnp.float32)
    for tap in range(KERNEL):
        summed = summed + taps[tap] * padded[:, tap : tap + rows]
    middle, mid_normal, mid_inverse = norm_forward(summed.reshape(clips * rows, width), gain_mid)
    swished = (middle * jax.nn.sigmoid(middle)).astype(jnp.bfloat16)
    kept = (
        normal,
        inverse,
        entry,
        joined,
        opened,
        padded,
        middle,
        mid_normal,
        mid_inverse,
        swished,
    )
    return (matmul(swished, conv_out), kept)


def conv_back(grad_branch, kept, gain_in, gain_mid, conv_in, depthwise, conv_out, shape):
    clips, rows, width = shape
    normal, inverse, entry, joined, opened, padded, middle, mid_normal, mid_inverse, swished = kept
    taps = depthwise.astype(jnp.float32)
    grad_low = grad_branch.astype(jnp.bfloat16)
    grad_conv_out = matmul_left_t(swished, grad_low)
    grad_middle = matmul_right_t(grad_low, conv_out) * swish_grad(middle)
    grad_summed, grad_gain_mid = norm_backward(grad_middle, mid_normal, mid_inverse, gain_mid)
    grad_summed = grad_summed.reshape(clips, rows, width)
    grad_taps = jnp.stack(
        [jnp.sum(grad_summed * padded[:, tap : tap + rows], (0, 1)) for tap in range(KERNEL)]
    )
    grad_padded = jnp.zeros((clips, rows + KERNEL - 1, width), jnp.float32)
    for tap in range(KERNEL):
        grad_padded = grad_padded + jnp.pad(
            grad_summed * taps[tap], ((0, 0), (tap, KERNEL - 1 - tap), (0, 0))
        )
    from_later = from_behind(grad_padded[:, : KERNEL - 1].astype(jnp.bfloat16), "seq", -1).astype(
        jnp.float32
    )
    grad_glu = (
        grad_padded[:, KERNEL - 1 :]
        .at[:, rows - (KERNEL - 1) :]
        .add(from_later)
        .reshape(clips * rows, width)
    )
    value_part = joined[:, :width]
    grad_joined = jnp.concatenate(
        [grad_glu * opened, grad_glu * value_part * opened * (1.0 - opened)], 1
    )
    grad_joined = grad_joined.astype(jnp.bfloat16)
    grad_conv_in = matmul_left_t(entry, grad_joined)
    grad_in, grad_gain_in = norm_backward(
        matmul_right_t(grad_joined, conv_in), normal, inverse, gain_in
    )
    return (grad_in, grad_gain_in, grad_gain_mid, grad_conv_in, grad_taps, grad_conv_out)


def on_device(
    tokens,
    ffn_in,
    ffn_out,
    qkv,
    attn_out,
    conv_in,
    conv_out,
    depthwise,
    gains,
    rel_table,
    cotangent,
):
    clips, rows, width = tokens.shape
    shape = (clips, rows, width)
    flat_rows = clips * rows
    gathered = (
        lax.all_gather(ffn_in, "group", axis=1, tiled=True),
        lax.all_gather(ffn_out, "group", axis=1, tiled=True),
        lax.all_gather(qkv, "group", axis=1, tiled=True),
        lax.all_gather(attn_out, "group", axis=0, tiled=True),
        lax.all_gather(conv_in, "group", axis=0, tiled=True),
        lax.all_gather(conv_out, "group", axis=0, tiled=True),
        lax.all_gather(depthwise, "group", axis=1, tiled=True),
        lax.all_gather(gains, "group", axis=1, tiled=True),
    )
    f_in, f_out, proj, a_out, c_in, c_out, depth, gain_rows = gathered
    gain_f = gain_rows.astype(jnp.float32)
    start = tokens.reshape(flat_rows, width).astype(jnp.float32)
    first_branch, first_kept = feed_forward(start, gain_f[0], f_in[0], f_out[0])
    after_first = start + 0.5 * first_branch
    attn_branch, attn_kept = attention_forward(
        after_first, gain_f[1], proj, a_out, rel_table, shape
    )
    after_attn = after_first + attn_branch
    conv_branch, conv_kept = conv_forward(
        after_attn, gain_f[2], gain_f[3], c_in, depth, c_out, shape
    )
    after_conv = after_attn + conv_branch
    second_branch, second_kept = feed_forward(after_conv, gain_f[4], f_in[1], f_out[1])
    final = after_conv + 0.5 * second_branch
    result, final_normal, final_inverse = norm_forward(final, gain_f[5])
    squares = jnp.stack(
        [
            jnp.sum(member * member)
            for member in (final, first_branch, attn_branch, conv_branch, second_branch)
        ]
    )
    back_weights = (
        lax.all_gather(ffn_in, "group", axis=1, tiled=True),
        lax.all_gather(ffn_out, "group", axis=1, tiled=True),
        lax.all_gather(qkv, "group", axis=1, tiled=True),
        lax.all_gather(attn_out, "group", axis=0, tiled=True),
        lax.all_gather(conv_in, "group", axis=0, tiled=True),
        lax.all_gather(conv_out, "group", axis=0, tiled=True),
        lax.all_gather(depthwise, "group", axis=1, tiled=True),
        lax.all_gather(gains, "group", axis=1, tiled=True),
    )
    f_in, f_out, proj, a_out, c_in, c_out, depth, gain_rows = back_weights
    gain_f = gain_rows.astype(jnp.float32)
    grad = cotangent.reshape(flat_rows, width).astype(jnp.float32)
    grad, grad_gain_final = norm_backward(grad, final_normal, final_inverse, gain_f[5])
    back_in, grad_gain_second, grad_in_second, grad_out_second = feed_back(
        0.5 * grad, second_kept, gain_f[4], f_in[1], f_out[1]
    )
    grad = grad + back_in
    back_in, grad_gain_conv, grad_gain_mid, grad_conv_in, grad_taps, grad_conv_out = conv_back(
        grad, conv_kept, gain_f[2], gain_f[3], c_in, depth, c_out, shape
    )
    grad = grad + back_in
    back_in, grad_gain_attn, grad_qkv, grad_attn_out, grad_table = attention_back(
        grad, attn_kept, gain_f[1], proj, a_out, rel_table, shape
    )
    grad = grad + back_in
    back_in, grad_gain_first, grad_in_first, grad_out_first = feed_back(
        0.5 * grad, first_kept, gain_f[0], f_in[0], f_out[0]
    )
    grad = grad + back_in
    stacked_in = jnp.stack([grad_in_first, grad_in_second])
    stacked_out = jnp.stack([grad_out_first, grad_out_second])
    gain_grads = jnp.stack(
        [
            grad_gain_first,
            grad_gain_attn,
            grad_gain_conv,
            grad_gain_mid,
            grad_gain_second,
            grad_gain_final,
        ]
    )
    owned = (
        lax.psum_scatter(
            stacked_in.astype(jnp.bfloat16), "group", scatter_dimension=1, tiled=True
        ).astype(jnp.float32),
        lax.psum_scatter(
            stacked_out.astype(jnp.bfloat16), "group", scatter_dimension=1, tiled=True
        ).astype(jnp.float32),
        lax.psum_scatter(
            grad_qkv.astype(jnp.bfloat16), "group", scatter_dimension=1, tiled=True
        ).astype(jnp.float32),
        lax.psum_scatter(
            grad_attn_out.astype(jnp.bfloat16), "group", scatter_dimension=0, tiled=True
        ).astype(jnp.float32),
        lax.psum_scatter(
            grad_conv_in.astype(jnp.bfloat16), "group", scatter_dimension=0, tiled=True
        ).astype(jnp.float32),
        lax.psum_scatter(
            grad_conv_out.astype(jnp.bfloat16), "group", scatter_dimension=0, tiled=True
        ).astype(jnp.float32),
        lax.psum_scatter(
            grad_taps.astype(jnp.bfloat16), "group", scatter_dimension=1, tiled=True
        ).astype(jnp.float32),
        lax.psum_scatter(
            gain_grads.astype(jnp.bfloat16), "group", scatter_dimension=1, tiled=True
        ).astype(jnp.float32),
    )
    own_in, own_out, own_qkv, own_attn, own_cin, own_cout, own_taps, own_gains = owned
    summed = (
        lax.psum(own_in.astype(jnp.bfloat16), ("seq", "replica")).astype(jnp.float32),
        lax.psum(own_out.astype(jnp.bfloat16), ("seq", "replica")).astype(jnp.float32),
        lax.psum(own_qkv.astype(jnp.bfloat16), ("seq", "replica")).astype(jnp.float32),
        lax.psum(own_attn.astype(jnp.bfloat16), ("seq", "replica")).astype(jnp.float32),
        lax.psum(own_cin.astype(jnp.bfloat16), ("seq", "replica")).astype(jnp.float32),
        lax.psum(own_cout.astype(jnp.bfloat16), ("seq", "replica")).astype(jnp.float32),
        lax.psum(own_taps.astype(jnp.bfloat16), ("seq", "replica")).astype(jnp.float32),
        lax.psum(own_gains.astype(jnp.bfloat16), ("seq", "replica")).astype(jnp.float32),
    )
    totals = lax.psum((squares, grad_table), ("seq", "group", "replica"))
    matrices = summed[:6]
    taps_owned = summed[6]
    gains_owned = summed[7]
    count = (
        flat_rows * width * lax.axis_size("seq") * lax.axis_size("group") * lax.axis_size("replica")
    )
    stats = jnp.sqrt(totals[0] / count)
    return (
        result.astype(jnp.bfloat16).reshape(shape),
        grad.astype(jnp.bfloat16).reshape(shape),
        matrices[0],
        matrices[1],
        matrices[2],
        matrices[3],
        matrices[4],
        matrices[5],
        taps_owned,
        gains_owned,
        totals[1],
        stats,
    )


def solution(mesh):
    in_specs = (
        P(("group", "replica"), "seq", None),
        P(None, "group", None),
        P(None, "group", None),
        P(None, "group", None),
        P("group", None),
        P("group", None),
        P("group", None),
        P(None, "group"),
        P(None, "group"),
        P(),
        P(("group", "replica"), "seq", None),
    )
    out_specs = (
        P(("group", "replica"), "seq", None),
        P(("group", "replica"), "seq", None),
        P(None, "group", None),
        P(None, "group", None),
        P(None, "group", None),
        P("group", None),
        P("group", None),
        P("group", None),
        P(None, "group"),
        P(None, "group"),
        P(),
        P(),
    )
    return jax.shard_map(
        on_device, mesh=mesh, in_specs=in_specs, out_specs=out_specs, check_vma=False
    )
```

profile of v0, /device:TPU:0, one launch (start us, length us, event | category | flops | bytes accessed | tf_op | source)
XLA Modules:
  0.0 2258.4 jit_solution(10843111838597775830)
XLA Ops:
  11.9 28.2 %all_gather.32 = bf16[6,1024]{1,0:T(8,128)(2,1)S(1)} all-gather(bf16[6,128]{1,0:T(8,128)(2,1)S(1)} %copy-done.131), channel_id=1, replica_groups=mesh['seq'=2,'group'=8,'replica'=2] {'group'}, dimensions={1}, use_global_device_ids=true | all-gather | bytes 13824 | tf_op jit(solution)/shard_map/all_gather | solution.py:291
  40.7 26.9 %all_gather.37 = bf16[31,1024]{1,0:T(8,128)(2,1)S(1)} all-gather(bf16[31,128]{1,0:T(8,128)(2,1)S(1)} %copy-done.130), channel_id=1, replica_groups=mesh['seq'=2,'group'=8,'replica'=2] {'group'}, dimensions={1}, use_global_device_ids=true | all-gather | bytes 71424 | tf_op jit(solution)/shard_map/all_gather | solution.py:290
  68.5 173.2 %all-gather.7.cloned.1.call-done = bf16[2,1024,4096]{2,1,0:T(8,128)(2,1)} async-done(((bf16[2,128,4096]{2,1,0:T(8,128)(2,1)}), bf16[2,1024,4096]{2,1,0:T(8,128)(2,1)}) %all-gather.7.cloned.1.call-update) | async-done | bytes 16777232 | tf_op jit(solution)/shard_map/all_gather | solution.py:284
  252.2 217.6 %all-gather.9.cloned.1.call-done = bf16[2,4096,1024]{2,1,0:T(8,128)(2,1)} async-done(((bf16[2,512,1024]{2,1,0:T(8,128)(2,1)}), bf16[2,4096,1024]{2,1,0:T(8,128)(2,1)}) %all-gather.9.cloned.1.call-update) | async-done | bytes 16777232 | tf_op jit(solution)/shard_map/all_gather | solution.py:285
  481.2 87.9 %all-gather.11.cloned.1.call-done = bf16[3,1024,1024]{2,1,0:T(8,128)(2,1)} async-done(((bf16[3,128,1024]{2,1,0:T(8,128)(2,1)}), bf16[3,1024,1024]{2,1,0:T(8,128)(2,1)}) %all-gather.11.cloned.1.call-update) | async-done | bytes 6291472 | tf_op jit(solution)/shard_map/all_gather | solution.py:286
  600.6 25.7 %reshape.584 = f32[1,16,299520]{2,1,0:T(8,128)} reshape(f32[1,16,512,585]{3,2,1,0:T(8,128)} %pad.139.clone) | data formatting | bytes 38338560 | tf_op jit(solution)/shard_map/reshape | solution.py:68
  626.3 15.0 slice.526
  641.3 34.9 %reshape.585 = f32[16,512,584]{2,1,0:T(8,128)} reshape(f32[1,16,299008]{2,1,0:T(8,128)} %slice.526) | data formatting | bytes 38273024 | tf_op jit(solution)/shard_map/reshape | solution.py:69
  676.2 22.1 copy.55
  854.2 18.6 pad_add_fusion
  916.6 13.9 multiply_convert_fusion
  941.1 14.1 copy.57
  958.1 26.6 %reshape.593 = bf16[1,16,299008]{2,1,0:T(8,128)(2,1)} reshape(bf16[16,512,584]{2,1,0:T(8,128)(2,1)} %copy.57) | data formatting | bytes 19136512 | tf_op jit(solution)/shard_map/reshape | solution.py:75
  993.9 32.5 %reshape.594 = bf16[1,16,512,585]{3,2,1,0:T(8,128)(2,1)} reshape(bf16[1,16,299520]{2,1,0:T(8,128)(2,1)} %pad.171) | data formatting | bytes 19169280 | tf_op jit(solution)/shard_map/reshape | solution.py:77
  1048.2 14.3 copy.65
  1195.2 65.9 %reduce-scatter.23.cloned.1.call-done = bf16[128,1024]{1,0:T(8,128)(2,1)} async-done(((bf16[1024,1024]{1,0:T(8,128)(2,1)}), bf16[128,1024]{1,0:T(8,128)(2,1)}) %reduce-scatter.23.cloned.1.call-update) | async-done | bytes 262160 | tf_op jit(solution)/shard_map/reduce_scatter | solution.py:373
  1261.2 70.5 %reduce-scatter.19.cloned.1.call-done = bf16[128,1024]{1,0:T(8,128)(2,1)} async-done(((bf16[1024,1024]{1,0:T(8,128)(2,1)}), bf16[128,1024]{1,0:T(8,128)(2,1)}) %reduce-scatter.19.cloned.1.call-update) | async-done | bytes 262160 | tf_op jit(solution)/shard_map/reduce_scatter | solution.py:367
  1331.6 90.4 %reduce-scatter.21.cloned.1.call-done = bf16[128,2048]{1,0:T(8,128)(2,1)} async-done(((bf16[1024,2048]{1,0:T(8,128)(2,1)}), bf16[128,2048]{1,0:T(8,128)(2,1)}) %reduce-scatter.21.cloned.1.call-update) | async-done | bytes 524304 | tf_op jit(solution)/shard_map/reduce_scatter | solution.py:370
  1422.0 286.0 %reduce-scatter.17.cloned.1.call-done = bf16[2,512,1024]{2,1,0:T(8,128)(2,1)} async-done(((bf16[2,4096,1024]{2,1,0:T(8,128)(2,1)}), bf16[2,512,1024]{2,1,0:T(8,128)(2,1)}) %reduce-scatter.17.cloned.1.call-update) | async-done | bytes 2097168 | tf_op jit(solution)/shard_map/reduce_scatter | solution.py:361
  1708.0 284.7 %reduce-scatter.15.cloned.1.call-done = bf16[2,128,4096]{2,1,0:T(8,128)(2,1)} async-done(((bf16[2,1024,4096]{2,1,0:T(8,128)(2,1)}), bf16[2,128,4096]{2,1,0:T(8,128)(2,1)}) %reduce-scatter.15.cloned.1.call-update) | async-done | bytes 2097168 | tf_op jit(solution)/shard_map/reduce_scatter | solution.py:358
  1998.1 39.8 %all-reduce.33 = (f32[73,64]{0,1:T(8,128)}, f32[5]{0:T(128)S(1)}) all-reduce(f32[73,64]{0,1:T(8,128)S(1)} %fusion.97, f32[5]{0:T(128)S(1)} %stack.260), channel_id=1, replica_groups=mesh['seq'=2,'group'=8,'replica'=2] {'seq','group','replica'}, use_global_device_ids=true, to_apply=%region_80.81 | all-reduce | flops 4677 | bytes 37416 | tf_op jit(solution)/shard_map/psum | solution.py:394
  2038.4 18.8 reduce-scatter.27.cloned.1.call-done
  2062.0 59.6 %reduce-scatter.29.cloned.1.call-done = bf16[128,6]{1,0:T(8,128)(2,1)} async-done(((bf16[1024,6]{1,0:T(8,128)(2,1)}), bf16[128,6]{1,0:T(8,128)(2,1)}) %reduce-scatter.29.cloned.1.call-update) | async-done | bytes 1552
  2133.8 106.6 %all-reduce.38.cloned.1.call-done = (bf16[3,128,1024]{1,2,0:T(8,128)(2,1)}, bf16[2,128,4096]{2,1,0:T(8,128)(2,1)}, bf16[2,512,1024]{2,1,0:T(8,128)(2,1)}, bf16[1...) async-done(((bf16[3,128,1024]{1,2,0:T(8,128)(2,1)}, bf16[2,128,4096]{2,1,0:T(8,128)(2,1)}, bf16[2,512,1024]{2,1,0:T(8,128)(2,1)}, ...) | async-done | bytes 6029328 | tf_op jit(solution)/shard_map/psum | solution.py:387
  (502 shorter events, 468.4 us)
Async XLA Ops:
  7.2 575.0 %copy-start = (bf16[73,64]{0,1:T(8,128)(2,1)S(1)}, bf16[73,64]{0,1:T(8,128)(2,1)}, u32[]{:S(2)}) copy-start(bf16[73,64]{0,1:T(8,128)(2,1)} %param.26) | copy-start | bytes 28036
  7.2 234.5 %all-gather.7.cloned.1.call-start = ((), (), s32[]{:S(2)}) async-start(), calls=%async_computation.8 | async-start | bytes 18874368 | tf_op jit(solution)/shard_map/all_gather | solution.py:284
  7.9 461.8 %all-gather.9.cloned.1.call-start = ((), (), s32[]{:S(2)}) async-start(), calls=%async_computation.9 | async-start | bytes 18874368 | tf_op jit(solution)/shard_map/all_gather | solution.py:285
  8.7 560.4 %all-gather.11.cloned.1.call-start = ((), (), s32[]{:S(2)}) async-start(), calls=%async_computation.10 | async-start | bytes 7077888 | tf_op jit(solution)/shard_map/all_gather | solution.py:286
  9.4 728.4 %all-gather.13.cloned.1.call-start = ((), (), s32[]{:S(2)}) async-start(), calls=%async_computation.11 | async-start | bytes 2359296 | tf_op jit(solution)/shard_map/all_gather | solution.py:287
  10.0 733.7 %all-gather.15.cloned.1.call-start = ((), (), s32[]{:S(2)}) async-start(), calls=%async_computation.12 | async-start | bytes 4718592 | tf_op jit(solution)/shard_map/all_gather | solution.py:288
  10.6 760.0 %all-gather.17.cloned.1.call-start = ((), (), s32[]{:S(2)}) async-start(), calls=%async_computation.13 | async-start | bytes 2359296 | tf_op jit(solution)/shard_map/all_gather | solution.py:289
  11.2 1179.8 %reduce-scatter.25.cloned.1.call-start = ((), (), s32[]{:S(2)}) async-start(), calls=%async_computation.19 | async-start | bytes 7077888
  11.5 240.7 %copy-start.81 = (f32[512]{0:T(512)}, f32[512]{0:T(512)S(1)}, u32[]{:S(2)}) copy-start(f32[512]{0:T(512)S(1)} %broadcast_multiply_fusion.17) | copy-start | bytes 6148
  11.9 240.2 %copy-start.118 = (f32[512]{0:T(512)}, f32[512]{0:T(512)S(1)}, u32[]{:S(2)}) copy-start(f32[512]{0:T(512)S(1)} %add_rsqrt_fusion.5) | copy-start | bytes 6148
  576.0 122.2 %collective-permute-start = (bf16[2,1,64,1024]{3,2,0,1:T(8,128)(2,1)S(1)}, bf16[2,1,64,1024]{3,2,0,1:T(8,128)(2,1)S(1)}, u32[]{:S(2)}, u32[]{:S(2)}) collective-permute-start(bf16[2,1,64,1024]{3,2,0,1:T(8,128)(2,1)S(1)} %slice.521), channel_id=1, source_target_pairs={{0,16},{1,17},{2,18},{3,19},{4,20},{5,21},{6,22},{7,23},{8,24},{9,... | collective-permute-start | bytes 786440 | tf_op jit(solution)/shard_map/ppermute | solution.py:22
  580.7 117.5 %collective-permute-start.1 = (bf16[2,1,8,1024]{3,2,0,1:T(8,128)(2,1)S(1)}, bf16[2,1,8,1024]{3,2,0,1:T(8,128)(2,1)S(1)}, u32[]{:S(2)}, u32[]{:S(2)}) collective-permute-start(bf16[2,1,8,1024]{3,2,0,1:T(8,128)(2,1)S(1)} %slice.522), channel_id=1, source_target_pairs={{16,0},{17,1},{18,2},{19,3},{20,4},{21,5},{22,6},{23,7},{24,8},{25... | collective-permute-start | bytes 98312 | tf_op jit(solution)/shard_map/ppermute | solution.py:22
  751.3 6.7 collective-permute-start.2
  872.7 6.2 collective-permute-start.3
  955.2 84.5 %collective-permute-start.5 = (bf16[2,1,8,1024]{3,2,0,1:T(8,128)(2,1)S(1)}, bf16[2,1,8,1024]{3,2,0,1:T(8,128)(2,1)S(1)}, u32[]{:S(2)}, u32[]{:S(2)}) collective-permute-start(bf16[2,1,8,1024]{3,2,0,1:T(8,128)(2,1)S(1)} %slice.608), channel_id=1, source_target_pairs={{0,16},{1,17},{2,18},{3,19},{4,20},{5,21},{6,22},{7,23},{8,24},{9,... | collective-permute-start | bytes 98312 | tf_op jit(solution)/shard_map/ppermute | solution.py:22
  956.8 81.3 %collective-permute-start.4 = (bf16[2,1,64,1024]{3,2,0,1:T(8,128)(2,1)}, bf16[2,1,64,1024]{3,2,0,1:T(8,128)(2,1)}, u32[]{:S(2)}, u32[]{:S(2)}) collective-permute-start(bf16[2,1,64,1024]{3,2,0,1:T(8,128)(2,1)} %slice.606), channel_id=1, source_target_pairs={{16,0},{17,1},{18,2},{19,3},{20,4},{21,5},{22,6},{23,7},{24,8},{25... | collective-permute-start | bytes 786440 | tf_op jit(solution)/shard_map/ppermute | solution.py:22
  1072.7 188.5 %reduce-scatter.23.cloned.1.call-start = ((), (), s32[]{:S(2)}) async-start(), calls=%async_computation.18 | async-start | bytes 2359296 | tf_op jit(solution)/shard_map/reduce_scatter | solution.py:373
  1077.1 254.5 %reduce-scatter.19.cloned.1.call-start = ((), (), s32[]{:S(2)}) async-start(), calls=%async_computation.16 | async-start | bytes 2359296 | tf_op jit(solution)/shard_map/reduce_scatter | solution.py:367
  1082.6 339.4 %reduce-scatter.21.cloned.1.call-start = ((), (), s32[]{:S(2)}) async-start(), calls=%async_computation.17 | async-start | bytes 4718592 | tf_op jit(solution)/shard_map/reduce_scatter | solution.py:370
  1090.0 618.0 %reduce-scatter.17.cloned.1.call-start = ((), (), s32[]{:S(2)}) async-start(), calls=%async_computation.15 | async-start | bytes 18874368 | tf_op jit(solution)/shard_map/reduce_scatter | solution.py:361
  1135.1 857.6 %reduce-scatter.15.cloned.1.call-start = ((), (), s32[]{:S(2)}) async-start(), calls=%async_computation.14 | async-start | bytes 18874368 | tf_op jit(solution)/shard_map/reduce_scatter | solution.py:358
  1169.5 887.8 %reduce-scatter.27.cloned.1.call-start = ((), (), s32[]{:S(2)}) async-start(), calls=%async_computation.20 | async-start | bytes 294912
  1177.6 944.1 %reduce-scatter.29.cloned.1.call-start = ((), (), s32[]{:S(2)}) async-start(), calls=%async_computation.21 | async-start | bytes 294912
  1189.7 1050.7 %all-reduce.38.cloned.1.call-start = ((), (), s32[]{:S(2)}) async-start(), calls=%async_computation.22 | async-start | bytes 12058624 | tf_op jit(solution)/shard_map/psum | solution.py:387
  (138 other events, 1982.6 us)
Sparse Core Ops, SparseCore 0:
  10.2 231.4 all-gather.6
  243.9 225.7 all-gather.8
  471.9 97.2 all-gather.10
  571.1 47.4 all-gather.12
  620.6 71.8 all-gather.14
  694.5 47.5 all-gather.16
  1072.8 118.1 reduce-scatter.24
  1194.5 66.5 reduce-scatter.22
  1264.7 66.8 reduce-scatter.18
  1335.1 86.8 reduce-scatter.20
  1426.3 281.6 reduce-scatter.16
  1711.6 281.0 reduce-scatter.14
  1997.0 60.2 reduce-scatter.26
  2061.4 60.2 reduce-scatter.28
  2125.0 115.3 all-reduce.37
where the time goes:
time: 2270 us; the launch traced here: 2260 us
  waiting for transfers between devices  1470 us (65%)
  local copies, waits for them, and re-layouts  271 us (12%)
  matrix products  242 us (11%)
  other arithmetic  136 us (6%)
  blocking collectives  105 us (5%)
    reduce_scatter x1, waiting for transfers between devices, on_device(): lax.psum_scatter(stacked_out.astype(jnp.bfloat16), 'group', scatter_dimen...  286 us
    reduce_scatter x1, waiting for transfers between devices, on_device(): lax.psum_scatter(stacked_in.astype(jnp.bfloat16), 'group', scatter_dimens...  285 us
    all_gather x1, waiting for transfers between devices, on_device(): lax.all_gather(ffn_out, 'group', axis=1, tiled=True)  218 us
    all_gather x1, waiting for transfers between devices, on_device(): lax.all_gather(ffn_in, 'group', axis=1, tiled=True)  173 us
    psum x1, waiting for transfers between devices, on_device(): lax.psum(own_qkv.astype(jnp.bfloat16), ('seq', 'replica'))  107 us
    reduce_scatter x1, waiting for transfers between devices, on_device(): lax.psum_scatter(grad_conv_in.astype(jnp.bfloat16), 'group', scatter_dime...  90.4 us
    all_gather x1, waiting for transfers between devices, on_device(): lax.all_gather(qkv, 'group', axis=1, tiled=True)  87.9 us
    unnamed x18, waiting for transfers between devices  83.4 us
  transfers between devices with their start and end apart: 21, of which 14 were waited for; matrix products, arithmetic and copies ran while one was open for 18% of the time, Pallas kernels for 0%

commit v1 on v0

v1 whole, which is shorter than its diff:
```python
import functools

import jax
import jax.numpy as jnp
from jax import lax
from jax.experimental import pallas as pl
from jax.experimental.pallas import tpu as pltpu
from jax.sharding import PartitionSpec as P

HEAD_DIM = 64
KERNEL = 31
LEFT = 64
RIGHT = 8
WIN = 73
LANES = 128
BLOCK = 128
SPAN = 256
BACK_PAD = 64


EPSILON = 1e-05
NEGATIVE = -1e30


MESH = pl.DeviceIdType.MESH


def from_behind(value, axis, steps):
    count = lax.axis_size(axis)
    initial, last = (max(0, -steps), min(count, count - steps))
    return lax.ppermute(value, axis, [(source, source + steps) for source in range(initial, last)])


def norm_forward(values, gain):
    centered = values - jnp.mean(values, -1, keepdims=True)
    inverse = lax.rsqrt(jnp.mean(centered * centered, -1, keepdims=True) + EPSILON)
    normal = centered * inverse
    return (normal * gain, normal, inverse)


def norm_backward(grad_out, normal, inverse, gain):
    grad_normal = grad_out * gain
    grad_in = inverse * (
        grad_normal
        - jnp.mean(grad_normal, -1, keepdims=True)
        - normal * jnp.mean(grad_normal * normal, -1, keepdims=True)
    )
    grad_gain = jnp.sum(grad_out * normal, 0)
    return (grad_in, grad_gain)


def matmul(left, right):
    return jnp.dot(left, right, preferred_element_type=jnp.float32)


def matmul_left_t(left, right):
    return lax.dot_general(
        left, right, (((0,), (0,)), ((), ())), preferred_element_type=jnp.float32
    )


def matmul_right_t(left, right):
    return lax.dot_general(
        left, right, (((1,), (1,)), ((), ())), preferred_element_type=jnp.float32
    )


def swish_grad(values):
    logistic = jax.nn.sigmoid(values)
    return logistic + values * logistic * (1.0 - logistic)


def nt(left,right):
    return lax.dot_general(left,right,(((1,),(1,)),((),())),preferred_element_type=jnp.float32)
def tn(left,right):
    return lax.dot_general(left,right,(((0,),(0,)),((),())),preferred_element_type=jnp.float32)
def nn(left,right):
    return jnp.dot(left,right,preferred_element_type=jnp.float32)

def block_mask(first, block, limit):
    rows=lax.broadcasted_iota(jnp.int32,(BLOCK,SPAN),0)
    cols=lax.broadcasted_iota(jnp.int32,(BLOCK,SPAN),1)
    offset=cols-rows
    place=first+block*BLOCK+cols-LEFT
    return (offset>=0)&(offset<WIN)&(place>=0)&(place<limit)

def head_lanes(head):
    lanes=lax.broadcasted_iota(jnp.int32,(BLOCK,LANES),1)
    return (lanes>=head*HEAD_DIM)&(lanes<(head+1)*HEAD_DIM)

def block_probs(query, keys, table, mask):
    relative=pltpu.roll(nt(query,table),0,1,stride=1,stride_axis=0)
    raw=jnp.where(mask,(nt(query,keys)+relative)*(HEAD_DIM**-0.5),NEGATIVE)
    expo=jnp.exp(raw-jnp.max(raw,-1,keepdims=True))
    return expo*(1.0/jnp.sum(expo,-1,keepdims=True))

def attend_kernel(limit, first_ref, q_ref, k_ref, v_ref, t_ref, c_ref):
    table=t_ref[...]
    zero=jnp.zeros((BLOCK,LANES),jnp.bfloat16)
    for block in range(q_ref.shape[1]//BLOCK):
        rows=pl.ds(block*BLOCK,BLOCK); span=pl.ds(block*BLOCK,SPAN)
        query=q_ref[0,rows,:]; keys=k_ref[0,span,:]; values=v_ref[0,span,:]
        mask=block_mask(first_ref[0],block,limit)
        mixed=[]
        for head in range(2):
            probs=block_probs(jnp.where(head_lanes(head),query,zero),keys,table,mask)
            mixed.append(nn(probs.astype(jnp.bfloat16),values))
        c_ref[0,rows,:]=jnp.where(head_lanes(0),mixed[0],mixed[1]).astype(jnp.bfloat16)

def attend_back_kernel(limit, first_ref, q_ref, k_ref, v_ref, t_ref, g_ref, dq_ref, dk_ref, dv_ref, dt_ref, dk_sum, dv_sum):
    table=t_ref[...]
    zero=jnp.zeros((BLOCK,LANES),jnp.bfloat16)
    flip=(lax.broadcasted_iota(jnp.int32,(BLOCK,BLOCK),0)+lax.broadcasted_iota(jnp.int32,(BLOCK,BLOCK),1)==BLOCK-1).astype(jnp.float32).astype(jnp.bfloat16)
    dk_sum[...]=jnp.zeros_like(dk_sum); dv_sum[...]=jnp.zeros_like(dv_sum)
    @pl.when((pl.program_id(0)==0)&(pl.program_id(1)==0))
    def _(): dt_ref[...]=jnp.zeros_like(dt_ref)
    for block in range(q_ref.shape[1]//BLOCK):
        rows=pl.ds(block*BLOCK,BLOCK); span=pl.ds(block*BLOCK,SPAN)
        keys=k_ref[0,span,:]; values=v_ref[0,span,:]
        mask=block_mask(first_ref[0],block,limit)
        grad_query=[]
        for head in range(2):
            query=jnp.where(head_lanes(head),q_ref[0,rows,:],zero)
            grad=jnp.where(head_lanes(head),g_ref[0,rows,:],zero)
            probs=block_probs(query,keys,table,mask)
            grad_probs=nt(grad,values)
            grad_raw=probs*(grad_probs-jnp.sum(probs*grad_probs,-1,keepdims=True))
            grad_raw=grad_raw.astype(jnp.bfloat16)
            turned=pltpu.roll(nn(flip,grad_raw),SPAN-BLOCK+1,1,stride=1,stride_axis=0)
            unskewed=nn(flip,turned.astype(jnp.bfloat16)).astype(jnp.bfloat16)
            dv_sum[span,:]+=tn(probs.astype(jnp.bfloat16),grad)
            dk_sum[span,:]+=tn(grad_raw,query)
            dt_ref[...]+=tn(unskewed,query)
            grad_query.append(nn(grad_raw,keys)+nn(unskewed,table))
        dq_ref[0,rows,:]=(jnp.where(head_lanes(0),grad_query[0],grad_query[1])*(HEAD_DIM**-0.5)).astype(jnp.bfloat16)
    dk_ref[0]=(dk_sum[...]*(HEAD_DIM**-0.5)).astype(jnp.bfloat16)
    dv_ref[0]=dv_sum[...].astype(jnp.bfloat16)

def wide_table(table):
    return jnp.tile(jnp.pad(table,((0,SPAN-table.shape[0]),(0,0))),(1,LANES//HEAD_DIM))

def specs(clips,rows,width):
    own=pl.BlockSpec((1,rows,LANES),lambda c,h:(c,0,h))
    ext=pl.BlockSpec((1,rows+LEFT+BACK_PAD,LANES),lambda c,h:(c,0,h))
    tab=pl.BlockSpec((SPAN,LANES),lambda c,h:(0,0))
    return (pl.BlockSpec(memory_space=pltpu.SMEM),own,ext,tab),(clips,width//LANES)

def attend(query,keys,values,table,rows):
    clips,_,width=query.shape
    first=lax.axis_index('seq').astype(jnp.int32)[None]*rows
    limit=rows*lax.axis_size('seq')
    (sc,own,ext,tab),grid=specs(clips,rows,width)
    return pl.pallas_call(functools.partial(attend_kernel,limit),grid=grid,
        in_specs=[sc,own,ext,ext,tab],out_specs=own,
        out_shape=jax.ShapeDtypeStruct(query.shape,jnp.bfloat16),name="attend",
    )(first,query,keys,values,wide_table(table))

def attend_back(query,keys,values,table,grad,rows):
    clips,_,width=query.shape
    first=lax.axis_index('seq').astype(jnp.int32)[None]*rows
    limit=rows*lax.axis_size('seq')
    (sc,own,ext,tab),grid=specs(clips,rows,width)
    dq,dk,dv,dt=pl.pallas_call(functools.partial(attend_back_kernel,limit),grid=grid,
        in_specs=[sc,own,ext,ext,tab,own],out_specs=[own,ext,ext,tab],
        out_shape=[jax.ShapeDtypeStruct(query.shape,jnp.bfloat16),jax.ShapeDtypeStruct(keys.shape,jnp.bfloat16),jax.ShapeDtypeStruct(keys.shape,jnp.bfloat16),jax.ShapeDtypeStruct((SPAN,LANES),jnp.float32)],
        scratch_shapes=[pltpu.VMEM((rows+LEFT+BACK_PAD,LANES),jnp.float32)]*2,name="attend_back",
    )(first,query,keys,values,wide_table(table),grad)
    return dq,dk,dv,(dt[:WIN,:HEAD_DIM]+dt[:WIN,HEAD_DIM:])*(HEAD_DIM**-0.5)
def depth_of():
    return lax.axis_size("group") // 2


def place():
    group = lax.axis_index("group")
    return (group // 2, group % 2, lax.axis_index("seq"), lax.axis_index("replica"))


def greet(peers):
    barrier = pltpu.get_barrier_semaphore()
    for peer in peers:
        pl.semaphore_signal(barrier, inc=1, device_id=peer, device_id_type=MESH)
    pl.semaphore_wait(barrier, len(peers))


def neighbours():
    z, x, seq, replica = place()
    depth = depth_of()
    deep = [{"group": (z + steps) % depth * 2 + x} for steps in range(1, depth)]
    across = {"group": z * 2 + 1 - x}
    beside = {"seq": 1 - seq}
    twin = {"replica": 1 - replica}
    return (deep, across, beside, twin)


class Gather:
    def __init__(self, source, target, cut, low, high, rows, sends, recvs, at):
        depth = depth_of()
        self.source, self.target, self.cut, self.low, self.rows = (source, target, cut, low, rows)
        self.piece = (high - low) // (1, 2, 4)[cut]
        self.sends, self.recvs, self.at = (sends, recvs, at)
        self.z, self.x, self.seq, self.replica = place()
        self.deep, self.across, self.beside, self.twin = neighbours()
        self.depth = depth
        self.firsts = (0, depth - 1, 2 * depth - 1, 4 * depth - 2)
        self.started = []

    def spot(self, ref, owner, dy, dc):
        part = 0
        if self.cut:
            part = (self.replica + dc) % 2
        if self.cut == 2:
            part = part + 2 * ((self.seq + dy) % 2)
        first = pl.multiple_of(owner * self.rows + self.low + part * self.piece, self.piece)
        return ref.at[:, pl.ds(first, self.piece)]

    def owner(self, steps, dx):
        return (self.z + self.depth - steps) % self.depth * 2 + (self.x + dx) % 2

    def copy(self, steps, dx, dy, dc, kind, index, peer):
        mine = steps == 0 and dx == 0
        slot = self.at + self.firsts[kind] + index
        spot = self.spot(self.target, self.owner(steps, dx), dy, dc)
        return pltpu.make_async_remote_copy(
            src_ref=self.spot(self.source, 0, dy, dc) if mine else spot,
            dst_ref=spot,
            send_sem=self.sends.at[slot],
            recv_sem=self.recvs.at[slot],
            device_id=peer,
            device_id_type=MESH,
        )

    def send(self, copy):
        copy.start()
        self.started.append(copy)

    def to_beside(self, steps, dx):
        if self.cut == 2:
            index = dx * self.depth + steps - 1
            self.send(self.copy(steps, dx, 0, 0, 2, index, self.beside))

    def to_twin(self, steps, dx, dy):
        if self.cut:
            index = dy * (2 * self.depth - 1) + dx * self.depth + steps - 1
            self.send(self.copy(steps, dx, dy, 0, 3, index, self.twin))

    def open(self):
        for steps, peer in enumerate(self.deep, 1):
            self.send(self.copy(0, 0, 0, 0, 0, steps - 1, peer))
        self.send(self.copy(0, 0, 0, 0, 1, 0, self.across))

    def got(self, steps, dx, dy, dc, kind, index):
        self.copy(steps or self.depth, dx, dy, dc, kind, index, self.twin).wait_recv()

    def forward_deep(self):
        for steps in range(1, self.depth):
            self.got(steps, 0, 0, 0, 0, steps - 1)
            self.send(self.copy(steps, 0, 0, 0, 1, steps, self.across))
            self.to_beside(steps, 0)
            self.to_twin(steps, 0, 0)

    def forward_across(self):
        for steps in range(self.depth):
            self.got(steps, 1, 0, 0, 1, steps)
            self.to_beside(steps, 1)
            self.to_twin(steps, 1, 0)

    def others(self):
        return [(steps, dx) for dx in range(2) for steps in range(self.depth) if steps or dx]

    def forward_beside(self):
        if self.cut == 2:
            for steps, dx in self.others():
                self.got(steps, dx, 1, 0, 2, dx * self.depth + steps - 1)
                self.to_twin(steps, dx, 1)

    def close(self):
        if self.cut:
            for dy in range(self.cut):
                for steps, dx in self.others():
                    index = dy * (2 * self.depth - 1) + dx * self.depth + steps - 1
                    self.got(steps, dx, dy, 1, 3, index)
        for copy in self.started:
            copy.wait_send()


def gather_kernel(plan, count, *refs):
    ins, outs = (refs[:count], refs[count : count + len(plan)])
    helds, (sends, recvs, local) = (refs[count + len(plan) : -3], refs[-3:])
    deep, across, beside, twin = neighbours()
    peers = deep + [across, twin]
    if any(cut == 2 for _, _, cut, _ in plan):
        peers.append(beside)
    greet(peers)
    loads = [
        pltpu.make_async_copy(ins[at], held, local.at[0, at]) for at, held in enumerate(helds)
    ]
    for load in loads:
        load.start()
    jobs, stores, at = ([], [], 0)
    for number, (source, layers, cut, chunks) in enumerate(plan):
        ref = ins[source].at[pl.ds(layers[0], layers[1])]
        rows = ins[source].shape[1]
        for chunk in range(chunks):
            low, high = (rows * chunk // chunks, rows * (chunk + 1) // chunks)
            jobs.append(Gather(ref, outs[number], cut, low, high, rows, sends, recvs, at))
            at += (2, 6, 8)[cut] * depth_of()
    z, x, _, _ = place()
    ready = set()
    for tick in range(len(jobs) + 4):
        if tick < len(jobs):
            jobs[tick].open()
        if 1 <= tick < len(jobs) + 1:
            jobs[tick - 1].forward_deep()
        if 2 <= tick < len(jobs) + 2:
            jobs[tick - 2].forward_across()
        if 3 <= tick < len(jobs) + 3:
            jobs[tick - 3].forward_beside()
        if 4 <= tick:
            jobs[tick - 4].close()
        if tick < len(plan):
            source, layers, _, _ = plan[tick]
            if source not in ready:
                loads[source].wait()
                ready.add(source)
            rows = ins[source].shape[1]
            first = pl.multiple_of((z * 2 + x) * rows, rows)
            store = pltpu.make_async_copy(
                helds[source].at[pl.ds(layers[0], layers[1])],
                outs[tick].at[:, pl.ds(first, rows)],
                local.at[1, tick],
            )
            store.start()
            stores.append(store)
    for store in stores:
        store.wait()


def gather_weights(shards, plan):
    groups = lax.axis_size("group")
    total = sum((2, 6, 8)[cut] * depth_of() * chunks for _, _, cut, chunks in plan)
    return pl.pallas_call(
        functools.partial(gather_kernel, plan, len(shards)),
        in_specs=[pl.BlockSpec(memory_space=pl.ANY)] * len(shards),
        out_specs=[pl.BlockSpec(memory_space=pl.ANY)] * len(plan),
        out_shape=[
            jax.ShapeDtypeStruct(
                (layers[1], groups * shards[source].shape[1], shards[source].shape[2]), jnp.bfloat16
            )
            for source, layers, _, _ in plan
        ],
        scratch_shapes=[pltpu.VMEM(shard.shape, jnp.bfloat16) for shard in shards]
        + [
            pltpu.SemaphoreType.DMA((total,)),
            pltpu.SemaphoreType.DMA((total,)),
            pltpu.SemaphoreType.DMA((2, len(plan))),
        ],
        compiler_params=pltpu.CompilerParams(
            collective_id=1, has_side_effects=True, vmem_limit_bytes=24 << 20
        ),
        name="gather_weights",
    )(*shards)


def swap(value, axis, bit=1):
    return lax.ppermute(value, axis, [(i, i ^ bit) for i in range(lax.axis_size(axis))])


def along_depth(value, steps):
    depth = depth_of()
    pairs = [(i, (i // 2 + steps) % depth * 2 + i % 2) for i in range(2 * depth)]
    return lax.ppermute(value, "group", pairs)


def butterfly(value):
    for axis in ("replica", "seq", "group"):
        bit = 1
        while bit < lax.axis_size(axis):
            value = value + swap(value, axis, bit)
            bit *= 2
    return value


def reduce_gradient(left, right, halve):
    own_z, own_x, own_seq, own_replica = place()
    depth = depth_of()
    rows = left.shape[1] // (2 * depth)
    half = right.shape[1] // 2
    size = half // 2 if halve else half

    def product(part, replica, seq):
        first = replica * half + (seq * size if halve else 0)
        return matmul_left_t(part, lax.dynamic_slice_in_dim(right, first, size, 1))

    def side(value, x, axis):
        lead = value.shape[:axis]
        split = value.reshape(lead + (depth, 2, rows) + value.shape[axis + 1 :])
        picked = lax.dynamic_index_in_dim(split, x, axis + 1, False)
        return picked.reshape(lead + (depth * rows,) + value.shape[axis + 1 :])

    arrived = []
    if halve:
        far = swap(product(left, 1 - own_replica, 1 - own_seq).astype(jnp.bfloat16), "replica")
        arrived.append(swap(product(left, 1 - own_replica, own_seq).astype(jnp.bfloat16), "replica"))
        far = product(left, own_replica, 1 - own_seq) + far.astype(jnp.float32)
        arrived.append(swap(far.astype(jnp.bfloat16), "seq"))
    else:
        arrived.append(swap(product(left, 1 - own_replica, 0).astype(jnp.bfloat16), "replica"))

    def near(x):
        total = product(side(left, x, 1), own_replica, own_seq)
        for member in arrived:
            total = total + side(member, x, 0).astype(jnp.float32)
        return total

    away = swap(near((own_x + 1) % 2).astype(jnp.bfloat16), "group")
    mine = (near(own_x) + away.astype(jnp.float32)).astype(jnp.bfloat16).reshape(depth, rows, size)
    total = lax.dynamic_index_in_dim(mine, own_z, 0, False).astype(jnp.float32)
    for steps in range(1, depth):
        sent = lax.dynamic_index_in_dim(mine, (own_z + steps) % depth, 0, False)
        total = total + along_depth(sent, steps).astype(jnp.float32)
    owned = total.astype(jnp.bfloat16)
    if halve:
        other = swap(owned, "seq")
        owned = jnp.where(
            own_seq == 0, jnp.concatenate([owned, other], 1), jnp.concatenate([other, owned], 1)
        )
    else:
        bit = 1
        while bit < lax.axis_size("seq"):
            owned = owned.astype(jnp.float32) + swap(owned, "seq", bit).astype(jnp.float32)
            owned = owned.astype(jnp.bfloat16)
            bit *= 2
    other = swap(owned, "replica")
    owned = jnp.where(
        own_replica == 0, jnp.concatenate([owned, other], 1), jnp.concatenate([other, owned], 1)
    )
    return owned.astype(jnp.float32)


def feed_forward(resid, gain, w_in, w_out):
    normed, normal, inverse = norm_forward(resid, gain)
    entry = normed.astype(jnp.bfloat16)
    hidden_pre = matmul(entry, w_in)
    hidden = (hidden_pre * jax.nn.sigmoid(hidden_pre)).astype(jnp.bfloat16)
    return (matmul(hidden, w_out), (normal, inverse, entry, hidden_pre, hidden))


def feed_back(grad_branch, kept, gain, w_in, w_out, halve):
    normal, inverse, entry, hidden_pre, hidden = kept
    grad_low = grad_branch.astype(jnp.bfloat16)
    grad_w_out = reduce_gradient(hidden, grad_low, halve)
    grad_hidden = (matmul_right_t(grad_low, w_out) * swish_grad(hidden_pre)).astype(jnp.bfloat16)
    grad_w_in = reduce_gradient(entry, grad_hidden, halve)
    grad_in, grad_gain = norm_backward(matmul_right_t(grad_hidden, w_in), normal, inverse, gain)
    return (grad_in, grad_gain, grad_w_in, grad_w_out)


def attention_forward(resid, gain, qkv, attn_out, table, shape):
    clips, rows, width = shape
    normed, normal, inverse = norm_forward(resid, gain)
    entry = normed.astype(jnp.bfloat16)
    query, keys, values = [
        matmul(entry, qkv[part]).astype(jnp.bfloat16).reshape(shape) for part in range(3)
    ]
    tail = jnp.zeros((clips, BACK_PAD - RIGHT, width), jnp.bfloat16)

    def extend(value):
        before = from_behind(value[:, rows - LEFT :], "seq", 1)
        after = from_behind(value[:, :RIGHT], "seq", -1)
        return jnp.concatenate([before, value, after, tail], 1)

    keys, values = (extend(keys), extend(values))
    mixed = attend(query, keys, values, table, rows).reshape(clips * rows, width)
    return (matmul(mixed, attn_out), (normal, inverse, entry, query, keys, values, mixed))


def attention_back(grad_branch, kept, gain, qkv, attn_out, table, shape):
    clips, rows, width = shape
    normal, inverse, entry, query, keys, values, mixed = kept
    grad_low = grad_branch.astype(jnp.bfloat16)
    grad_attn_out = reduce_gradient(mixed, grad_low, False)
    grad_mixed = matmul_right_t(grad_low, attn_out).astype(jnp.bfloat16).reshape(shape)
    grad_query, grad_keys, grad_values, grad_table = attend_back(
        query, keys, values, table, grad_mixed, rows
    )

    def fold(grad):
        from_later = from_behind(grad[:, :LEFT], "seq", -1).astype(jnp.float32)
        from_earlier = from_behind(grad[:, LEFT + rows : LEFT + rows + RIGHT], "seq", 1)
        own = grad[:, LEFT : LEFT + rows].astype(jnp.float32)
        own = own + jnp.pad(from_later, ((0, 0), (rows - LEFT, 0), (0, 0)))
        own = own + jnp.pad(from_earlier.astype(jnp.float32), ((0, 0), (0, rows - RIGHT), (0, 0)))
        return own.astype(jnp.bfloat16).reshape(clips * rows, width)

    parts = [grad_query.reshape(clips * rows, width), fold(grad_keys), fold(grad_values)]
    grad_qkv = reduce_gradient(entry, jnp.concatenate(parts, 1), False)
    grad_qkv = grad_qkv.reshape(-1, 3, width).transpose(1, 0, 2)
    grad_entry = sum(matmul_right_t(part, qkv[at]) for at, part in enumerate(parts))
    grad_in, grad_gain = norm_backward(grad_entry, normal, inverse, gain)
    return (grad_in, grad_gain, grad_qkv, grad_attn_out, grad_table)


def conv_forward(resid, gain_in, gain_mid, conv_in, depthwise, conv_out, shape):
    clips, rows, width = shape
    normed, normal, inverse = norm_forward(resid, gain_in)
    entry = normed.astype(jnp.bfloat16)
    joined = matmul(entry, conv_in)
    opened = jax.nn.sigmoid(joined[:, width:])
    glu = (joined[:, :width] * opened).astype(jnp.bfloat16).reshape(clips, rows, width)
    before = from_behind(glu[:, rows - (KERNEL - 1) :], "seq", 1)
    padded = jnp.concatenate([before, glu], 1).astype(jnp.float32)
    taps = depthwise.astype(jnp.float32)
    summed = jnp.zeros((clips, rows, width), jnp.float32)
    for tap in range(KERNEL):
        summed = summed + taps[tap] * padded[:, tap : tap + rows]
    middle, mid_normal, mid_inverse = norm_forward(summed.reshape(clips * rows, width), gain_mid)
    swished = (middle * jax.nn.sigmoid(middle)).astype(jnp.bfloat16)
    kept = (
        normal,
        inverse,
        entry,
        joined,
        opened,
        padded,
        middle,
        mid_normal,
        mid_inverse,
        swished,
    )
    return (matmul(swished, conv_out), kept)


def conv_back(grad_branch, kept, gain_in, gain_mid, conv_in, depthwise, conv_out, shape):
    clips, rows, width = shape
    normal, inverse, entry, joined, opened, padded, middle, mid_normal, mid_inverse, swished = kept
    taps = depthwise.astype(jnp.float32)
    grad_low = grad_branch.astype(jnp.bfloat16)
    grad_conv_out = reduce_gradient(swished, grad_low, False)
    grad_middle = matmul_right_t(grad_low, conv_out) * swish_grad(middle)
    grad_summed, grad_gain_mid = norm_backward(grad_middle, mid_normal, mid_inverse, gain_mid)
    grad_summed = grad_summed.reshape(clips, rows, width)
    grad_taps = jnp.stack(
        [jnp.sum(grad_summed * padded[:, tap : tap + rows], (0, 1)) for tap in range(KERNEL)]
    )
    grad_padded = jnp.zeros((clips, rows + KERNEL - 1, width), jnp.float32)
    for tap in range(KERNEL):
        grad_padded = grad_padded + jnp.pad(
            grad_summed * taps[tap], ((0, 0), (tap, KERNEL - 1 - tap), (0, 0))
        )
    from_later = from_behind(grad_padded[:, : KERNEL - 1].astype(jnp.bfloat16), "seq", -1).astype(
        jnp.float32
    )
    grad_glu = (
        grad_padded[:, KERNEL - 1 :]
        .at[:, rows - (KERNEL - 1) :]
        .add(from_later)
        .reshape(clips * rows, width)
    )
    value_part = joined[:, :width]
    grad_joined = jnp.concatenate(
        [grad_glu * opened, grad_glu * value_part * opened * (1.0 - opened)], 1
    )
    grad_joined = grad_joined.astype(jnp.bfloat16)
    grad_conv_in = reduce_gradient(entry, grad_joined, False)
    grad_in, grad_gain_in = norm_backward(
        matmul_right_t(grad_joined, conv_in), normal, inverse, gain_in
    )
    return (grad_in, grad_gain_in, grad_gain_mid, grad_conv_in, grad_taps, grad_conv_out)


def on_device(
    tokens,
    ffn_in,
    ffn_out,
    qkv,
    attn_out,
    conv_in,
    conv_out,
    depthwise,
    gains,
    rel_table,
    cotangent,
):
    clips, rows, width = tokens.shape
    shape = (clips, rows, width)
    flat_rows = clips * rows
    halve = lax.axis_size("seq") == 2
    norms, taps = (gains.shape[0], depthwise.shape[0])
    lines = -(-(norms + taps) // 16) * 16
    small = jnp.concatenate([gains, depthwise], 0)
    small = jnp.pad(small, ((0, lines - norms - taps), (0, 0)))[None]
    shards = (small, ffn_in, ffn_out, qkv, attn_out[None], conv_in[None], conv_out[None])
    cut = 2 if halve else 1
    plan = (
        (0, (0, 1), 0, 1),
        (1, (0, 1), cut, 2),
        (2, (0, 1), cut, 2),
        (3, (0, 3), 1, 1),
        (4, (0, 1), 1, 1),
        (5, (0, 1), 1, 1),
        (6, (0, 1), 1, 1),
        (1, (1, 1), cut, 2),
        (2, (1, 1), cut, 2),
    )
    gathered = gather_weights(shards, plan)
    small = gathered[0].reshape(-1, lines, gains.shape[1]).transpose(1, 0, 2).reshape(lines, width)
    gain_f = small[:norms].astype(jnp.float32)
    depth = small[norms : norms + taps]
    f_in = (gathered[1][0], gathered[7][0])
    f_out = (gathered[2][0], gathered[8][0])
    proj, a_out, c_in, c_out = (gathered[3], gathered[4][0], gathered[5][0], gathered[6][0])
    start = tokens.reshape(flat_rows, width).astype(jnp.float32)
    first_branch, first_kept = feed_forward(start, gain_f[0], f_in[0], f_out[0])
    after_first = start + 0.5 * first_branch
    attn_branch, attn_kept = attention_forward(
        after_first, gain_f[1], proj, a_out, rel_table, shape
    )
    after_attn = after_first + attn_branch
    conv_branch, conv_kept = conv_forward(
        after_attn, gain_f[2], gain_f[3], c_in, depth, c_out, shape
    )
    after_conv = after_attn + conv_branch
    second_branch, second_kept = feed_forward(after_conv, gain_f[4], f_in[1], f_out[1])
    final = after_conv + 0.5 * second_branch
    result, final_normal, final_inverse = norm_forward(final, gain_f[5])
    squares = jnp.stack(
        [
            jnp.sum(member * member)
            for member in (final, first_branch, attn_branch, conv_branch, second_branch)
        ]
    )
    grad = cotangent.reshape(flat_rows, width).astype(jnp.float32)
    grad, grad_gain_final = norm_backward(grad, final_normal, final_inverse, gain_f[5])
    back_in, grad_gain_second, grad_in_second, grad_out_second = feed_back(
        0.5 * grad, second_kept, gain_f[4], f_in[1], f_out[1], halve
    )
    grad = grad + back_in
    back_in, grad_gain_conv, grad_gain_mid, grad_conv_in, grad_taps, grad_conv_out = conv_back(
        grad, conv_kept, gain_f[2], gain_f[3], c_in, depth, c_out, shape
    )
    grad = grad + back_in
    back_in, grad_gain_attn, grad_qkv, grad_attn_out, grad_table = attention_back(
        grad, attn_kept, gain_f[1], proj, a_out, rel_table, shape
    )
    grad = grad + back_in
    back_in, grad_gain_first, grad_in_first, grad_out_first = feed_back(
        0.5 * grad, first_kept, gain_f[0], f_in[0], f_out[0], halve
    )
    grad = grad + back_in
    gain_grads = jnp.stack(
        [
            grad_gain_first,
            grad_gain_attn,
            grad_gain_conv,
            grad_gain_mid,
            grad_gain_second,
            grad_gain_final,
        ]
    )
    loose = jnp.concatenate([grad_table.reshape(-1), squares])
    lines = -(-loose.shape[0] // width)
    loose = jnp.pad(loose, (0, lines * width - loose.shape[0])).reshape(lines, width)
    totals = butterfly(jnp.concatenate([gain_grads, grad_taps, loose], 0))
    owned = lax.dynamic_slice_in_dim(
        totals[: norms + taps], lax.axis_index("group") * gains.shape[1], gains.shape[1], 1
    )
    loose = totals[norms + taps :].reshape(-1)
    table_size = rel_table.shape[0] * rel_table.shape[1]
    count = (
        flat_rows * width * lax.axis_size("seq") * lax.axis_size("group") * lax.axis_size("replica")
    )
    stats = jnp.sqrt(loose[table_size : table_size + 5] / count)
    return (
        result.astype(jnp.bfloat16).reshape(shape),
        grad.astype(jnp.bfloat16).reshape(shape),
        jnp.stack([grad_in_first, grad_in_second]),
        jnp.stack([grad_out_first, grad_out_second]),
        grad_qkv,
        grad_attn_out,
        grad_conv_in,
        grad_conv_out,
        owned[norms:],
        owned[:norms],
        loose[:table_size].reshape(rel_table.shape),
        stats,
    )


def solution(mesh):
    in_specs = (
        P(("group", "replica"), "seq", None),
        P(None, "group", None),
        P(None, "group", None),
        P(None, "group", None),
        P("group", None),
        P("group", None),
        P("group", None),
        P(None, "group"),
        P(None, "group"),
        P(),
        P(("group", "replica"), "seq", None),
    )
    out_specs = (
        P(("group", "replica"), "seq", None),
        P(("group", "replica"), "seq", None),
        P(None, "group", None),
        P(None, "group", None),
        P(None, "group", None),
        P("group", None),
        P("group", None),
        P("group", None),
        P(None, "group"),
        P(None, "group"),
        P(),
        P(),
    )
    return jax.shard_map(
        on_device, mesh=mesh, in_specs=in_specs, out_specs=out_specs, check_vma=False
    )
```

time: 2270 us -> 1340 us (0.59)
  waiting for transfers between devices: 1470 us -> 358 us
  Pallas kernels: 0 us -> 317 us
  starting transfers between devices: 14.8 us -> 122 us
  blocking collectives: 105 us -> 0 us
  local copies, waits for them, and re-layouts: 271 us -> 212 us
  matrix products: 242 us -> 199 us
    reduce_scatter x5 -> x0, waiting for transfers between devices: 797 us -> none  [the longest x1 286 us: on_device(): lax.psum_scatter(stacked_out.astype(jnp.bfloat16), 'group', scatter_dimen...]
    all_gather x6 -> x0, waiting for transfers between devices: 479 us -> none  [the longest x1 218 us: on_device(): lax.all_gather(ffn_out, 'group', axis=1, tiled=True)]
    ppermute x0 -> x69, waiting for transfers between devices: none -> 357 us  [the longest x45 266 us: swap(): lax.ppermute(value, axis, [(i, i ^ bit) for i in range(lax.axis_size(axis...]
    pallas_call x0 -> x3, Pallas kernels: none -> 317 us  [the longest x1 232 us: gather_weights(): pl.pallas_call(functools.partial(gather_kernel, plan, len(shards)), in_sp...]
    reshape x7 -> x10, local copies, waits for them, and re-layouts: 143 us -> 25.9 us  [the longest x5 20.1 us: side(): split = value.reshape(lead + (depth, 2, rows) + value.shape[axis + 1:])]
    psum x1 -> x0, waiting for transfers between devices: 107 us -> none  [on_device(): lax.psum(own_qkv.astype(jnp.bfloat16), ('seq', 'replica'))]
    ppermute x0 -> x69, starting transfers between devices: none -> 94.8 us  [the longest x24 53.7 us: along_depth(): return lax.ppermute(value, 'group', pairs)]
    unnamed x18 -> x0, waiting for transfers between devices: 83.4 us -> none
  transfers between devices with their start and end apart: 21 -> 79, of which waited for: 14 -> 25; matrix products, arithmetic and copies ran while one was open for 18% -> 23% of each run, Pallas kernels for 0% -> 5%
where the time goes in v1:
time: 1340 us; the launch traced here: 1330 us
  waiting for transfers between devices  358 us (27%)
  Pallas kernels  317 us (24%)
  local copies, waits for them, and re-layouts  212 us (16%)
  matrix products  199 us (15%)
  other arithmetic  123 us (9%)
  starting transfers between devices  122 us (9%)
    ppermute x45, waiting for transfers between devices, swap(): lax.ppermute(value, axis, [(i, i ^ bit) for i in range(lax.axis_size(axis...  266 us
    pallas_call x1, Pallas kernels, gather_weights(): pl.pallas_call(functools.partial(gather_kernel, plan, len(shards)), in_sp...  232 us
    unnamed x417, local copies, waits for them, and re-layouts  95.5 us
    ppermute x24, waiting for transfers between devices, along_depth(): return lax.ppermute(value, 'group', pairs)  90.8 us
    dot_general x32, matrix products, matmul_left_t(): lax.dot_general(left, right, (((0,), (0,)), ((), ())), preferred_element_...  78.8 us
    dot_general x10, matrix products, matmul(): return jnp.dot(left, right, preferred_element_type=jnp.float32)  62.4 us
    pallas_call x1, Pallas kernels, attend_back(): pl.pallas_call(functools.partial(attend_back_kernel, limit), grid=grid, i...  61 us
    dot_general x10, matrix products, matmul_right_t(): lax.dot_general(left, right, (((1,), (1,)), ((), ())), preferred_element_...  57.4 us
  transfers between devices with their start and end apart: 79, of which 25 were waited for; matrix products, arithmetic and copies ran while one was open for 23% of the time, Pallas kernels for 5%

profile of v1, /device:TPU:0, one launch (start us, length us, event | category | flops | bytes accessed | tf_op | source)
XLA Modules:
  0.0 1334.8 jit_solution(12821918101544603000)
XLA Ops:
  9.7 231.9 %gather_weights.1 = (bf16[1,384,128]{2,1,0:T(8,128)(2,1)S(1)}, bf16[1,1024,4096]{2,1,0:T(8,128)(2,1)S(1)}, bf16[1,4096,1024]{2,1,0:T(8,128)(2,1)}, bf16[3,1024,1...) custom-call(bf16[1,48,128]{2,1,0:T(8,128)(2,1)S(1)} %fusion.302.refs, ...), custom_call_target="tpu_custom_call" | custom-call | tf_op jit(solution)/shard_map/gather_weights/pallas_call | solution.py:341
  245.6 15.0 %fusion.23 = (bf16[512,4096]{1,0:T(8,128)(2,1)S(1)}, f32[512,4096]{1,0:T(8,128)}) fusion(bf16[1,1024,4096]{2,1,0:T(8,128)(2,1)} %copy-done.7, bf16[1,512,1024]{2,1,0:T(8,128)(2,1)S(1)} %copy-done.29, f32[1024]{0:T(1024)S(1)} %bitcast.808, f32[512]{0:T(512)S(1)} %add_rsqrt_fusion.5, f32[512]{0:T(512)S(1)} %broadcast_multiply_fusion.17), kind=kOutput, calls=%fused_computation.23 | convolution fusion | flops 4308074496 | bytes 22028288 | tf_op jit(solution)/shard_map/dot_general | solution.py:53
  311.8 9.8 constant_dynamic-slice_fusion.29
  330.8 10.5 copy.109
  341.3 10.6 copy.106
  355.3 24.6 %attend.1 = bf16[1,512,1024]{2,1,0:T(8,128)(2,1)} custom-call(s32[1]{0:T(128)} %bitcast.11.first_ref, bf16[1,512,1024]{2,1,0:T(8,128)(2,1)} %fusion.150.q_ref, bf16[1,640,1024]{2,1,0:T(8,128)(2,1)} %get-tuple-element.270.k_ref, bf16[1,640,1024]{2,1,0:T(8,128)(2,1)} %get-tuple-element.269.v_ref, bf16[256,128]{1,0:T(8,128)(2,1)} %copy.48.t_ref), custom_call_target="tpu_custom_call" | custom-call | tf_op jit(solution)/shard_map/attend/pallas_call | solution.py:153
  414.3 9.8 fusion.321
  439.5 13.7 %fusion.22 = (bf16[512,4096]{1,0:T(8,128)(2,1)}, f32[512,4096]{1,0:T(8,128)}) fusion(bf16[512,1024]{1,0:T(8,128)(2,1)} %multiply_convert_fusion.10, bf16[1,1024,4096]{2,1,0:T(8,128)(2,1)} %get-tuple-element.44), kind=kOutput, calls=%fused_computation.22 | convolution fusion | flops 4305453056 | bytes 22020096 | tf_op jit(solution)/shard_map/dot_general | solution.py:53
  461.3 10.4 fusion.319
  476.5 10.3 multiply_convert_fusion.1
  534.0 19.2 %pad_add_fusion = f32[1,542,1024]{2,1,0:T(8,128)S(1)} fusion(f32[1,512,1024]{2,1,0:T(8,128)S(1)} %get-tuple-element.161, f32[1,512,1024]{2,1,0:T(8,128)S(1)} %get-tuple-element.162, f32[1,512,1024]{2,1,0:T(8,128)S(1)} %get-tuple-element.163, f32[1,512,1024]{2,1,0:T(8,128)S(1)} %get-tuple-element.164, f32[1,512,1024]{2,1,0:T(8,128)} %get-tuple-element.165, ...), kind=kLoop, calls=%fused_computation.53 | loop fusion | flops 16650240 | bytes 67231744 | tf_op jit(solution)/shard_map/add | solution.py:547
  586.0 9.8 constant_dynamic-slice_fusion.23
  595.8 10.6 copy.112
  617.8 10.7 copy.115
  644.7 61.0 %attend_back.1 = (bf16[1,512,1024]{2,1,0:T(8,128)(2,1)}, bf16[1,640,1024]{2,1,0:T(8,128)(2,1)}, bf16[1,640,1024]{2,1,0:T(8,128)(2,1)}, f32[256,128]{1,0:T(8,128)}) custom-call(s32[1]{0:T(128)} %bitcast.11.first_ref, bf16[1,512,1024]{2,1,0:T(8,128)(2,1)} %fusion.150.q_ref, bf16[1,640,1024]{2,1,0:T(8,128)(2,1)} %get-tuple-element.270.k_ref, ...), custom_call_target="tpu_custom_call" | custom-call | tf_op jit(solution)/shard_map/attend_back/pallas_call | solution.py:163
  754.0 10.5 multiply_convert_fusion
  904.0 14.6 %collective-permute-done.61 = bf16[512,1024]{1,0:T(8,128)(2,1)S(1)} collective-permute-done((bf16[512,1024]{1,0:T(8,128)(2,1)S(1)}, bf16[512,1024]{1,0:T(8,128)(2,1)S(1)}, u32[]{:S(2)}, u32[]{:S(2)}) %collective-permute-start.61) | collective-permute-done | bytes 1048608 | tf_op jit(solution)/shard_map/ppermute | solution.py:365
  950.4 156.1 %collective-permute-done.65 = bf16[128,1024]{1,0:T(8,128)(2,1)S(1)} collective-permute-done((bf16[128,1024]{1,0:T(8,128)(2,1)S(1)}, bf16[128,1024]{1,0:T(8,128)(2,1)S(1)}, u32[]{:S(2)}, u32[]{:S(2)}) %collective-permute-start.65) | collective-permute-done | bytes 262176 | tf_op jit(solution)/shard_map/ppermute | solution.py:365
  1128.3 17.1 %collective-permute-done.47 = bf16[512,1536]{1,0:T(8,128)(2,1)S(1)} collective-permute-done((bf16[512,1536]{1,0:T(8,128)(2,1)S(1)}, bf16[512,1536]{1,0:T(8,128)(2,1)S(1)}, u32[]{:S(2)}, u32[]{:S(2)}) %collective-permute-start.47) | collective-permute-done | bytes 1572896 | tf_op jit(solution)/shard_map/ppermute | solution.py:365
  1154.9 35.5 %collective-permute-done.40 = bf16[2048,256]{1,0:T(8,128)(2,1)} collective-permute-done((bf16[2048,256]{1,0:T(8,128)(2,1)}, bf16[2048,256]{1,0:T(8,128)(2,1)}, u32[]{:S(2)}, u32[]{:S(2)}) %collective-permute-start.40) | collective-permute-done | bytes 1048608 | tf_op jit(solution)/shard_map/ppermute | solution.py:365
  1197.9 13.0 collective-permute-done.49
  1240.2 16.3 %collective-permute-done.24 = bf16[128,1024]{1,0:T(8,128)(2,1)S(1)} collective-permute-done((bf16[128,1024]{1,0:T(8,128)(2,1)S(1)}, bf16[128,1024]{1,0:T(8,128)(2,1)S(1)}, u32[]{:S(2)}, u32[]{:S(2)}) %collective-permute-start.24) | collective-permute-done | bytes 262176 | tf_op jit(solution)/shard_map/ppermute | solution.py:371
  1262.6 16.3 %collective-permute-done.42 = bf16[512,256]{1,0:T(8,128)(2,1)S(1)} collective-permute-done((bf16[512,256]{1,0:T(8,128)(2,1)S(1)}, bf16[512,256]{1,0:T(8,128)(2,1)S(1)}, u32[]{:S(2)}, u32[]{:S(2)}) %collective-permute-start.42) | collective-permute-done | bytes 262176 | tf_op jit(solution)/shard_map/ppermute | solution.py:371
  1282.2 13.6 %collective-permute-done.33 = bf16[512,256]{1,0:T(8,128)(2,1)S(1)} collective-permute-done((bf16[512,256]{1,0:T(8,128)(2,1)S(1)}, bf16[512,256]{1,0:T(8,128)(2,1)S(1)}, u32[]{:S(2)}, u32[]{:S(2)}) %collective-permute-start.33) | collective-permute-done | bytes 262176 | tf_op jit(solution)/shard_map/ppermute | solution.py:371
  (779 shorter events, 580.3 us)
Async XLA Ops:
  269.5 82.5 %collective-permute-start.3 = (bf16[1,8,1024]{2,1,0:T(8,128)(2,1)}, bf16[1,8,1024]{2,1,0:T(8,128)(2,1)}, u32[]{:S(2)}, u32[]{:S(2)}) collective-permute-start(bf16[1,8,1024]{2,1,0:T(8,128)(2,1)} %slice.532), channel_id=1, source_target_pairs={{16,0},{17,1},{18,2},{19,3},{20,4},{21,5},{22,6},{23,7},{24,8},{25... | collective-permute-start | bytes 49160 | tf_op jit(solution)/shard_map/ppermute | solution.py:31
  271.4 80.6 %collective-permute-start.2 = (bf16[1,64,1024]{2,1,0:T(8,128)(2,1)}, bf16[1,64,1024]{2,1,0:T(8,128)(2,1)S(1)}, u32[]{:S(2)}, u32[]{:S(2)}) collective-permute-start(bf16[1,64,1024]{2,1,0:T(8,128)(2,1)} %slice.531), channel_id=1, source_target_pairs={{0,16},{1,17},{2,18},{3,19},{4,20},{5,21},{6,22},{7,23},{8,24},{9,... | collective-permute-start | bytes 393224 | tf_op jit(solution)/shard_map/ppermute | solution.py:31
  278.6 73.5 %collective-permute-start.1 = (bf16[1,8,1024]{2,1,0:T(8,128)(2,1)}, bf16[1,8,1024]{2,1,0:T(8,128)(2,1)}, u32[]{:S(2)}, u32[]{:S(2)}) collective-permute-start(bf16[1,8,1024]{2,1,0:T(8,128)(2,1)} %slice.530), channel_id=1, source_target_pairs={{16,0},{17,1},{18,2},{19,3},{20,4},{21,5},{22,6},{23,7},{24,8},{25... | collective-permute-start | bytes 49160 | tf_op jit(solution)/shard_map/ppermute | solution.py:31
  280.5 71.5 %collective-permute-start = (bf16[1,64,1024]{2,1,0:T(8,128)(2,1)}, bf16[1,64,1024]{2,1,0:T(8,128)(2,1)S(1)}, u32[]{:S(2)}, u32[]{:S(2)}) collective-permute-start(bf16[1,64,1024]{2,1,0:T(8,128)(2,1)} %slice.529), channel_id=1, source_target_pairs={{0,16},{1,17},{2,18},{3,19},{4,20},{5,21},{6,22},{7,23},{8,24},{9,... | collective-permute-start | bytes 393224 | tf_op jit(solution)/shard_map/ppermute | solution.py:31
  576.0 213.4 %collective-permute-start.67 = (bf16[1024,512]{1,0:T(8,128)(2,1)}, bf16[1024,512]{1,0:T(8,128)(2,1)}, u32[]{:S(2)}, u32[]{:S(2)}) collective-permute-start(bf16[1024,512]{1,0:T(8,128)(2,1)} %convolution_convert_fusion.10), channel_id=1, source_target_pairs={{0,1},{1,0},{2,3},{3,2},{4,5},{5,4},{6,7},{7,6},{8,9},{9,8},{10,11... | collective-permute-start | bytes 3145736 | tf_op jit(solution)/shard_map/ppermute | solution.py:365
  585.3 282.0 %collective-permute-start.37 = (bf16[4096,256]{1,0:T(8,128)(2,1)}, bf16[4096,256]{1,0:T(8,128)(2,1)}, u32[]{:S(2)}, u32[]{:S(2)}) collective-permute-start(bf16[4096,256]{1,0:T(8,128)(2,1)} %convolution_convert_fusion.1), channel_id=1, source_target_pairs={{0,1},{1,0},{2,3},{3,2},{4,5},{5,4},{6,7},{7,6},{8,9},{9,8},{10,11... | collective-permute-start | bytes 6291464 | tf_op jit(solution)/shard_map/ppermute | solution.py:365
  617.8 269.0 %collective-permute-start.19 = (bf16[1024,1024]{1,0:T(8,128)(2,1)}, bf16[1024,1024]{1,0:T(8,128)(2,1)}, u32[]{:S(2)}, u32[]{:S(2)}) collective-permute-start(bf16[1024,1024]{1,0:T(8,128)(2,1)} %convolution_convert_fusion.7), channel_id=1, source_target_pairs={{0,1},{1,0},{2,3},{3,2},{4,5},{5,4},{6,7},{7,6},{8,9},{9,8},{10,11... | collective-permute-start | bytes 6291464 | tf_op jit(solution)/shard_map/ppermute | solution.py:365
  740.1 52.6 %collective-permute-start.53 = (bf16[1024,512]{1,0:T(8,128)(2,1)}, bf16[1024,512]{1,0:T(8,128)(2,1)}, u32[]{:S(2)}, u32[]{:S(2)}) collective-permute-start(bf16[1024,512]{1,0:T(8,128)(2,1)} %convolution_convert_fusion.11), channel_id=1, source_target_pairs={{0,1},{1,0},{2,3},{3,2},{4,5},{5,4},{6,7},{7,6},{8,9},{9,8},{10,11... | collective-permute-start | bytes 3145736 | tf_op jit(solution)/shard_map/ppermute | solution.py:365
  836.6 45.1 %collective-permute-start.20 = (bf16[1024,1024]{1,0:T(8,128)(2,1)}, bf16[1024,1024]{1,0:T(8,128)(2,1)}, u32[]{:S(2)}, u32[]{:S(2)}) collective-permute-start(bf16[1024,1024]{1,0:T(8,128)(2,1)} %convolution_convert_fusion.6), channel_id=1, source_target_pairs={{0,1},{1,0},{2,3},{3,2},{4,5},{5,4},{6,7},{7,6},{8,9},{9,8},{10,11... | collective-permute-start | bytes 6291464 | tf_op jit(solution)/shard_map/ppermute | solution.py:365
  881.8 39.9 %collective-permute-start.11 = (bf16[1024,1024]{1,0:T(8,128)(2,1)}, bf16[1024,1024]{1,0:T(8,128)(2,1)}, u32[]{:S(2)}, u32[]{:S(2)}) collective-permute-start(bf16[1024,1024]{1,0:T(8,128)(2,1)} %convolution_convert_fusion.8), channel_id=1, source_target_pairs={{0,1},{1,0},{2,3},{3,2},{4,5},{5,4},{6,7},{7,6},{8,9},{9,8},{10,11... | collective-permute-start | bytes 6291464 | tf_op jit(solution)/shard_map/ppermute | solution.py:365
  886.7 61.6 %collective-permute-start.46 = (bf16[1024,1536]{1,0:T(8,128)(2,1)S(1)}, bf16[1024,1536]{1,0:T(8,128)(2,1)S(1)}, u32[]{:S(2)}, u32[]{:S(2)}) collective-permute-start(bf16[1024,1536]{1,0:T(8,128)(2,1)S(1)} %copy-done.198), channel_id=1, source_target_pairs={{0,1},{1,0},{2,3},{3,2},{4,5},{5,4},{6,7},{7,6},{8,9},{9,8},{10,11... | collective-permute-start | bytes 9437192 | tf_op jit(solution)/shard_map/ppermute | solution.py:365
  918.6 192.2 %collective-permute-start.21 = (bf16[1024,1024]{1,0:T(8,128)(2,1)}, bf16[1024,1024]{1,0:T(8,128)(2,1)S(1)}, u32[]{:S(2)}, u32[]{:S(2)}) collective-permute-start(bf16[1024,1024]{1,0:T(8,128)(2,1)} %add_convert_fusion.2), channel_id=1, source_target_pairs={{0,16},{16,0},{1,17},{17,1},{2,18},{18,2},{3,19},{19,3},{4,20},{20... | collective-permute-start | bytes 6291464 | tf_op jit(solution)/shard_map/ppermute | solution.py:365
  927.2 187.1 %collective-permute-start.39 = (bf16[4096,256]{1,0:T(8,128)(2,1)}, bf16[4096,256]{1,0:T(8,128)(2,1)S(1)}, u32[]{:S(2)}, u32[]{:S(2)}) collective-permute-start(bf16[4096,256]{1,0:T(8,128)(2,1)} %add_convert_fusion), channel_id=1, source_target_pairs={{0,16},{16,0},{1,17},{17,1},{2,18},{18,2},{3,19},{19,3},{4,20},{20... | collective-permute-start | bytes 6291464 | tf_op jit(solution)/shard_map/ppermute | solution.py:365
  936.9 182.6 %collective-permute-start.30 = (bf16[4096,256]{1,0:T(8,128)(2,1)}, bf16[4096,256]{1,0:T(8,128)(2,1)S(1)}, u32[]{:S(2)}, u32[]{:S(2)}) collective-permute-start(bf16[4096,256]{1,0:T(8,128)(2,1)} %add_convert_fusion.1), channel_id=1, source_target_pairs={{0,16},{16,0},{1,17},{17,1},{2,18},{18,2},{3,19},{19,3},{4,20},{20... | collective-permute-start | bytes 6291464 | tf_op jit(solution)/shard_map/ppermute | solution.py:365
  947.9 175.9 %collective-permute-start.12 = (bf16[1024,1024]{1,0:T(8,128)(2,1)}, bf16[1024,1024]{1,0:T(8,128)(2,1)S(1)}, u32[]{:S(2)}, u32[]{:S(2)}) collective-permute-start(bf16[1024,1024]{1,0:T(8,128)(2,1)} %add_convert_fusion.3), channel_id=1, source_target_pairs={{0,16},{16,0},{1,17},{17,1},{2,18},{18,2},{3,19},{19,3},{4,20},{20... | collective-permute-start | bytes 6291464 | tf_op jit(solution)/shard_map/ppermute | solution.py:365
  948.4 158.1 %collective-permute-start.65 = (bf16[128,1024]{1,0:T(8,128)(2,1)S(1)}, bf16[128,1024]{1,0:T(8,128)(2,1)S(1)}, u32[]{:S(2)}, u32[]{:S(2)}) collective-permute-start(bf16[128,1024]{1,0:T(8,128)(2,1)S(1)} %fusion.209), channel_id=1, source_target_pairs={{0,16},{16,0},{1,17},{17,1},{2,18},{18,2},{3,19},{19,3},{4,20},{20... | collective-permute-start | bytes 786440 | tf_op jit(solution)/shard_map/ppermute | solution.py:365
  1113.8 78.8 %collective-permute-start.22 = (bf16[512,1024]{1,0:T(8,128)(2,1)}, bf16[512,1024]{1,0:T(8,128)(2,1)}, u32[]{:S(2)}, u32[]{:S(2)}) collective-permute-start(bf16[512,1024]{1,0:T(8,128)(2,1)} %fusion.50), channel_id=1, source_target_pairs={{0,2},{2,0},{4,6},{6,4},{8,10},{10,8},{12,14},{14,12},{1,3},{3,1},... | collective-permute-start | bytes 3145736 | tf_op jit(solution)/shard_map/ppermute | solution.py:365
  1118.0 72.4 %collective-permute-start.40 = (bf16[2048,256]{1,0:T(8,128)(2,1)}, bf16[2048,256]{1,0:T(8,128)(2,1)}, u32[]{:S(2)}, u32[]{:S(2)}) collective-permute-start(bf16[2048,256]{1,0:T(8,128)(2,1)} %fusion.44), channel_id=1, source_target_pairs={{0,2},{2,0},{4,6},{6,4},{8,10},{10,8},{12,14},{14,12},{1,3},{3,1},... | collective-permute-start | bytes 3145736 | tf_op jit(solution)/shard_map/ppermute | solution.py:365
  1123.3 99.2 %collective-permute-start.31 = (bf16[2048,256]{1,0:T(8,128)(2,1)}, bf16[2048,256]{1,0:T(8,128)(2,1)}, u32[]{:S(2)}, u32[]{:S(2)}) collective-permute-start(bf16[2048,256]{1,0:T(8,128)(2,1)} %fusion.47), channel_id=1, source_target_pairs={{0,2},{2,0},{4,6},{6,4},{8,10},{10,8},{12,14},{14,12},{1,3},{3,1},... | collective-permute-start | bytes 3145736 | tf_op jit(solution)/shard_map/ppermute | solution.py:365
  1126.8 107.8 %collective-permute-start.13 = (bf16[512,1024]{1,0:T(8,128)(2,1)}, bf16[512,1024]{1,0:T(8,128)(2,1)}, u32[]{:S(2)}, u32[]{:S(2)}) collective-permute-start(bf16[512,1024]{1,0:T(8,128)(2,1)} %fusion.53), channel_id=1, source_target_pairs={{0,2},{2,0},{4,6},{6,4},{8,10},{10,8},{12,14},{14,12},{1,3},{3,1},... | collective-permute-start | bytes 3145736 | tf_op jit(solution)/shard_map/ppermute | solution.py:365
  1154.9 41.6 %collective-permute-start.48 = (bf16[128,1536]{0,1:T(8,128)(2,1)}, bf16[128,1536]{0,1:T(8,128)(2,1)S(1)}, u32[]{:S(2)}, u32[]{:S(2)}) collective-permute-start(bf16[128,1536]{0,1:T(8,128)(2,1)} %bitcast.767), channel_id=1, source_target_pairs={{0,4},{2,6},{4,8},{6,10},{8,12},{10,14},{12,0},{14,2},{1,5},{3,7},... | collective-permute-start | bytes 1179656 | tf_op jit(solution)/shard_map/ppermute | solution.py:371
  1196.6 41.8 %collective-permute-start.23 = (bf16[128,1024]{1,0:T(8,128)(2,1)S(1)}, bf16[128,1024]{1,0:T(8,128)(2,1)S(1)}, u32[]{:S(2)}, u32[]{:S(2)}) collective-permute-start(bf16[128,1024]{1,0:T(8,128)(2,1)S(1)} %get-tuple-element.221), channel_id=1, source_target_pairs={{0,4},{2,6},{4,8},{6,10},{8,12},{10,14},{12,0},{14,2},{1,5},{3,7},... | collective-permute-start | bytes 786440 | tf_op jit(solution)/shard_map/ppermute | solution.py:371
  1238.3 40.6 %collective-permute-start.42 = (bf16[512,256]{1,0:T(8,128)(2,1)S(1)}, bf16[512,256]{1,0:T(8,128)(2,1)S(1)}, u32[]{:S(2)}, u32[]{:S(2)}) collective-permute-start(bf16[512,256]{1,0:T(8,128)(2,1)S(1)} %get-tuple-element.215), channel_id=1, source_target_pairs={{0,8},{2,10},{4,12},{6,14},{8,0},{10,2},{12,4},{14,6},{1,9},{3,11}... | collective-permute-start | bytes 786440 | tf_op jit(solution)/shard_map/ppermute | solution.py:371
  1238.4 40.5 %collective-permute-start.32 = (bf16[512,256]{1,0:T(8,128)(2,1)S(1)}, bf16[512,256]{1,0:T(8,128)(2,1)S(1)}, u32[]{:S(2)}, u32[]{:S(2)}) collective-permute-start(bf16[512,256]{1,0:T(8,128)(2,1)S(1)} %get-tuple-element.210), channel_id=1, source_target_pairs={{0,4},{2,6},{4,8},{6,10},{8,12},{10,14},{12,0},{14,2},{1,5},{3,7},... | collective-permute-start | bytes 786440 | tf_op jit(solution)/shard_map/ppermute | solution.py:371
  (256 other events, 3575.3 us)

commit v2 on v1

--- a/solution.py
+++ b/solution.py
@@ -380,61 +380,259 @@
     return value
 
 
-def reduce_gradient(left, right, halve):
-    own_z, own_x, own_seq, own_replica = place()
-    depth = depth_of()
-    rows = left.shape[1] // (2 * depth)
-    half = right.shape[1] // 2
-    size = half // 2 if halve else half
-
-    def product(part, replica, seq):
-        first = replica * half + (seq * size if halve else 0)
-        return matmul_left_t(part, lax.dynamic_slice_in_dim(right, first, size, 1))
-
-    def side(value, x, axis):
-        lead = value.shape[:axis]
-        split = value.reshape(lead + (depth, 2, rows) + value.shape[axis + 1 :])
-        picked = lax.dynamic_index_in_dim(split, x, axis + 1, False)
-        return picked.reshape(lead + (depth * rows,) + value.shape[axis + 1 :])
-
-    arrived = []
-    if halve:
-        far = swap(product(left, 1 - own_replica, 1 - own_seq).astype(jnp.bfloat16), "replica")
-        arrived.append(swap(product(left, 1 - own_replica, own_seq).astype(jnp.bfloat16), "replica"))
-        far = product(left, own_replica, 1 - own_seq) + far.astype(jnp.float32)
-        arrived.append(swap(far.astype(jnp.bfloat16), "seq"))
+def add_slabs(count, target, *sources):
+    def body(at, carry):
+        total = sources[0](at)[...].astype(jnp.float32)
+        for source in sources[1:]:
+            total = total + source(at)[...].astype(jnp.float32)
+        target(at)[...] = total.astype(jnp.bfloat16)
+        return carry
+
+    lax.fori_loop(0, count, body, 0)
+
+
+class Reduce:
+    def __init__(self, source, target, low, left, cut, rows, width, buffers, sends, recvs, local):
+        self.source, self.target, self.low, self.left, self.cut = (source, target, low, left, cut)
+        self.piece, self.width = (rows // (2 * cut), width)
+        self.buffers, self.sends, self.recvs, self.local = (buffers, sends, recvs, local)
+        self.z, self.x, self.seq, self.replica = place()
+        self.deep, self.across, self.beside, self.twin = neighbours()
+        self.depth, self.span = (depth_of(), lax.axis_size("seq"))
+        self.started, self.slots = ([], 0)
+        self.stages = [
+            self.exchange_twin,
+            self.exchange_seq,
+            self.exchange_across,
+            self.exchange_deep,
+            self.settle,
+            self.hand_over,
+            self.close,
+        ]
+
+    def row(self, dy, dc):
+        part = (self.replica + dc) % 2
+        if self.cut == 2:
+            part = part + 2 * ((self.seq + dy) % 2)
+        return pl.ds(pl.multiple_of(self.low + part * self.piece, self.piece), self.piece)
+
+    def block(self, dy, dc):
+        return self.source.at[:, :, self.row(dy, dc), pl.ds(self.left, self.width)]
+
+    def send(self, source, target, slot, peer):
+        copy = pltpu.make_async_remote_copy(
+            src_ref=source,
+            dst_ref=target,
+            send_sem=self.sends.at[slot],
+            recv_sem=self.recvs.at[slot],
+            device_id=peer,
+            device_id_type=MESH,
+        )
+        copy.start()
+        self.started.append(copy)
+
+    def wait(self, target, slot):
+        pltpu.make_async_remote_copy(
+            src_ref=target,
+            dst_ref=target,
+            send_sem=self.sends.at[slot],
+            recv_sem=self.recvs.at[slot],
+            device_id=self.twin,
+            device_id_type=MESH,
+        ).wait_recv()
+
+    def exchange_twin(self):
+        own, came = (self.buffers["own"], self.buffers["came"])
+        self.loads = []
+        for dy in reversed(range(self.cut)):
+            self.send(self.block(dy, 1), came.at[dy], dy, self.twin)
+            load = pltpu.make_async_copy(self.block(dy, 0), own.at[dy], self.local.at[dy])
+            load.start()
+            self.loads.append(load)
+
+    def exchange_seq(self):
+        if self.cut == 2:
+            own, came, away = [self.buffers[name] for name in ("own", "came", "to_seq")]
+            self.loads[0].wait()
+            self.wait(came.at[1], 1)
+            spot = lambda ref: lambda at: ref.at[at // 2, at % 2]
+            add_slabs(2 * self.depth, spot(away), spot(own.at[1]), spot(came.at[1]))
+            self.send(away, self.buffers["from_seq"], 2, self.beside)
+
+    def parts(self, x):
+        names = [self.buffers["own"].at[0], self.buffers["came"].at[0]]
+        if self.cut == 2:
+            names.append(self.buffers["from_seq"])
+        return [lambda at, ref=ref: ref.at[at, x] for ref in names]
+
+    def exchange_across(self):
+        self.loads[-1].wait()
+        self.wait(self.buffers["came"].at[0], 0)
+        if self.cut == 2:
+            self.wait(self.buffers["from_seq"], 2)
+        away = self.buffers["to_x"]
+        add_slabs(self.depth, lambda at: away.at[at], *self.parts(1 - self.x))
+        self.send(away, self.buffers["from_x"], 3, self.across)
+
+    def exchange_deep(self):
+        mine, came, far = [self.buffers[name] for name in ("mine", "from_x", "from_z")]
+        self.wait(came, 3)
+        add_slabs(self.depth, lambda at: mine.at[at], lambda at: came.at[at], *self.parts(self.x))
+        for steps, peer in enumerate(self.deep, 1):
+            spot = mine.at[(self.z + steps) % self.depth]
+            self.send(spot, far.at[steps - 1], 3 + steps, peer)
+
+    def settle(self):
+        mine, far = (self.buffers["mine"], self.buffers["from_z"])
+        for steps in range(1, self.depth):
+            self.wait(far.at[steps - 1], 3 + steps)
+        sources = [lambda at: mine.at[self.z]]
+        sources += [lambda at, steps=steps: far.at[steps - 1] for steps in range(1, self.depth)]
+        done = self.buffers["done"]
+        self.last = 4 + self.depth
+        if self.cut == 2:
+            add_slabs(1, lambda at: done, *sources)
+            self.publish(done)
+            self.send(done, self.spot(0, 0), self.last, self.beside)
+        else:
+            shared = self.buffers["shared"]
+            add_slabs(1, lambda at: shared.at[self.seq], *sources)
+            for steps in range(1, self.span):
+                peer = {"seq": (self.seq + steps) % self.span}
+                spot = shared.at[self.seq]
+                self.send(spot, spot, self.last + 2 + steps, peer)
+
+    def spot(self, dy, dc):
+        return self.target.at[self.row(dy, dc), pl.ds(self.left, self.width)]
+
+    def publish(self, done):
+        self.store = pltpu.make_async_copy(done, self.spot(0, 0), self.local.at[2])
+        self.store.start()
+        self.send(done, self.spot(0, 0), self.last + 1, self.twin)
+
+    def hand_over(self):
+        if self.cut == 2:
+            self.wait(self.spot(1, 0), self.last)
+            self.send(self.spot(1, 0), self.spot(1, 0), self.last + 2, self.twin)
+        else:
+            shared = self.buffers["shared"]
+            for steps in range(1, self.span):
+                self.wait(shared.at[(self.seq + self.span - steps) % self.span], self.last + 2 + steps)
+            done = self.buffers["done"]
+            sources = [lambda at, turn=turn: shared.at[turn] for turn in range(self.span)]
+            add_slabs(1, lambda at: done, *sources)
+            self.publish(done)
+
+    def close(self):
+        self.wait(self.spot(0, 1), self.last + 1)
+        if self.cut == 2:
+            self.wait(self.spot(1, 1), self.last + 2)
+        self.store.wait()
+        for copy in self.started:
+            copy.wait_send()
+
+
+def reduce_shapes(cut, rows, width):
+    depth, span = (depth_of(), lax.axis_size("seq"))
+    piece = rows // (2 * cut)
+    shapes = {
+        "own": (cut, depth, 2, piece, width),
+        "came": (cut, depth, 2, piece, width),
+        "to_x": (depth, piece, width),
+        "from_x": (depth, piece, width),
+        "mine": (depth, piece, width),
+        "from_z": (depth - 1, piece, width),
+        "done": (piece, width),
+    }
+    if cut == 2:
+        shapes["to_seq"] = shapes["from_seq"] = (depth, 2, piece, width)
     else:
-        arrived.append(swap(product(left, 1 - own_replica, 0).astype(jnp.bfloat16), "replica"))
-
-    def near(x):
-        total = product(side(left, x, 1), own_replica, own_seq)
-        for member in arrived:
-            total = total + side(member, x, 0).astype(jnp.float32)
-        return total
-
-    away = swap(near((own_x + 1) % 2).astype(jnp.bfloat16), "group")
-    mine = (near(own_x) + away.astype(jnp.float32)).astype(jnp.bfloat16).reshape(depth, rows, size)
-    total = lax.dynamic_index_in_dim(mine, own_z, 0, False).astype(jnp.float32)
-    for steps in range(1, depth):
-        sent = lax.dynamic_index_in_dim(mine, (own_z + steps) % depth, 0, False)
-        total = total + along_depth(sent, steps).astype(jnp.float32)
-    owned = total.astype(jnp.bfloat16)
-    if halve:
-        other = swap(owned, "seq")
-        owned = jnp.where(
-            own_seq == 0, jnp.concatenate([owned, other], 1), jnp.concatenate([other, owned], 1)
+        shapes["shared"] = (span, piece, width)
+    return shapes
+
+
+def reduce_plan(grads, rows, width, halve):
+    plan = []
+    for source, grad in enumerate(grads):
+        for low in range(0, grad.shape[2], rows):
+            for left in range(0, grad.shape[3], width):
+                plan.append((source, low, left, 2 if halve and len(plan) % 2 == 0 else 1))
+    return plan
+
+
+def reduce_scratch(plan, rows, width):
+    depth, span = (depth_of(), lax.axis_size("seq"))
+    scratch = []
+    for cut in (1, 2):
+        count = sum(member[3] == cut for member in plan)
+        if count:
+            scratch += [
+                pltpu.VMEM((count,) + shape, jnp.bfloat16)
+                for shape in reduce_shapes(cut, rows, width).values()
+            ]
+    slots = 7 + depth + span
+    return scratch + [
+        pltpu.SemaphoreType.DMA((len(plan), slots)),
+        pltpu.SemaphoreType.DMA((len(plan), slots)),
+        pltpu.SemaphoreType.DMA((len(plan), 3)),
+    ]
+
+
+def reduce_ticks(plan, rows, width, sources, targets, scratch):
+    held, (sends, recvs, local) = (list(scratch[:-3]), scratch[-3:])
+    stacks = {}
+    for cut in (1, 2):
+        if any(member[3] == cut for member in plan):
+            stacks[cut] = {name: held.pop(0) for name in reduce_shapes(cut, rows, width)}
+    jobs, used = ([], {1: 0, 2: 0})
+    for number, (source, low, left, cut) in enumerate(plan):
+        buffers = {name: ref.at[used[cut]] for name, ref in stacks[cut].items()}
+        used[cut] += 1
+        sems = (sends.at[number], recvs.at[number], local.at[number])
+        jobs.append(
+            Reduce(sources[source], targets[source], low, left, cut, rows, width, buffers, *sems)
         )
-    else:
-        bit = 1
-        while bit < lax.axis_size("seq"):
-            owned = owned.astype(jnp.float32) + swap(owned, "seq", bit).astype(jnp.float32)
-            owned = owned.astype(jnp.bfloat16)
-            bit *= 2
-    other = swap(owned, "replica")
-    owned = jnp.where(
-        own_replica == 0, jnp.concatenate([owned, other], 1), jnp.concatenate([other, owned], 1)
-    )
-    return owned.astype(jnp.float32)
+    stages = len(jobs[0].stages)
+
+    def tick(turn):
+        for stage in range(stages):
+            if 0 <= turn - stage < len(jobs):
+                jobs[turn - stage].stages[stage]()
+
+    return [functools.partial(tick, turn) for turn in range(len(jobs) + stages - 1)]
+
+
+def reduce_greet():
+    deep, across, _, twin = neighbours()
+    span = lax.axis_size("seq")
+    seq = lax.axis_index("seq")
+    greet(deep + [across, twin] + [{"seq": (seq + steps) % span} for steps in range(1, span)])
+
+
+def reduce_kernel(plan, rows, width, count, *refs):
+    sources, targets, scratch = (refs[:count], refs[count : 2 * count], refs[2 * count :])
+    reduce_greet()
+    for tick in reduce_ticks(plan, rows, width, sources, targets, scratch):
+        tick()
+
+
+def reduce_gradients(grads, halve, number):
+    groups = lax.axis_size("group")
+    width = min(grad.shape[1] for grad in grads)
+    rows = width // groups
+    grads = [grad.reshape(groups // 2, 2, grad.shape[0] // groups, grad.shape[1]) for grad in grads]
+    plan = reduce_plan(grads, rows, width, halve)
+    return pl.pallas_call(
+        functools.partial(reduce_kernel, plan, rows, width, len(grads)),
+        in_specs=[pl.BlockSpec(memory_space=pl.ANY)] * len(grads),
+        out_specs=[pl.BlockSpec(memory_space=pl.ANY)] * len(grads),
+        out_shape=[jax.ShapeDtypeStruct(grad.shape[2:], jnp.bfloat16) for grad in grads],
+        scratch_shapes=reduce_scratch(plan, rows, width),
+        compiler_params=pltpu.CompilerParams(
+            collective_id=number, has_side_effects=True, vmem_limit_bytes=48 << 20
+        ),
+        name="reduce_gradients",
+    )(*grads)
 
 
 def feed_forward(resid, gain, w_in, w_out):
@@ -445,12 +643,12 @@
     return (matmul(hidden, w_out), (normal, inverse, entry, hidden_pre, hidden))
 
 
-def feed_back(grad_branch, kept, gain, w_in, w_out, halve):
+def feed_back(grad_branch, kept, gain, w_in, w_out):
     normal, inverse, entry, hidden_pre, hidden = kept
     grad_low = grad_branch.astype(jnp.bfloat16)
-    grad_w_out = reduce_gradient(hidden, grad_low, halve)
+    grad_w_out = matmul_left_t(hidden, grad_low).astype(jnp.bfloat16)
     grad_hidden = (matmul_right_t(grad_low, w_out) * swish_grad(hidden_pre)).astype(jnp.bfloat16)
-    grad_w_in = reduce_gradient(entry, grad_hidden, halve)
+    grad_w_in = matmul_left_t(entry, grad_hidden).astype(jnp.bfloat16)
     grad_in, grad_gain = norm_backward(matmul_right_t(grad_hidden, w_in), normal, inverse, gain)
     return (grad_in, grad_gain, grad_w_in, grad_w_out)
 
@@ -478,7 +676,7 @@
     clips, rows, width = shape
     normal, inverse, entry, query, keys, values, mixed = kept
     grad_low = grad_branch.astype(jnp.bfloat16)
-    grad_attn_out = reduce_gradient(mixed, grad_low, False)
+    grad_attn_out = matmul_left_t(mixed, grad_low).astype(jnp.bfloat16)
     grad_mixed = matmul_right_t(grad_low, attn_out).astype(jnp.bfloat16).reshape(shape)
     grad_query, grad_keys, grad_values, grad_table = attend_back(
         query, keys, values, table, grad_mixed, rows
@@ -493,8 +691,7 @@
         return own.astype(jnp.bfloat16).reshape(clips * rows, width)
 
     parts = [grad_query.reshape(clips * rows, width), fold(grad_keys), fold(grad_values)]
-    grad_qkv = reduce_gradient(entry, jnp.concatenate(parts, 1), False)
-    grad_qkv = grad_qkv.reshape(-1, 3, width).transpose(1, 0, 2)
+    grad_qkv = [matmul_left_t(entry, part).astype(jnp.bfloat16) for part in parts]
     grad_entry = sum(matmul_right_t(part, qkv[at]) for at, part in enumerate(parts))
     grad_in, grad_gain = norm_backward(grad_entry, normal, inverse, gain)
     return (grad_in, grad_gain, grad_qkv, grad_attn_out, grad_table)
@@ -535,7 +732,7 @@
     normal, inverse, entry, joined, opened, padded, middle, mid_normal, mid_inverse, swished = kept
     taps = depthwise.astype(jnp.float32)
     grad_low = grad_branch.astype(jnp.bfloat16)
-    grad_conv_out = reduce_gradient(swished, grad_low, False)
+    grad_conv_out = matmul_left_t(swished, grad_low).astype(jnp.bfloat16)
     grad_middle = matmul_right_t(grad_low, conv_out) * swish_grad(middle)
     grad_summed, grad_gain_mid = norm_backward(grad_middle, mid_normal, mid_inverse, gain_mid)
     grad_summed = grad_summed.reshape(clips, rows, width)
@@ -561,7 +758,7 @@
         [grad_glu * opened, grad_glu * value_part * opened * (1.0 - opened)], 1
     )
     grad_joined = grad_joined.astype(jnp.bfloat16)
-    grad_conv_in = reduce_gradient(entry, grad_joined, False)
+    grad_conv_in = matmul_left_t(entry, grad_joined).astype(jnp.bfloat16)
     grad_in, grad_gain_in = norm_backward(
         matmul_right_t(grad_joined, conv_in), normal, inverse, gain_in
     )
@@ -632,7 +829,7 @@
     grad = cotangent.reshape(flat_rows, width).astype(jnp.float32)
     grad, grad_gain_final = norm_backward(grad, final_normal, final_inverse, gain_f[5])
     back_in, grad_gain_second, grad_in_second, grad_out_second = feed_back(
-        0.5 * grad, second_kept, gain_f[4], f_in[1], f_out[1], halve
+        0.5 * grad, second_kept, gain_f[4], f_in[1], f_out[1]
     )
     grad = grad + back_in
     back_in, grad_gain_conv, grad_gain_mid, grad_conv_in, grad_taps, grad_conv_out = conv_back(
@@ -644,9 +841,14 @@
     )
     grad = grad + back_in
     back_in, grad_gain_first, grad_in_first, grad_out_first = feed_back(
-        0.5 * grad, first_kept, gain_f[0], f_in[0], f_out[0], halve
+        0.5 * grad, first_kept, gain_f[0], f_in[0], f_out[0]
     )
     grad = grad + back_in
+    wide = jnp.float32
+    second = reduce_gradients([grad_out_second, grad_in_second], halve, 2)
+    middle = [grad_conv_out, grad_conv_in, grad_attn_out] + grad_qkv
+    middle = reduce_gradients(middle, halve, 3)
+    first = reduce_gradients([grad_out_first, grad_in_first], halve, 4)
     gain_grads = jnp.stack(
         [
             grad_gain_first,
@@ -673,12 +875,12 @@
     return (
         result.astype(jnp.bfloat16).reshape(shape),
         grad.astype(jnp.bfloat16).reshape(shape),
-        jnp.stack([grad_in_first, grad_in_second]),
-        jnp.stack([grad_out_first, grad_out_second]),
-        grad_qkv,
-        grad_attn_out,
-        grad_conv_in,
-        grad_conv_out,
+        jnp.stack([first[1], second[1]]).astype(wide),
+        jnp.stack([first[0], second[0]]).astype(wide),
+        jnp.stack(middle[3:]).astype(wide),
+        middle[2].astype(wide),
+        middle[1].astype(wide),
+        middle[0].astype(wide),
         owned[norms:],
         owned[:norms],
         loose[:table_size].reshape(rel_table.shape),

time: 1340 us -> 993 us (0.74)
  waiting for transfers between devices: 358 us -> 10 us
  Pallas kernels: 317 us -> 631 us
  local copies, waits for them, and re-layouts: 212 us -> 33.1 us
  starting transfers between devices: 122 us -> 39.4 us
  other arithmetic: 123 us -> 94.1 us
  matrix products: 199 us -> 174 us
    pallas_call x0 -> x3, Pallas kernels: none -> 313 us  [reduce_gradients(): pl.pallas_call(functools.partial(reduce_kernel, plan, rows, width, len(gr...]
    ppermute x45 -> x5, waiting for transfers between devices: 266 us -> 6.36 us  [swap(): lax.ppermute(value, axis, [(i, i ^ bit) for i in range(lax.axis_size(axis...]
    ppermute x24 -> x0, waiting for transfers between devices: 90.8 us -> none  [along_depth(): return lax.ppermute(value, 'group', pairs)]
    unnamed x417 -> x231, local copies, waits for them, and re-layouts: 95.5 us -> 17.1 us
    dynamic_slice x24 -> x0, local copies, waits for them, and re-layouts: 60 us -> none  [the longest x20 53 us: side(): picked = lax.dynamic_index_in_dim(split, x, axis + 1, False)]
    ppermute x24 -> x0, starting transfers between devices: 53.7 us -> none  [along_depth(): return lax.ppermute(value, 'group', pairs)]
    ppermute x45 -> x5, starting transfers between devices: 41.1 us -> 8.17 us  [swap(): lax.ppermute(value, axis, [(i, i ^ bit) for i in range(lax.axis_size(axis...]
    reshape x7 -> x0, local copies, waits for them, and re-layouts: 25.8 us -> none  [the longest x5 20.1 us: side(): split = value.reshape(lead + (depth, 2, rows) + value.shape[axis + 1:])]
  transfers between devices with their start and end apart: 79 -> 15, of which waited for: 25 -> 5; matrix products, arithmetic and copies ran while one was open for 23% -> 3% of each run, Pallas kernels for 5% -> 32%
where the time goes in v2:
time: 993 us; the launch traced here: 984 us
  Pallas kernels  631 us (64%)
  matrix products  174 us (18%)
  other arithmetic  94.1 us (9%)
  starting transfers between devices  39.4 us (4%)
  local copies, waits for them, and re-layouts  33.1 us (3%)
  waiting for transfers between devices  10 us (1%)
    pallas_call x3, Pallas kernels, reduce_gradients(): pl.pallas_call(functools.partial(reduce_kernel, plan, rows, width, len(gr...  313 us
    pallas_call x1, Pallas kernels, gather_weights(): pl.pallas_call(functools.partial(gather_kernel, plan, len(shards)), in_sp...  232 us
    dot_general x10, matrix products, matmul_right_t(): lax.dot_general(left, right, (((1,), (1,)), ((), ())), preferred_element_...  62.8 us
    dot_general x10, matrix products, matmul_left_t(): lax.dot_general(left, right, (((0,), (0,)), ((), ())), preferred_element_...  61.2 us
    pallas_call x1, Pallas kernels, attend_back(): pl.pallas_call(functools.partial(attend_back_kernel, limit), grid=grid, i...  61.1 us
    dot_general x10, matrix products, matmul(): return jnp.dot(left, right, preferred_element_type=jnp.float32)  49.7 us
    ppermute x10, starting transfers between devices, from_behind(): lax.ppermute(value, axis, [(source, source + steps) for source in range(i...  31.3 us
    pallas_call x1, Pallas kernels, attend(): pl.pallas_call(functools.partial(attend_kernel, limit), grid=grid, in_spe...  24.5 us
  transfers between devices with their start and end apart: 15, of which 5 were waited for; matrix products, arithmetic and copies ran while one was open for 3% of the time, Pallas kernels for 32%

profile of v2, /device:TPU:0, one launch (start us, length us, event | category | flops | bytes accessed | tf_op | source)
XLA Modules:
  0.0 983.7 jit_solution(13130991727420319311)
XLA Ops:
  9.7 231.9 %gather_weights.1 = (bf16[1,384,128]{2,1,0:T(8,128)(2,1)S(1)}, bf16[1,1024,4096]{2,1,0:T(8,128)(2,1)S(1)}, bf16[1,4096,1024]{2,1,0:T(8,128)(2,1)}, bf16[3,1024,1...) custom-call(bf16[1,48,128]{2,1,0:T(8,128)(2,1)S(1)} %fusion.183.refs, ...), custom_call_target="tpu_custom_call" | custom-call | tf_op jit(solution)/shard_map/gather_weights/pallas_call | solution.py:341
  242.4 7.8 fusion.14
  251.7 11.0 %fusion.207 = (f32[512]{0:T(512)S(1)}, f32[512,1024]{1,0:T(8,128)S(1)}, f32[]{:T(128)}) fusion(bf16[1,512,1024]{2,1,0:T(8,128)(2,1)S(1)} %copy-done.22, bf16[1,4096,1024]{2,1,0:T(8,128)(2,1)S(1)} %copy-done.103, f32[512,4096]{1,0:T(8,128)} %fusion.14), kind=kOutput, calls=%fused_computation.343 | convolution fusion | flops 4308598272 | bytes 19924996 | tf_op jit(solution)/shard_map/dot_general | solution.py:53
  277.0 5.8 collective-permute-start
  289.3 24.5 %attend.1 = bf16[1,512,1024]{2,1,0:T(8,128)(2,1)} custom-call(s32[1]{0:T(128)} %bitcast.11.first_ref, bf16[1,512,1024]{2,1,0:T(8,128)(2,1)} %fusion.141.q_ref, bf16[1,640,1024]{2,1,0:T(8,128)(2,1)} %get-tuple-element.220.k_ref, bf16[1,640,1024]{2,1,0:T(8,128)(2,1)} %get-tuple-element.219.v_ref, bf16[256,128]{1,0:T(8,128)(2,1)} %copy.24.t_ref), custom_call_target="tpu_custom_call" | custom-call | tf_op jit(solution)/shard_map/attend/pallas_call | solution.py:153
  328.7 10.0 %fusion.205 = (f32[512]{0:T(512)S(1)}, f32[1,512,1024]{2,1,0:T(8,128)S(1)}) fusion(f32[1,542,1024]{2,1,0:T(8,128)S(1)} %maximum_convert_fusion.2, f32[1024]{0:T(1024)S(1)} %bitcast.544, f32[1024]{0:T(1024)S(1)} %bitcast.546, f32[1024]{0:T(1024)S(1)} %bitcast.548, f32[1024]{0:T(1024)S(1)} %bitcast.550, f32[1024]{0:T(1024)S(1)} %bitcast.552, ...), kind=kLoop, calls=%fused_computation.341 | loop fusion | flops 32505344 | bytes 67237888 | tf_op jit(solution)/shard_map/reduce_sum | solution.py:35
  344.1 7.0 fusion.6
  351.1 10.3 %fusion.203 = (f32[512]{0:T(512)S(1)}, f32[512,1024]{1,0:T(8,128)S(1)}, f32[]{:T(128)}) fusion(f32[512,1024]{1,0:T(8,128)S(1)} %get-tuple-element.136, bf16[1,4096,1024]{2,1,0:T(8,128)(2,1)} %get-tuple-element.55, f32[512,4096]{1,0:T(8,128)} %fusion.6), kind=kOutput, calls=%fused_computation.339 | convolution fusion | flops 4308073984 | bytes 20973572 | tf_op jit(solution)/shard_map/dot_general | solution.py:53
  364.5 12.1 %multiply_convert_fusion.1 = bf16[512,4096]{1,0:T(8,128)(2,1)} fusion(bf16[1,4096,1024]{2,1,0:T(8,128)(2,1)} %get-tuple-element.55, f32[512,4096]{1,0:T(8,128)} %fusion.6, f32[512,1024]{1,0:T(8,128)S(1)} %get-tuple-element.134, bf16[1,512,1024]{2,1,0:T(8,128)(2,1)S(1)} %copy-done.36, f32[512]{0:T(512)S(1)} %get-tuple-element.226, ...), kind=kOutput, calls=%fused_computation.17 | convolution fusion | flops 4319084544 | bytes 24129536 | tf_op jit(solution)/shard_map/dot_general | solution.py:63
  376.5 12.2 %convolution_convert_fusion.1 = bf16[4096,1024]{1,0:T(8,128)(2,1)} fusion(f32[512,1024]{1,0:T(8,128)S(1)} %get-tuple-element.134, bf16[1,512,1024]{2,1,0:T(8,128)(2,1)S(1)} %copy-done.36, f32[512]{0:T(512)S(1)} %get-tuple-element.226, f32[512]{0:T(512)S(1)} %get-tuple-element.227, f32[1024]{0:T(1024)S(1)} %bitcast.516, f32[512]{0:T(512)S(1)} %add_rsqrt_fusion, ...), kind=kOutput, calls=%fused_computation.21 | convolution fusion | flops 4314890240 | bytes 19935232 | tf_op jit(solution)/shard_map/dot_general | solution.py:57
  388.7 9.3 multiply_reduce_fusion.5
  407.9 7.2 convolution_convert_fusion
  415.1 7.9 fusion.87
  426.9 9.1 multiply_bitcast_fusion.29
  436.0 11.1 %multiply_bitcast_fusion.30 = (f32[1,512,1024]{2,1,0:T(8,128)S(1)}, f32[1,512,1024]{2,1,0:T(8,128)S(1)}, f32[1,512,1024]{2,1,0:T(8,128)}, f32[1,512,1024]{2,1,0:...) fusion(f32[512,1024]{1,0:T(8,128)S(1)} %get-tuple-element.132, ...), kind=kLoop, calls=%fused_computation.205 | loop fusion | flops 9437184 | bytes 39919616 | tf_op jit(solution)/shard_map/mul | solution.py:745
  447.1 21.6 %pad_add_fusion = f32[1,542,1024]{2,1,0:T(8,128)S(1)} fusion(f32[1,512,1024]{2,1,0:T(8,128)S(1)} %get-tuple-element.152, f32[1,512,1024]{2,1,0:T(8,128)} %get-tuple-element.153, f32[1,512,1024]{2,1,0:T(8,128)} %get-tuple-element.154, f32[1,512,1024]{2,1,0:T(8,128)} %get-tuple-element.155, f32[1,512,1024]{2,1,0:T(8,128)} %get-tuple-element.156, ...), kind=kLoop, calls=%fused_computation.49 | loop fusion | flops 16650240 | bytes 67231744 | tf_op jit(solution)/shard_map/add | solution.py:744
  471.7 114.1 %reduce_gradients.4 = (bf16[512,1024]{1,0:T(8,128)(2,1)S(1)}, bf16[128,4096]{1,0:T(8,128)(2,1)S(1)}) custom-call(bf16[4,2,512,1024]{3,2,1,0:T(8,128)(2,1)} %bitcast.499, bf16[4,2,128,4096]{3,2,1,0:T(8,128)(2,1)} %bitcast.500), custom_call_target="tpu_custom_call" | custom-call | tf_op jit(solution)/shard_map/reduce_gradients/pallas_call | solution.py:625
  604.9 61.1 %attend_back.1 = (bf16[1,512,1024]{2,1,0:T(8,128)(2,1)}, bf16[1,640,1024]{2,1,0:T(8,128)(2,1)}, bf16[1,640,1024]{2,1,0:T(8,128)(2,1)}, f32[256,128]{1,0:T(8,128)}) custom-call(s32[1]{0:T(128)} %bitcast.11.first_ref, bf16[1,512,1024]{2,1,0:T(8,128)(2,1)} %fusion.141.q_ref, bf16[1,640,1024]{2,1,0:T(8,128)(2,1)} %get-tuple-element.220.k_ref, ...), custom_call_target="tpu_custom_call" | custom-call | tf_op jit(solution)/shard_map/attend_back/pallas_call | solution.py:163
  707.0 12.7 %multiply_convert_fusion = bf16[512,4096]{1,0:T(8,128)(2,1)} fusion(bf16[1,4096,1024]{2,1,0:T(8,128)(2,1)} %get-tuple-element.49, f32[512,4096]{1,0:T(8,128)} %fusion.14, f32[512,1024]{1,0:T(8,128)S(1)} %multiply_add_fusion), kind=kOutput, calls=%fused_computation.16 | convolution fusion | flops 4314890240 | bytes 23068672 | tf_op jit(solution)/shard_map/dot_general | solution.py:63
  719.7 11.0 %convolution_convert_fusion.3 = bf16[4096,1024]{1,0:T(8,128)(2,1)} fusion(f32[512,1024]{1,0:T(8,128)S(1)} %multiply_add_fusion, f32[512,4096]{1,0:T(8,128)} %fusion.14), kind=kOutput, calls=%fused_computation.23 | convolution fusion | flops 4310695936 | bytes 18874368 | tf_op jit(solution)/shard_map/dot_general | solution.py:57
  730.7 8.6 fusion.45
  739.7 9.5 convolution_convert_fusion.2
  750.0 105.8 %reduce_gradients.3 = (bf16[512,1024]{1,0:T(8,128)(2,1)S(1)}, bf16[128,4096]{1,0:T(8,128)(2,1)S(1)}) custom-call(bf16[4,2,512,1024]{3,2,1,0:T(8,128)(2,1)} %bitcast.501, bf16[4,2,128,4096]{3,2,1,0:T(8,128)(2,1)} %bitcast.502), custom_call_target="tpu_custom_call" | custom-call | tf_op jit(solution)/shard_map/reduce_gradients/pallas_call | solution.py:625
  883.3 93.2 %reduce_gradients.5 = (bf16[128,1024]{1,0:T(8,128)(2,1)S(1)}, bf16[128,2048]{1,0:T(8,128)(2,1)S(1)}, bf16[128,1024]{1,0:T(8,128)(2,1)S(1)}, bf16[128,1024]{1,0:T...) custom-call(bf16[4,2,128,1024]{3,2,1,0:T(8,128)(2,1)S(1)} %bitcast.483, ...), custom_call_target="tpu_custom_call" | custom-call | tf_op jit(solution)/shard_map/reduce_gradients/pallas_call | solution.py:625
  (369 shorter events, 166.5 us)
Async XLA Ops:
  2.3 240.1 %copy-start.47 = (f32[512]{0:T(512)}, f32[512]{0:T(512)S(1)}, u32[]{:S(2)}) copy-start(f32[512]{0:T(512)S(1)} %broadcast_multiply_fusion.17) | copy-start | bytes 6148
  3.9 238.4 %copy-start.95 = (f32[512]{0:T(512)}, f32[512]{0:T(512)S(1)}, u32[]{:S(2)}) copy-start(f32[512]{0:T(512)S(1)} %add_rsqrt_fusion.5) | copy-start | bytes 6148
  9.7 232.7 %copy-start.22 = (bf16[1,512,1024]{2,1,0:T(8,128)(2,1)S(1)}, bf16[1,512,1024]{2,1,0:T(8,128)(2,1)}, u32[]{:S(2)}) copy-start(bf16[1,512,1024]{2,1,0:T(8,128)(2,1)} %param.13) | copy-start | bytes 3145732
  241.6 41.2 %copy-start.10 = (bf16[3,1024,1024]{2,1,0:T(8,128)(2,1)}, bf16[3,1024,1024]{2,1,0:T(8,128)(2,1)S(1)}, u32[]{:S(2)}) copy-start(bf16[3,1024,1024]{2,1,0:T(8,128)(2,1)S(1)} %get-tuple-element.50) | copy-start | bytes 18874372
  241.6 72.2 %copy-start.14 = (bf16[1,1024,1024]{2,1,0:T(8,128)(2,1)}, bf16[1,1024,1024]{2,1,0:T(8,128)(2,1)S(1)}, u32[]{:S(2)}) copy-start(bf16[1,1024,1024]{2,1,0:T(8,128)(2,1)S(1)} %get-tuple-element.51) | copy-start | bytes 6291460
  242.3 20.7 %copy-start.43 = (f32[1,8,128]{2,0,1:T(1,128)}, f32[1,8,128]{2,0,1:T(1,128)S(1)}, u32[]{:S(2)}) copy-start(f32[1,8,128]{2,0,1:T(1,128)S(1)} %get-tuple-element.217) | copy-start | bytes 12292
  265.8 20.2 %collective-permute-start.3 = (bf16[1,8,1024]{2,1,0:T(8,128)(2,1)}, bf16[1,8,1024]{2,1,0:T(8,128)(2,1)}, u32[]{:S(2)}, u32[]{:S(2)}) collective-permute-start(bf16[1,8,1024]{2,1,0:T(8,128)(2,1)} %slice.532), channel_id=1, source_target_pairs={{16,0},{17,1},{18,2},{19,3},{20,4},{21,5},{22,6},{23,7},{24,8},{25... | collective-permute-start | bytes 49160 | tf_op jit(solution)/shard_map/ppermute | solution.py:31
  267.8 18.2 %collective-permute-start.2 = (bf16[1,64,1024]{2,1,0:T(8,128)(2,1)}, bf16[1,64,1024]{2,1,0:T(8,128)(2,1)S(1)}, u32[]{:S(2)}, u32[]{:S(2)}) collective-permute-start(bf16[1,64,1024]{2,1,0:T(8,128)(2,1)} %slice.531), channel_id=1, source_target_pairs={{0,16},{1,17},{2,18},{3,19},{4,20},{5,21},{6,22},{7,23},{8,24},{9,... | collective-permute-start | bytes 393224 | tf_op jit(solution)/shard_map/ppermute | solution.py:31
  275.1 10.9 %collective-permute-start.1 = (bf16[1,8,1024]{2,1,0:T(8,128)(2,1)}, bf16[1,8,1024]{2,1,0:T(8,128)(2,1)}, u32[]{:S(2)}, u32[]{:S(2)}) collective-permute-start(bf16[1,8,1024]{2,1,0:T(8,128)(2,1)} %slice.530), channel_id=1, source_target_pairs={{16,0},{17,1},{18,2},{19,3},{20,4},{21,5},{22,6},{23,7},{24,8},{25... | collective-permute-start | bytes 49160 | tf_op jit(solution)/shard_map/ppermute | solution.py:31
  277.0 9.0 collective-permute-start
  323.1 5.2 collective-permute-start.4
  338.6 61.9 %copy-start.20 = (f32[1,512,1024]{2,1,0:T(8,128)}, f32[1,512,1024]{2,1,0:T(8,128)S(1)}, u32[]{:S(2)}) copy-start(f32[1,512,1024]{2,1,0:T(8,128)S(1)} %get-tuple-element.138) | copy-start | bytes 6291460
  468.7 118.1 %collective-permute-start.5 = (bf16[1,30,1024]{2,1,0:T(8,128)(2,1)S(1)}, bf16[1,30,1024]{2,1,0:T(8,128)(2,1)S(1)}, u32[]{:S(2)}, u32[]{:S(2)}) collective-permute-start(bf16[1,30,1024]{2,1,0:T(8,128)(2,1)S(1)} %slice.745), channel_id=1, source_target_pairs={{16,0},{17,1},{18,2},{19,3},{20,4},{21,5},{22,6},{23,7},{24,8},{25... | collective-permute-start | bytes 184328 | tf_op jit(solution)/shard_map/ppermute | solution.py:31
  679.3 17.8 %collective-permute-start.7 = (bf16[1,8,1024]{2,1,0:T(8,128)(2,1)S(1)}, bf16[1,8,1024]{2,1,0:T(8,128)(2,1)}, u32[]{:S(2)}, u32[]{:S(2)}) collective-permute-start(bf16[1,8,1024]{2,1,0:T(8,128)(2,1)S(1)} %slice.513), channel_id=1, source_target_pairs={{0,16},{1,17},{2,18},{3,19},{4,20},{5,21},{6,22},{7,23},{8,24},{9,... | collective-permute-start | bytes 49160 | tf_op jit(solution)/shard_map/ppermute | solution.py:31
  683.8 13.3 %collective-permute-start.6 = (bf16[1,64,1024]{2,1,0:T(8,128)(2,1)S(1)}, bf16[1,64,1024]{2,1,0:T(8,128)(2,1)}, u32[]{:S(2)}, u32[]{:S(2)}) collective-permute-start(bf16[1,64,1024]{2,1,0:T(8,128)(2,1)S(1)} %slice.512), channel_id=1, source_target_pairs={{16,0},{17,1},{18,2},{19,3},{20,4},{21,5},{22,6},{23,7},{24,8},{25... | collective-permute-start | bytes 393224 | tf_op jit(solution)/shard_map/ppermute | solution.py:31
  690.3 10.1 %collective-permute-start.9 = (bf16[1,8,1024]{2,1,0:T(8,128)(2,1)S(1)}, bf16[1,8,1024]{2,1,0:T(8,128)(2,1)S(1)}, u32[]{:S(2)}, u32[]{:S(2)}) collective-permute-start(bf16[1,8,1024]{2,1,0:T(8,128)(2,1)S(1)} %slice.516), channel_id=1, source_target_pairs={{0,16},{1,17},{2,18},{3,19},{4,20},{5,21},{6,22},{7,23},{8,24},{9,... | collective-permute-start | bytes 49160 | tf_op jit(solution)/shard_map/ppermute | solution.py:31
  695.8 6.9 collective-permute-start.8
  707.0 23.7 %slice-start = ((s8[8388608]{0:T(1024)(128)(4,1)}), s8[4194304]{0:T(1024)(128)(4,1)S(1)}, s32[]{:S(2)}) async-start(s8[8388608]{0:T(1024)(128)(4,1)} %bitcast.497), calls=%async_computation | async-start | bytes 8388608
  749.9 108.3 %collective-permute-start.10 = (f32[42,1024]{1,0:T(8,128)S(1)}, f32[42,1024]{1,0:T(8,128)S(1)}, u32[]{:S(2)}, u32[]{:S(2)}) collective-permute-start(f32[42,1024]{1,0:T(8,128)S(1)} %concatenate.38), channel_id=1, source_target_pairs={{0,1},{1,0},{2,3},{3,2},{4,5},{5,4},{6,7},{7,6},{8,9},{9,8},{10,11... | collective-permute-start | bytes 516104 | tf_op jit(solution)/shard_map/ppermute | solution.py:365
  749.9 105.8 %copy-start.4 = (bf16[128,4096]{1,0:T(8,128)(2,1)S(1)}, bf16[128,4096]{1,0:T(8,128)(2,1)}, u32[]{:S(2)}) copy-start(bf16[128,4096]{1,0:T(8,128)(2,1)} %copy-done.3) | copy-start | bytes 3145732
  858.2 7.2 collective-permute-start.11
  865.5 6.4 collective-permute-start.12
  872.0 7.1 collective-permute-start.13
  879.1 101.5 %collective-permute-start.14 = (f32[42,1024]{1,0:T(8,128)S(1)}, f32[42,1024]{1,0:T(8,128)S(1)}, u32[]{:S(2)}, u32[]{:S(2)}) collective-permute-start(f32[42,1024]{1,0:T(8,128)S(1)} %add.494), channel_id=1, source_target_pairs={{0,8},{2,10},{4,12},{6,14},{8,0},{10,2},{12,4},{14,6},{1,9},{3,11}... | collective-permute-start | bytes 516104 | tf_op jit(solution)/shard_map/ppermute | solution.py:365
  (106 other events, 767.4 us)

commit v3 on v1

--- a/solution.py
+++ b/solution.py
@@ -380,61 +380,720 @@
     return value
 
 
-def reduce_gradient(left, right, halve):
-    own_z, own_x, own_seq, own_replica = place()
-    depth = depth_of()
-    rows = left.shape[1] // (2 * depth)
-    half = right.shape[1] // 2
-    size = half // 2 if halve else half
-
-    def product(part, replica, seq):
-        first = replica * half + (seq * size if halve else 0)
-        return matmul_left_t(part, lax.dynamic_slice_in_dim(right, first, size, 1))
-
-    def side(value, x, axis):
-        lead = value.shape[:axis]
-        split = value.reshape(lead + (depth, 2, rows) + value.shape[axis + 1 :])
-        picked = lax.dynamic_index_in_dim(split, x, axis + 1, False)
-        return picked.reshape(lead + (depth * rows,) + value.shape[axis + 1 :])
-
-    arrived = []
-    if halve:
-        far = swap(product(left, 1 - own_replica, 1 - own_seq).astype(jnp.bfloat16), "replica")
-        arrived.append(swap(product(left, 1 - own_replica, own_seq).astype(jnp.bfloat16), "replica"))
-        far = product(left, own_replica, 1 - own_seq) + far.astype(jnp.float32)
-        arrived.append(swap(far.astype(jnp.bfloat16), "seq"))
-    else:
-        arrived.append(swap(product(left, 1 - own_replica, 0).astype(jnp.bfloat16), "replica"))
-
-    def near(x):
-        total = product(side(left, x, 1), own_replica, own_seq)
-        for member in arrived:
-            total = total + side(member, x, 0).astype(jnp.float32)
-        return total
-
-    away = swap(near((own_x + 1) % 2).astype(jnp.bfloat16), "group")
-    mine = (near(own_x) + away.astype(jnp.float32)).astype(jnp.bfloat16).reshape(depth, rows, size)
-    total = lax.dynamic_index_in_dim(mine, own_z, 0, False).astype(jnp.float32)
-    for steps in range(1, depth):
-        sent = lax.dynamic_index_in_dim(mine, (own_z + steps) % depth, 0, False)
-        total = total + along_depth(sent, steps).astype(jnp.float32)
-    owned = total.astype(jnp.bfloat16)
-    if halve:
-        other = swap(owned, "seq")
-        owned = jnp.where(
-            own_seq == 0, jnp.concatenate([owned, other], 1), jnp.concatenate([other, owned], 1)
+def add_slabs(count, target, *sources):
+    def body(at, carry):
+        total = sources[0](at)[...].astype(jnp.float32)
+        for source in sources[1:]:
+            total = total + source(at)[...].astype(jnp.float32)
+        target(at)[...] = total.astype(jnp.bfloat16)
+        return carry
+
+    lax.fori_loop(0, count, body, 0)
+
+
+class Reduce:
+    def __init__(self, pool, number, source, target, low, left, cut):
+        self.pool, self.number, self.cut = (pool, number, cut)
+        self.source, self.target, self.low, self.left = (source, target, low, left)
+        self.depth, self.span = (depth_of(), lax.axis_size("seq"))
+        self.width = pool.width
+        self.piece = pool.rows // (2 * cut)
+        self.last = 4 + self.depth
+        self.started = []
+        self.stages = [
+            self.exchange_twin,
+            self.exchange_seq,
+            self.exchange_across,
+            self.exchange_deep,
+            self.settle,
+            self.hand_over,
+            self.close,
+        ]
+        self.done_stages = 0
+        self.ready = source is not None
+        self.turn = pool.cuts.setdefault(cut, [])
+        self.rank = len(self.turn)
+        self.turn.append(self)
+        self.own = pool.own.at[number % pool.ring]
+        self.came = pool.came.at[number % pool.ring]
+        self.from_x = pool.from_x.at[number % pool.ring, :, pl.ds(0, self.piece)]
+        self.from_z = pool.from_z.at[number, :, pl.ds(0, self.piece)]
+        self.finished = pool.finished.at[number % pool.ring, pl.ds(0, self.piece)]
+        if cut == 2:
+            self.from_seq = pool.from_seq.at[self.rank % pool.ring]
+        else:
+            self.shared = pool.shared.at[self.rank]
+
+    def locate(self):
+        self.z, self.x, self.seq, self.replica = place()
+        self.deep, self.across, self.beside, self.twin = neighbours()
+
+    def part(self, dy, dc):
+        part = (self.replica + dc) % 2
+        if self.cut == 2:
+            part = part + 2 * ((self.seq + dy) % 2)
+        return part
+
+    def row(self, dy, dc, low=0):
+        first = pl.multiple_of(low + self.part(dy, dc) * self.piece, self.piece)
+        return pl.ds(first, self.piece)
+
+    def half(self, dy):
+        return pl.ds(dy * self.piece, self.piece)
+
+    def remote(self, source, target, slot, peer):
+        return pltpu.make_async_remote_copy(
+            src_ref=source,
+            dst_ref=target,
+            send_sem=self.pool.sends.at[self.number, slot],
+            recv_sem=self.pool.recvs.at[self.number, slot],
+            device_id=peer,
+            device_id_type=MESH,
         )
-    else:
-        bit = 1
-        while bit < lax.axis_size("seq"):
-            owned = owned.astype(jnp.float32) + swap(owned, "seq", bit).astype(jnp.float32)
-            owned = owned.astype(jnp.bfloat16)
-            bit *= 2
-    other = swap(owned, "replica")
-    owned = jnp.where(
-        own_replica == 0, jnp.concatenate([owned, other], 1), jnp.concatenate([other, owned], 1)
-    )
-    return owned.astype(jnp.float32)
+
+    def send(self, ends, slot, peer):
+        make = lambda peer: self.remote(*ends(), slot, peer)
+        make(peer).start()
+        self.started.append(make)
+
+    def wait(self, target, slot):
+        self.remote(target, target, slot, self.twin).wait_recv()
+
+    def load(self, dy):
+        source = self.source.at[:, :, self.row(dy, 0, self.low), pl.ds(self.left, self.width)]
+        target = self.own.at[:, :, self.row(dy, 0)]
+        return pltpu.make_async_copy(source, target, self.pool.local.at[self.number, dy])
+
+    def credit(self, kind, behind, peer):
+        if behind >= self.pool.ring:
+            pl.semaphore_wait(self.pool.credits.at[kind], 1)
+
+    def release(self, kind, ahead, peer):
+        if ahead:
+            pl.semaphore_signal(
+                self.pool.credits.at[kind], inc=1, device_id=peer, device_id_type=MESH
+            )
+
+    def exchange_twin(self):
+        self.credit(0, self.number, self.twin)
+        for dy in reversed(range(self.cut)):
+            if self.source is None:
+                ends = lambda dy=dy: (
+                    self.own.at[:, :, self.row(dy, 1)],
+                    self.came.at[:, :, self.half(dy)],
+                )
+            else:
+                ends = lambda dy=dy: (
+                    self.source.at[:, :, self.row(dy, 1, self.low), pl.ds(self.left, self.width)],
+                    self.came.at[:, :, self.half(dy)],
+                )
+                self.load(dy).start()
+            self.send(ends, dy, self.twin)
+
+    def exchange_seq(self):
+        if self.cut == 2:
+            if self.source is not None:
+                self.load(1).wait()
+            self.wait(self.came.at[:, :, self.half(1)], 1)
+            own = lambda at: self.own.at[at // 2, at % 2, self.row(1, 0)]
+            came = lambda at: self.came.at[at // 2, at % 2, self.half(1)]
+            add_slabs(2 * self.depth, own, own, came)
+            self.credit(1, self.rank, self.beside)
+            self.send(lambda: (self.own.at[:, :, self.row(1, 0)], self.from_seq), 2, self.beside)
+
+    def spots(self, x):
+        sources = [
+            lambda at: self.own.at[at, x, self.row(0, 0)],
+            lambda at: self.came.at[at, x, self.half(0)],
+        ]
+        if self.cut == 2:
+            sources.append(lambda at: self.from_seq.at[at, x])
+        return sources
+
+    def exchange_across(self):
+        if self.source is not None:
+            self.load(0).wait()
+        self.wait(self.came.at[:, :, self.half(0)], 0)
+        if self.cut == 2:
+            self.wait(self.from_seq, 2)
+        sources = self.spots(1 - self.x)
+        add_slabs(self.depth, sources[0], *sources)
+        self.credit(2, self.number, self.across)
+        ends = lambda: (self.own.at[:, 1 - self.x, self.row(0, 0)], self.from_x)
+        self.send(ends, 3, self.across)
+
+    def exchange_deep(self):
+        self.wait(self.from_x, 3)
+        sources = self.spots(self.x)
+        add_slabs(self.depth, sources[0], lambda at: self.from_x.at[at], *sources)
+        for steps, peer in enumerate(self.deep, 1):
+            ends = lambda steps=steps: (
+                self.own.at[(self.z + steps) % self.depth, self.x, self.row(0, 0)],
+                self.from_z.at[steps - 1],
+            )
+            self.send(ends, 3 + steps, peer)
+        total = self.pool.total
+        self.release(0, self.number + self.pool.ring < total, self.twin)
+        self.release(2, self.number + self.pool.ring < total, self.across)
+        if self.cut == 2:
+            self.release(1, self.rank + self.pool.ring < self.pool.pairs, self.beside)
+
+    def settle(self):
+        for steps in range(1, self.depth):
+            self.wait(self.from_z.at[steps - 1], 3 + steps)
+        self.flush()
+        sources = [lambda at: self.own.at[self.z, self.x, self.row(0, 0)]]
+        sources += [lambda at, steps=steps: self.from_z.at[steps - 1] for steps in range(1, self.depth)]
+        if self.cut == 2:
+            add_slabs(1, lambda at: self.finished, *sources)
+            self.publish()
+            self.send(lambda: (self.finished, self.spot(0, 0)), self.last, self.beside)
+        else:
+            add_slabs(1, lambda at: self.shared.at[self.seq], *sources)
+            for steps in range(1, self.span):
+                peer = {"seq": (self.seq + steps) % self.span}
+                ends = lambda: (self.shared.at[self.seq], self.shared.at[self.seq])
+                self.send(ends, self.last + 2 + steps, peer)
+
+    def spot(self, dy, dc):
+        return self.target.at[self.row(dy, dc, self.low), pl.ds(self.left, self.width)]
+
+    def store(self):
+        return pltpu.make_async_copy(
+            self.finished, self.spot(0, 0), self.pool.local.at[self.number, 2]
+        )
+
+    def publish(self):
+        self.store().start()
+        self.send(lambda: (self.finished, self.spot(0, 0)), self.last + 1, self.twin)
+
+    def hand_over(self):
+        if self.cut == 2:
+            self.wait(self.spot(1, 0), self.last)
+            self.send(lambda: (self.spot(1, 0), self.spot(1, 0)), self.last + 2, self.twin)
+        else:
+            for steps in range(1, self.span):
+                turn = (self.seq + self.span - steps) % self.span
+                self.wait(self.shared.at[turn], self.last + 2 + steps)
+            sources = [lambda at, turn=turn: self.shared.at[turn] for turn in range(self.span)]
+            add_slabs(1, lambda at: self.finished, *sources)
+            self.publish()
+
+    def close(self):
+        self.wait(self.spot(0, 1), self.last + 1)
+        if self.cut == 2:
+            self.wait(self.spot(1, 1), self.last + 2)
+        self.store().wait()
+        self.flush()
+
+    def flush(self):
+        for make in self.started:
+            make(self.twin).wait_send()
+        self.started = []
+
+    def step(self):
+        self.locate()
+        self.stages[self.done_stages]()
+        self.done_stages += 1
+
+
+class Pool:
+    def __init__(self, rows, width, plan, refs):
+        self.ring = Pool.slots()
+        self.rows, self.width, self.plan = (rows, width, plan)
+        self.total = len(plan)
+        self.pairs = sum(cut == 2 for cut in plan)
+        names = list(Pool.shapes(rows, width, plan))
+        for name, ref in zip(names, refs):
+            setattr(self, name, ref)
+        self.sends, self.recvs, self.local, self.credits = refs[len(names) :]
+        self.cuts, self.jobs, self.next = ({}, [], 0)
+
+    @staticmethod
+    def slots():
+        return 6 if lax.axis_size("seq") == 2 else 4
+
+    @staticmethod
+    def shapes(rows, width, plan):
+        depth, span = (depth_of(), lax.axis_size("seq"))
+        ring = min(Pool.slots(), len(plan))
+        pairs = sum(cut == 2 for cut in plan)
+        shapes = {
+            "own": (ring, depth, 2, rows, width),
+            "came": (ring, depth, 2, rows // 2, width),
+            "from_x": (ring, depth, rows // 2, width),
+            "from_z": (len(plan), depth - 1, rows // 2, width),
+            "finished": (ring, rows // 2, width),
+        }
+        if pairs:
+            shapes["from_seq"] = (min(ring, pairs), depth, 2, rows // 4, width)
+        if pairs < len(plan):
+            shapes["shared"] = (len(plan) - pairs, span, rows // 2, width)
+        return shapes
+
+    @staticmethod
+    def scratch(rows, width, plan):
+        slots = 7 + depth_of() + lax.axis_size("seq")
+        shapes = Pool.shapes(rows, width, plan).values()
+        return [pltpu.VMEM(shape, jnp.bfloat16) for shape in shapes] + [
+            pltpu.SemaphoreType.DMA((len(plan), slots)),
+            pltpu.SemaphoreType.DMA((len(plan), slots)),
+            pltpu.SemaphoreType.DMA((len(plan), 3)),
+            pltpu.SemaphoreType.REGULAR((3,)),
+        ]
+
+    def add(self, target, low, left, source=None):
+        number = len(self.jobs)
+        while number >= self.ring and self.jobs[number - self.ring].done_stages < 5:
+            self.pump()
+        job = Reduce(self, number, source, target, low, left, self.plan[number])
+        self.jobs.append(job)
+        return job
+
+    def pump(self):
+        active = [job for job in self.jobs if job.ready and 0 < job.done_stages < 7]
+        fresh = [job for job in self.jobs if job.ready and job.done_stages == 0]
+        for job in fresh[:1]:
+            job.step()
+        for job in reversed(active):
+            job.step()
+
+    def drain(self):
+        while any(job.done_stages < 7 for job in self.jobs):
+            self.pump()
+
+
+def row_blocks(total, size, body):
+    def step(at, carry):
+        body(pl.ds(pl.multiple_of(at * size, size), size))
+        return carry
+
+    lax.fori_loop(0, total // size, step, 0)
+
+
+def norm_parts(values):
+    centered = values - jnp.mean(values, -1, keepdims=True)
+    inverse = lax.rsqrt(jnp.mean(centered * centered, -1, keepdims=True) + EPSILON)
+    return (centered * inverse, inverse)
+
+
+def norm_rows(source, gain, target):
+    def body(rows):
+        normal, _ = norm_parts(source[rows, :].astype(jnp.float32))
+        target[rows, :] = (normal * gain).astype(target.dtype)
+
+    row_blocks(source.shape[0], 64, body)
+
+
+def norm_back_rows(source, gain, grads, resid, sums, line):
+    sums[pl.ds(line, 1), :] = jnp.zeros_like(sums[pl.ds(line, 1), :])
+
+    def body(rows):
+        normal, inverse = norm_parts(source[rows, :].astype(jnp.float32))
+        grad = grads[rows, :]
+        grad_normal = grad * gain
+        resid[rows, :] += inverse * (
+            grad_normal
+            - jnp.mean(grad_normal, -1, keepdims=True)
+            - normal * jnp.mean(grad_normal * normal, -1, keepdims=True)
+        )
+        sums[pl.ds(line, 1), :] += jnp.sum(grad * normal, 0, keepdims=True)
+
+    row_blocks(source.shape[0], 64, body)
+
+
+def cast_rows(source, target, scale=1.0):
+    def body(rows):
+        target[rows, :] = (source[rows, :] * scale).astype(jnp.bfloat16)
+
+    row_blocks(source.shape[0], 64, body)
+
+
+def transposed_rows(left, right, target, size=256):
+    def body(cols):
+        target[:, cols] = nt(left[...], right[cols, :]).astype(target.dtype)
+
+    row_blocks(right.shape[0], size, body)
+
+
+def add_transposed(left, right, target, size=256):
+    def body(cols):
+        target[:, cols] += nt(left[...], right[cols, :])
+
+    row_blocks(right.shape[0], size, body)
+
+
+def gradient_into(job, left, right):
+    depth, _, rows, width = job.own.shape
+
+    def step(z, carry):
+        cols = pl.ds(pl.multiple_of(z * 2 * rows, 2 * rows), 2 * rows)
+        value = tn(left[:, cols], right[...]).astype(jnp.bfloat16)
+        job.own[z, 0] = value[:rows]
+        job.own[z, 1] = value[rows:]
+        return carry
+
+    lax.fori_loop(0, depth, step, 0)
+    job.ready = True
+
+
+class Stream:
+    def __init__(self, buffers, sems, copies):
+        self.buffers, self.sems, self.copies = (buffers, sems, copies)
+        self.issued = self.taken = 0
+        for _ in range(len(buffers) - 1):
+            self.issue()
+
+    def parts(self, number):
+        slot = number % len(self.buffers)
+        made = self.copies[number](self.buffers[slot])
+        return [
+            pltpu.make_async_copy(source, target, self.sems.at[slot, at])
+            for at, (source, target) in enumerate(made)
+        ]
+
+    def issue(self):
+        if self.issued < len(self.copies):
+            for copy in self.parts(self.issued):
+                copy.start()
+            self.issued += 1
+
+    def take(self):
+        for copy in self.parts(self.taken):
+            copy.wait()
+        self.taken += 1
+        self.issue()
+        return self.buffers[(self.taken - 1) % len(self.buffers)]
+
+
+def module_copies(w_in, w_out, groups):
+    chunks = w_out.shape[1]
+    rows = w_out.shape[2]
+    copies = []
+    for chunk in range(chunks):
+        copies.append(
+            lambda slot, chunk=chunk: [
+                (w_out.at[group, chunk], slot.at[pl.ds(group * rows, rows)])
+                for group in range(groups)
+            ]
+        )
+        copies.append(
+            lambda slot, chunk=chunk: [
+                (
+                    w_in.at[:, pl.ds((group * chunks + chunk) * rows, rows)],
+                    slot.at[:, pl.ds(group * rows, rows)],
+                )
+                for group in range(groups)
+            ]
+        )
+    return copies
+
+
+def saved_copies(saved, groups, rows):
+    chunks = saved.shape[1] // (groups * rows)
+    return [
+        lambda slot, chunk=chunk: [
+            (
+                saved.at[:, pl.ds((group * chunks + chunk) * rows, rows)],
+                slot.at[:, pl.ds(group * rows, rows)],
+            )
+            for group in range(groups)
+        ]
+        for chunk in range(chunks)
+    ]
+
+
+def module_back(pool, pump, weights, saved, buffers, chunks, outs):
+    entry, low, hidden, grad_hidden, total = buffers
+    grad_in, grad_out = outs
+    width = total.shape[1]
+    total[...] = jnp.zeros_like(total)
+    for chunk in range(chunks):
+        before = saved.take()
+        w_out = weights.take()
+
+        def body(cols):
+            value = before[:, cols].astype(jnp.float32)
+            logistic = jax.nn.sigmoid(value)
+            hidden[:, cols] = (value * logistic).astype(jnp.bfloat16)
+            slope = logistic * (1.0 + value * (1.0 - logistic))
+            grad = nt(low[...], w_out[cols, :]) * slope
+            grad_hidden[:, cols] = grad.astype(jnp.bfloat16)
+
+        row_blocks(width, 256, body)
+        job = pool.add(grad_out, chunk * pool.rows, 0)
+        gradient_into(job, hidden, low)
+        pump()
+        job = pool.add(grad_in, 0, chunk * width)
+        gradient_into(job, entry, grad_hidden)
+        pump()
+        add_transposed(grad_hidden, weights.take(), total)
+        pump()
+def late_back_kernel(settings, *refs):
+    plan, early, count, clips, rows, limit = settings
+    first_ref, table_ref, gains = refs[:3]
+    grad, x1, x0, u0, mixed, query, keys, values, a_out, qkv, w_in, w_out = refs[3:15]
+    refs = refs[15:]
+    sources, refs = (refs[:count], refs[count:])
+    grad_x, gain_sums, dt_ref, to_attn, to_q, to_k, to_v, to_out, to_in = refs[:9]
+    refs = refs[9:]
+    targets, refs = (refs[:count], refs[count:])
+    resid, total, resid_in, low, entry, mixed_grad, q_ref, dq_ref = refs[:8]
+    k_ref, v_ref, dk_ref, dv_ref, later, earlier, dk_sum, dv_sum, slots = refs[8:17]
+    local, slot_sems, saved_sems, halo_sems = refs[17:21]
+    width = total.shape[1]
+    groups = lax.axis_size("group")
+    part = width // groups
+    span = lax.axis_size("seq")
+    chunks = w_out.shape[1]
+    reduce_greet()
+    pool = Pool(part, width, plan, refs[21:])
+    loads = [
+        pltpu.make_async_copy(source, target, local.at[at])
+        for at, (source, target) in enumerate(
+            (
+                (grad, resid),
+                (mixed, entry),
+                (query, q_ref),
+                (keys, k_ref),
+                (values, v_ref),
+                (x1, resid_in),
+            )
+        )
+    ]
+    for load in loads:
+        load.start()
+    copies = [lambda slot: [(a_out, slot)]]
+    copies += [lambda slot, at=at: [(qkv.at[at], slot)] for at in range(3)]
+    copies += module_copies(w_in, w_out, groups)
+    weights = Stream([slots.at[at] for at in range(3)], slot_sems, copies)
+    waiting = list(early)
+
+    def feed():
+        number = len(pool.jobs)
+        free = number < pool.ring or pool.jobs[number - pool.ring].done_stages >= 5
+        if waiting and free and not any(job.done_stages == 0 for job in pool.jobs):
+            source, low_row, left = waiting.pop(0)
+            pool.add(targets[source], low_row, left, sources[source])
+
+    def pump():
+        feed()
+        pool.pump()
+
+    pump()
+    loads[0].wait()
+    cast_rows(resid, low)
+    loads[1].wait()
+    job = pool.add(to_attn, 0, 0)
+    gradient_into(job, entry, low)
+    pump()
+    transposed_rows(low, weights.take(), mixed_grad)
+    pump()
+    for load in loads[2:]:
+        load.wait()
+    table = table_ref[...]
+    zero = jnp.zeros((BLOCK, LANES), jnp.bfloat16)
+    across = lax.broadcasted_iota(jnp.int32, (BLOCK, BLOCK), 0)
+    across = across + lax.broadcasted_iota(jnp.int32, (BLOCK, BLOCK), 1)
+    flip = (across == BLOCK - 1).astype(jnp.float32).astype(jnp.bfloat16)
+    dt_ref[...] = jnp.zeros_like(dt_ref)
+    blocks = rows // BLOCK
+    for pair in range(width // LANES):
+        lanes = pl.ds(pair * LANES, LANES)
+        dk_sum[...] = jnp.zeros_like(dk_sum)
+        dv_sum[...] = jnp.zeros_like(dv_sum)
+
+        def attend_block(at, carry):
+            clip, block = (at // blocks, at % blocks)
+            here = pl.ds(pl.multiple_of(at * BLOCK, BLOCK), BLOCK)
+            near = pl.ds(pl.multiple_of(block * BLOCK, BLOCK), SPAN)
+            key = k_ref[clip, near, lanes]
+            value = v_ref[clip, near, lanes]
+            mask = block_mask(first_ref[0], block, limit)
+            grad_query = []
+            for head in range(2):
+                q = jnp.where(head_lanes(head), q_ref[here, lanes], zero)
+                g = jnp.where(head_lanes(head), mixed_grad[here, lanes], zero)
+                probs = block_probs(q, key, table, mask)
+                grad_probs = nt(g, value)
+                grad_raw = probs * (grad_probs - jnp.sum(probs * grad_probs, -1, keepdims=True))
+                grad_raw = grad_raw.astype(jnp.bfloat16)
+                turned = pltpu.roll(
+                    nn(flip, grad_raw), SPAN - BLOCK + 1, 1, stride=1, stride_axis=0
+                )
+                unskewed = nn(flip, turned.astype(jnp.bfloat16)).astype(jnp.bfloat16)
+                dv_sum[clip, near, :] += tn(probs.astype(jnp.bfloat16), g)
+                dk_sum[clip, near, :] += tn(grad_raw, q)
+                dt_ref[...] += tn(unskewed, q)
+                grad_query.append(nn(grad_raw, key) + nn(unskewed, table))
+            both = jnp.where(head_lanes(0), grad_query[0], grad_query[1])
+            dq_ref[here, lanes] = (both * HEAD_DIM**-0.5).astype(jnp.bfloat16)
+            return carry
+
+        lax.fori_loop(0, clips * blocks, attend_block, 0)
+        dk_ref[:, :, lanes] = (dk_sum[...] * HEAD_DIM**-0.5).astype(jnp.bfloat16)
+        dv_ref[:, :, lanes] = dv_sum[...].astype(jnp.bfloat16)
+        pump()
+
+    _, _, seq, _ = place()
+    free = [ref.at[0, pl.ds(0, rows)] for ref in (k_ref, v_ref)]
+    saved = Stream(free, saved_sems, saved_copies(u0, groups, part))
+    edges = []
+    for at, ref in enumerate((dk_ref, dv_ref)):
+        for way, (target, low_row, size, step) in enumerate(
+            ((later, 0, LEFT, span - 1), (earlier, LEFT + rows, 2 * RIGHT, 1))
+        ):
+            edges.append(
+                pltpu.make_async_remote_copy(
+                    src_ref=ref.at[:, pl.ds(low_row, size)],
+                    dst_ref=target.at[at],
+                    send_sem=halo_sems.at[0, 2 * at + way],
+                    recv_sem=halo_sems.at[1, 2 * at + way],
+                    device_id={"seq": (seq + step) % span},
+                    device_id_type=MESH,
+                )
+            )
+    for edge in edges:
+        edge.start()
+    gain = gains[pl.ds(1, 1), :]
+    norm_rows(resid_in, gain, entry)
+    job = pool.add(to_q, 0, 0)
+    gradient_into(job, entry, dq_ref)
+    total[...] = jnp.zeros_like(total)
+    add_transposed(dq_ref, weights.take(), total)
+    pump()
+    for edge in edges:
+        edge.wait()
+    for at, (ref, flat) in enumerate(((dk_ref, mixed_grad), (dv_ref, q_ref))):
+        for clip in range(clips):
+            base = clip * rows
+            flat[pl.ds(base, rows), :] = ref[clip, pl.ds(LEFT, rows), :]
+            tail = pl.ds(base + rows - LEFT, LEFT)
+            zero_tail = jnp.zeros((LEFT, width), jnp.float32)
+            came = jnp.where(seq < span - 1, later[at, clip].astype(jnp.float32), zero_tail)
+            flat[tail, :] = (flat[tail, :].astype(jnp.float32) + came).astype(jnp.bfloat16)
+            head = pl.ds(base, 2 * RIGHT)
+            zero_head = jnp.zeros((2 * RIGHT, width), jnp.float32)
+            came = jnp.where(seq > 0, earlier[at, clip].astype(jnp.float32), zero_head)
+            flat[head, :] = (flat[head, :].astype(jnp.float32) + came).astype(jnp.bfloat16)
+    for target, flat in ((to_k, mixed_grad), (to_v, q_ref)):
+        job = pool.add(target, 0, 0)
+        gradient_into(job, entry, flat)
+        pump()
+        add_transposed(flat, weights.take(), total)
+        pump()
+    norm_back_rows(resid_in, gain, total, resid, gain_sums, 1)
+    load = pltpu.make_async_copy(x0, dq_ref, local.at[0])
+    load.start()
+    cast_rows(resid, low, 0.5)
+    load.wait()
+    gain = gains[pl.ds(0, 1), :]
+    norm_rows(dq_ref, gain, entry)
+    buffers = (entry, low, mixed_grad, q_ref, total)
+    module_back(pool, pump, weights, saved, buffers, chunks, (to_in, to_out))
+    while waiting:
+        pump()
+    norm_back_rows(dq_ref, gain, total, resid, gain_sums, 0)
+    cast_rows(resid, low)
+    store = pltpu.make_async_copy(low, grad_x, local.at[1])
+    store.start()
+    pool.drain()
+    store.wait()
+
+
+def reduce_views(grads):
+    groups = lax.axis_size("group")
+    return [grad.reshape(groups // 2, 2, grad.shape[0] // groups, grad.shape[1]) for grad in grads]
+
+
+def early_list(views, rows, width):
+    return [
+        (source, low, left)
+        for source, view in enumerate(views)
+        for low in range(0, view.shape[2], rows)
+        for left in range(0, view.shape[3], width)
+    ]
+
+
+def reduce_greet():
+    deep, across, _, twin = neighbours()
+    span = lax.axis_size("seq")
+    seq = lax.axis_index("seq")
+    greet(deep + [across, twin] + [{"seq": (seq + steps) % span} for steps in range(1, span)])
+
+
+def late_back(grad, x1, x0, u0, kept, table, gains, weights, grads, rows, halve):
+    query, keys, values, mixed = kept
+    a_out, qkv, w_in, w_out = weights
+    clips, ext, width = keys.shape
+    flat = clips * rows
+    groups = lax.axis_size("group")
+    part = width // groups
+    chunks = w_out.shape[0] // width
+    views = reduce_views(grads)
+    early = early_list(views, part, width)
+    count = len(early) + 4 + 2 * chunks
+    plan = [2 if halve and at % 2 == 0 else 1 for at in range(count)]
+    first = lax.axis_index("seq").astype(jnp.int32)[None] * rows
+    limit = rows * lax.axis_size("seq")
+    hbm = pl.BlockSpec(memory_space=pl.ANY)
+    vmem = pl.BlockSpec(memory_space=pltpu.VMEM)
+    low = lambda *shape: jax.ShapeDtypeStruct(shape, jnp.bfloat16)
+    wide = lambda *shape: jax.ShapeDtypeStruct(shape, jnp.float32)
+    holds = [pltpu.VMEM((flat, width), jnp.float32)] * 3
+    holds += [pltpu.VMEM((flat, width), jnp.bfloat16)] * 5
+    holds += [pltpu.VMEM((clips, ext, width), jnp.bfloat16)] * 4
+    holds += [
+        pltpu.VMEM((2, clips, LEFT, width), jnp.bfloat16),
+        pltpu.VMEM((2, clips, 2 * RIGHT, width), jnp.bfloat16),
+        pltpu.VMEM((clips, ext, LANES), jnp.float32),
+        pltpu.VMEM((clips, ext, LANES), jnp.float32),
+        pltpu.VMEM((3, width, width), jnp.bfloat16),
+        pltpu.SemaphoreType.DMA((6,)),
+        pltpu.SemaphoreType.DMA((3, groups)),
+        pltpu.SemaphoreType.DMA((2, groups)),
+        pltpu.SemaphoreType.DMA((2, 4)),
+    ]
+    results = pl.pallas_call(
+        functools.partial(late_back_kernel, (plan, early, len(views), clips, rows, limit)),
+        in_specs=[pl.BlockSpec(memory_space=pltpu.SMEM), vmem, vmem] + [hbm] * (12 + len(views)),
+        out_specs=[hbm, vmem, vmem] + [hbm] * (6 + len(views)),
+        out_shape=[low(flat, width), wide(8, width), wide(SPAN, LANES)]
+        + [low(part, width)] * 4
+        + [low(chunks * part, width), low(part, chunks * width)]
+        + [low(*view.shape[2:]) for view in views],
+        scratch_shapes=holds + Pool.scratch(part, width, plan),
+        compiler_params=pltpu.CompilerParams(
+            collective_id=3, has_side_effects=True, vmem_limit_bytes=62 << 20
+        ),
+        name="late_back",
+    )(
+        first,
+        wide_table(table),
+        gains,
+        grad,
+        x1,
+        x0,
+        u0,
+        mixed,
+        query.reshape(flat, width),
+        keys,
+        values,
+        a_out,
+        qkv,
+        w_in,
+        w_out.reshape(groups, chunks, part, width),
+        *views,
+    )
+    grad_x, gain_sums, dt = results[:3]
+    dt = (dt[:WIN, :HEAD_DIM] + dt[:WIN, HEAD_DIM:]) * HEAD_DIM**-0.5
+    return grad_x, gain_sums, dt, results[3:9], results[9:]
+
+
+def unmix(grad, groups):
+    rows, width = grad.shape
+    chunks = width // (rows * groups)
+    return grad.reshape(rows, chunks, groups, rows).transpose(0, 2, 1, 3).reshape(rows, width)
 
 
 def feed_forward(resid, gain, w_in, w_out):
@@ -445,12 +1104,12 @@
     return (matmul(hidden, w_out), (normal, inverse, entry, hidden_pre, hidden))
 
 
-def feed_back(grad_branch, kept, gain, w_in, w_out, halve):
+def feed_back(grad_branch, kept, gain, w_in, w_out):
     normal, inverse, entry, hidden_pre, hidden = kept
     grad_low = grad_branch.astype(jnp.bfloat16)
-    grad_w_out = reduce_gradient(hidden, grad_low, halve)
+    grad_w_out = matmul_left_t(hidden, grad_low).astype(jnp.bfloat16)
     grad_hidden = (matmul_right_t(grad_low, w_out) * swish_grad(hidden_pre)).astype(jnp.bfloat16)
-    grad_w_in = reduce_gradient(entry, grad_hidden, halve)
+    grad_w_in = matmul_left_t(entry, grad_hidden).astype(jnp.bfloat16)
     grad_in, grad_gain = norm_backward(matmul_right_t(grad_hidden, w_in), normal, inverse, gain)
     return (grad_in, grad_gain, grad_w_in, grad_w_out)
 
@@ -478,7 +1137,7 @@
     clips, rows, width = shape
     normal, inverse, entry, query, keys, values, mixed = kept
     grad_low = grad_branch.astype(jnp.bfloat16)
-    grad_attn_out = reduce_gradient(mixed, grad_low, False)
+    grad_attn_out = matmul_left_t(mixed, grad_low).astype(jnp.bfloat16)
     grad_mixed = matmul_right_t(grad_low, attn_out).astype(jnp.bfloat16).reshape(shape)
     grad_query, grad_keys, grad_values, grad_table = attend_back(
         query, keys, values, table, grad_mixed, rows
@@ -493,8 +1152,7 @@
         return own.astype(jnp.bfloat16).reshape(clips * rows, width)
 
     parts = [grad_query.reshape(clips * rows, width), fold(grad_keys), fold(grad_values)]
-    grad_qkv = reduce_gradient(entry, jnp.concatenate(parts, 1), False)
-    grad_qkv = grad_qkv.reshape(-1, 3, width).transpose(1, 0, 2)
+    grad_qkv = [matmul_left_t(entry, part).astype(jnp.bfloat16) for part in parts]
     grad_entry = sum(matmul_right_t(part, qkv[at]) for at, part in enumerate(parts))
     grad_in, grad_gain = norm_backward(grad_entry, normal, inverse, gain)
     return (grad_in, grad_gain, grad_qkv, grad_attn_out, grad_table)
@@ -535,7 +1193,7 @@
     normal, inverse, entry, joined, opened, padded, middle, mid_normal, mid_inverse, swished = kept
     taps = depthwise.astype(jnp.float32)
     grad_low = grad_branch.astype(jnp.bfloat16)
-    grad_conv_out = reduce_gradient(swished, grad_low, False)
+    grad_conv_out = matmul_left_t(swished, grad_low).astype(jnp.bfloat16)
     grad_middle = matmul_right_t(grad_low, conv_out) * swish_grad(middle)
     grad_summed, grad_gain_mid = norm_backward(grad_middle, mid_normal, mid_inverse, gain_mid)
     grad_summed = grad_summed.reshape(clips, rows, width)
@@ -561,7 +1219,7 @@
         [grad_glu * opened, grad_glu * value_part * opened * (1.0 - opened)], 1
     )
     grad_joined = grad_joined.astype(jnp.bfloat16)
-    grad_conv_in = reduce_gradient(entry, grad_joined, False)
+    grad_conv_in = matmul_left_t(entry, grad_joined).astype(jnp.bfloat16)
     grad_in, grad_gain_in = norm_backward(
         matmul_right_t(grad_joined, conv_in), normal, inverse, gain_in
     )
@@ -632,21 +1290,50 @@
     grad = cotangent.reshape(flat_rows, width).astype(jnp.float32)
     grad, grad_gain_final = norm_backward(grad, final_normal, final_inverse, gain_f[5])
     back_in, grad_gain_second, grad_in_second, grad_out_second = feed_back(
-        0.5 * grad, second_kept, gain_f[4], f_in[1], f_out[1], halve
+        0.5 * grad, second_kept, gain_f[4], f_in[1], f_out[1]
     )
     grad = grad + back_in
     back_in, grad_gain_conv, grad_gain_mid, grad_conv_in, grad_taps, grad_conv_out = conv_back(
         grad, conv_kept, gain_f[2], gain_f[3], c_in, depth, c_out, shape
     )
     grad = grad + back_in
-    back_in, grad_gain_attn, grad_qkv, grad_attn_out, grad_table = attention_back(
-        grad, attn_kept, gain_f[1], proj, a_out, rel_table, shape
-    )
-    grad = grad + back_in
-    back_in, grad_gain_first, grad_in_first, grad_out_first = feed_back(
-        0.5 * grad, first_kept, gain_f[0], f_in[0], f_out[0], halve
-    )
-    grad = grad + back_in
+    if halve and clips == 1 and gains.shape[1] % LANES == 0:
+        early = [grad_out_second, grad_in_second, grad_conv_out, grad_conv_in]
+        grad, gain_sums, grad_table, mine, early = late_back(
+            grad,
+            after_first,
+            tokens.reshape(flat_rows, width),
+            first_kept[3].astype(jnp.bfloat16),
+            attn_kept[3:],
+            rel_table,
+            small[:8].astype(jnp.float32),
+            (a_out, proj, f_in[0], f_out[0]),
+            early,
+            rows,
+            halve,
+        )
+        grad_gain_first, grad_gain_attn = (gain_sums[0], gain_sums[1])
+        grad_attn_out, grad_out_first = (mine[0], mine[4])
+        grad_qkv, grad_in_first = (mine[1:4], unmix(mine[5], lax.axis_size("group")))
+        grad_out_second, grad_in_second, grad_conv_out, grad_conv_in = early
+    else:
+        back_in, grad_gain_attn, grad_qkv, grad_attn_out, grad_table = attention_back(
+            grad, attn_kept, gain_f[1], proj, a_out, rel_table, shape
+        )
+        grad = grad + back_in
+        back_in, grad_gain_first, grad_in_first, grad_out_first = feed_back(
+            0.5 * grad, first_kept, gain_f[0], f_in[0], f_out[0]
+        )
+        grad = grad + back_in
+        matrices = [grad_in_first, grad_in_second, grad_out_first, grad_out_second]
+        matrices += [grad_attn_out, grad_conv_in, grad_conv_out] + grad_qkv
+        matrices = [
+            lax.psum(lax.psum_scatter(member, "group", tiled=True), ("seq", "replica"))
+            for member in matrices
+        ]
+        grad_in_first, grad_in_second, grad_out_first, grad_out_second = matrices[:4]
+        grad_attn_out, grad_conv_in, grad_conv_out = matrices[4:7]
+        grad_qkv = matrices[7:]
     gain_grads = jnp.stack(
         [
             grad_gain_first,
@@ -673,12 +1360,12 @@
     return (
         result.astype(jnp.bfloat16).reshape(shape),
         grad.astype(jnp.bfloat16).reshape(shape),
-        jnp.stack([grad_in_first, grad_in_second]),
-        jnp.stack([grad_out_first, grad_out_second]),
-        grad_qkv,
-        grad_attn_out,
-        grad_conv_in,
-        grad_conv_out,
+        jnp.stack([grad_in_first, grad_in_second]).astype(jnp.float32),
+        jnp.stack([grad_out_first, grad_out_second]).astype(jnp.float32),
+        jnp.stack(grad_qkv).astype(jnp.float32),
+        grad_attn_out.astype(jnp.float32),
+        grad_conv_in.astype(jnp.float32),
+        grad_conv_out.astype(jnp.float32),
         owned[norms:],
         owned[:norms],
         loose[:table_size].reshape(rel_table.shape),

time: 1340 us -> 818 us (0.61)
  waiting for transfers between devices: 358 us -> 20.2 us
  Pallas kernels: 317 us -> 541 us
  local copies, waits for them, and re-layouts: 212 us -> 28.7 us
  starting transfers between devices: 122 us -> 25.7 us
  matrix products: 199 us -> 104 us
  other arithmetic: 123 us -> 87.5 us
    ppermute x45 -> x5, waiting for transfers between devices: 266 us -> 14.5 us  [swap(): lax.ppermute(value, axis, [(i, i ^ bit) for i in range(lax.axis_size(axis...]
    pallas_call x1, Pallas kernels: 61 us -> 285 us  [late_back(): pl.pallas_call(functools.partial(late_back_kernel, (plan, early, len(view...]
    ppermute x24 -> x0, waiting for transfers between devices: 90.8 us -> none  [along_depth(): return lax.ppermute(value, 'group', pairs)]
    unnamed x417 -> x115, local copies, waits for them, and re-layouts: 95.5 us -> 15.8 us
    dynamic_slice x24 -> x0, local copies, waits for them, and re-layouts: 60 us -> none  [the longest x20 53 us: side(): picked = lax.dynamic_index_in_dim(split, x, axis + 1, False)]
    ppermute x24 -> x0, starting transfers between devices: 53.7 us -> none  [along_depth(): return lax.ppermute(value, 'group', pairs)]
    dot_general x32 -> x4, matrix products: 78.8 us -> 26.9 us  [matmul_left_t(): lax.dot_general(left, right, (((0,), (0,)), ((), ())), preferred_element_...]
    ppermute x45 -> x5, starting transfers between devices: 41.1 us -> 7.64 us  [swap(): lax.ppermute(value, axis, [(i, i ^ bit) for i in range(lax.axis_size(axis...]
  transfers between devices with their start and end apart: 79 -> 11, of which waited for: 25 -> 7; matrix products, arithmetic and copies ran while one was open for 23% -> 2% of each run, Pallas kernels for 5% -> 0%
where the time goes in v3:
time: 818 us; the launch traced here: 809 us
  Pallas kernels  541 us (66%)
  matrix products  104 us (13%)
  other arithmetic  87.5 us (11%)
  local copies, waits for them, and re-layouts  28.7 us (4%)
  starting transfers between devices  25.7 us (3%)
  waiting for transfers between devices  20.2 us (2%)
    pallas_call x1, Pallas kernels, late_back(): pl.pallas_call(functools.partial(late_back_kernel, (plan, early, len(view...  285 us
    pallas_call x1, Pallas kernels, gather_weights(): pl.pallas_call(functools.partial(gather_kernel, plan, len(shards)), in_sp...  232 us
    dot_general x10, matrix products, matmul(): return jnp.dot(left, right, preferred_element_type=jnp.float32)  50.4 us
    dot_general x4, matrix products, matmul_right_t(): lax.dot_general(left, right, (((1,), (1,)), ((), ())), preferred_element_...  27.1 us
    dot_general x4, matrix products, matmul_left_t(): lax.dot_general(left, right, (((0,), (0,)), ((), ())), preferred_element_...  26.9 us
    pallas_call x1, Pallas kernels, attend(): pl.pallas_call(functools.partial(attend_kernel, limit), grid=grid, in_spe...  24.5 us
    add x1, other arithmetic, conv_back(): grad_padded + jnp.pad(grad_summed * taps[tap], ((0, 0), (tap, KERNEL - 1...  18.7 us
    ppermute x6, starting transfers between devices, from_behind(): lax.ppermute(value, axis, [(source, source + steps) for source in range(i...  18.1 us
  transfers between devices with their start and end apart: 11, of which 7 were waited for; matrix products, arithmetic and copies ran while one was open for 2% of the time, Pallas kernels for 0%

profile of v3, /device:TPU:0, one launch (start us, length us, event | category | flops | bytes accessed | tf_op | source)
XLA Modules:
  0.0 809.5 jit_solution(18365992437257055461)
XLA Ops:
  9.6 231.9 %gather_weights.1 = (bf16[1,384,128]{2,1,0:T(8,128)(2,1)S(1)}, bf16[1,1024,4096]{2,1,0:T(8,128)(2,1)S(1)}, bf16[1,4096,1024]{2,1,0:T(8,128)(2,1)}, bf16[3,1024,1...) custom-call(bf16[1,48,128]{2,1,0:T(8,128)(2,1)S(1)} %fusion.118.refs, ...), custom_call_target="tpu_custom_call" | custom-call | tf_op jit(solution)/shard_map/gather_weights/pallas_call | solution.py:341
  244.3 8.7 %fusion.143 = (bf16[512,4096]{1,0:T(8,128)(2,1)}, f32[512,4096]{1,0:T(8,128)}) fusion(bf16[1,1024,4096]{2,1,0:T(8,128)(2,1)S(1)} %get-tuple-element.47, bf16[1,512,1024]{2,1,0:T(8,128)(2,1)S(1)} %copy-done.16, f32[1024]{0:T(1024)S(1)} %bitcast.547, f32[512]{0:T(512)S(1)} %add_rsqrt_fusion.5, f32[512]{0:T(512)S(1)} %broadcast_multiply_fusion.13), kind=kOutput, calls=%fused_computation.278 | convolution fusion | flops 4299685888 | bytes 22028288 | tf_op jit(solution)/shard_map/dot_general | solution.py:53
  253.7 10.9 %fusion.139 = (f32[512]{0:T(512)S(1)}, f32[512,1024]{1,0:T(8,128)S(1)}, f32[]{:T(128)}) fusion(bf16[1,512,1024]{2,1,0:T(8,128)(2,1)S(1)} %copy-done.16, bf16[1,4096,1024]{2,1,0:T(8,128)(2,1)S(1)} %copy-done.17, f32[512,4096]{1,0:T(8,128)} %get-tuple-element.217), kind=kOutput, calls=%fused_computation.274 | convolution fusion | flops 4308598272 | bytes 19924996 | tf_op jit(solution)/shard_map/dot_general | solution.py:53
  269.8 5.6 collective-permute-start.2
  279.2 5.8 collective-permute-start
  292.1 24.5 %attend.1 = bf16[1,512,1024]{2,1,0:T(8,128)(2,1)} custom-call(s32[1]{0:T(128)} %bitcast.11.first_ref.refs_0_, bf16[1,512,1024]{2,1,0:T(8,128)(2,1)} %bitcast.417, bf16[1,640,1024]{2,1,0:T(8,128)(2,1)} %get-tuple-element.212.k_ref.refs_9_, bf16[1,640,1024]{2,1,0:T(8,128)(2,1)} %get-tuple-element.211.v_ref.refs_10_, bf16[256,128]{1,0:T(8,128)(2,1)} %copy.25.t_ref.refs_1_), custom_call_target="tpu_custom_call" | custom-call | tf_op jit(solution)/shard_map/attend/pallas_call | solution.py:153
  316.6 4.1 fusion.138
  330.8 10.0 %fusion.137 = (f32[512]{0:T(512)S(1)}, f32[1,512,1024]{2,1,0:T(8,128)S(1)}) fusion(f32[1,542,1024]{2,1,0:T(8,128)S(1)} %maximum_convert_fusion.2, f32[1024]{0:T(1024)S(1)} %bitcast.465, f32[1024]{0:T(1024)S(1)} %bitcast.467, f32[1024]{0:T(1024)S(1)} %bitcast.469, f32[1024]{0:T(1024)S(1)} %bitcast.471, f32[1024]{0:T(1024)S(1)} %bitcast.473, ...), kind=kLoop, calls=%fused_computation.272 | loop fusion | flops 32505344 | bytes 67237888 | tf_op jit(solution)/shard_map/reduce_sum | solution.py:35
  345.5 6.9 fusion.6
  352.4 10.3 %fusion.135 = (f32[512]{0:T(512)S(1)}, f32[512,1024]{1,0:T(8,128)S(1)}, f32[]{:T(128)}) fusion(f32[512,1024]{1,0:T(8,128)S(1)} %get-tuple-element.128, bf16[1,4096,1024]{2,1,0:T(8,128)(2,1)} %get-tuple-element.54, f32[512,4096]{1,0:T(8,128)} %fusion.6), kind=kOutput, calls=%fused_computation.270 | convolution fusion | flops 4308073984 | bytes 20973572 | tf_op jit(solution)/shard_map/dot_general | solution.py:53
  365.7 12.1 %multiply_convert_fusion = bf16[512,4096]{1,0:T(8,128)(2,1)} fusion(bf16[1,4096,1024]{2,1,0:T(8,128)(2,1)} %get-tuple-element.54, f32[512,4096]{1,0:T(8,128)} %fusion.6, f32[512,1024]{1,0:T(8,128)S(1)} %get-tuple-element.126, bf16[1,512,1024]{2,1,0:T(8,128)(2,1)S(1)} %copy-done.24, f32[512]{0:T(512)S(1)} %get-tuple-element.218, ...), kind=kOutput, calls=%fused_computation.10 | convolution fusion | flops 4319084544 | bytes 24129536 | tf_op jit(solution)/shard_map/dot_general | solution.py:63
  377.8 12.2 %convolution_convert_fusion.1 = bf16[4096,1024]{1,0:T(8,128)(2,1)} fusion(f32[512,1024]{1,0:T(8,128)S(1)} %get-tuple-element.126, bf16[1,512,1024]{2,1,0:T(8,128)(2,1)S(1)} %copy-done.24, f32[512]{0:T(512)S(1)} %get-tuple-element.218, f32[512]{0:T(512)S(1)} %get-tuple-element.219, f32[1024]{0:T(1024)S(1)} %bitcast.461, f32[512]{0:T(512)S(1)} %add_rsqrt_fusion, ...), kind=kOutput, calls=%fused_computation.14 | convolution fusion | flops 4314890240 | bytes 19935232 | tf_op jit(solution)/shard_map/dot_general | solution.py:57
  390.0 8.7 %multiply_reduce_fusion.5 = (f32[1024]{0:T(1024)S(1)}, f32[512]{0:T(512)S(1)}, f32[512]{0:T(512)S(1)}, f32[512,1024]{1,0:T(8,128)S(1)}) fusion(f32[512,1024]{1,0:T(8,128)S(1)} %copy-done.23, f32[512]{0:T(512)S(1)} %add_rsqrt_fusion.1, f32[512]{0:T(512)S(1)} %broadcast_multiply_fusion.9, f32[1024]{0:T(1024)S(1)} %bitcast.518, ...), kind=kOutput, calls=%fused_computation.124 | convolution fusion | flops 4299159552 | bytes 16793600 | tf_op jit(solution)/shard_map/dot_general | solution.py:63
  401.5 3.5 multiply_reduce_fusion.6
  407.9 7.1 convolution_convert_fusion
  415.0 7.2 fusion.61
  425.6 9.2 %multiply_bitcast_fusion.29 = (f32[1,512,1024]{2,1,0:T(8,128)}, f32[1,512,1024]{2,1,0:T(8,128)}, f32[1,512,1024]{2,1,0:T(8,128)}, f32[1,512,1024]{2,1,0:T(8,128)...) fusion(f32[512,1024]{1,0:T(8,128)S(1)} %get-tuple-element.124, ...), kind=kLoop, calls=%fused_computation.160 | loop fusion | flops 6815744 | bytes 29413376 | tf_op jit(solution)/shard_map/mul | solution.py:1206
  434.7 8.7 %multiply_bitcast_fusion.30 = (f32[1,512,1024]{2,1,0:T(8,128)S(1)}, f32[1,512,1024]{2,1,0:T(8,128)S(1)}, f32[1,512,1024]{2,1,0:T(8,128)S(1)}, f32[1,512,1024]{2,...) fusion(f32[512,1024]{1,0:T(8,128)S(1)} %get-tuple-element.124, ...), kind=kLoop, calls=%fused_computation.161 | loop fusion | flops 9437184 | bytes 39919616 | tf_op jit(solution)/shard_map/mul | solution.py:1206
  443.4 18.7 %pad_add_fusion = f32[1,542,1024]{2,1,0:T(8,128)S(1)} fusion(f32[1,512,1024]{2,1,0:T(8,128)S(1)} %get-tuple-element.144, f32[1,512,1024]{2,1,0:T(8,128)S(1)} %get-tuple-element.145, f32[1,512,1024]{2,1,0:T(8,128)S(1)} %get-tuple-element.146, f32[1,512,1024]{2,1,0:T(8,128)S(1)} %get-tuple-element.147, f32[1,512,1024]{2,1,0:T(8,128)S(1)} %get-tuple-element.148, ...), kind=kLoop, calls=%fused_computation.31 | loop fusion | flops 16650240 | bytes 67231744 | tf_op jit(solution)/shard_map/add | solution.py:1205
  463.8 4.5 collective-permute-done.5
  469.0 3.4 multiply_convert_fusion.4
  475.9 4.6 convolution_convert_fusion.2
  482.6 285.0 %late_back.1 = (bf16[512,1024]{1,0:T(8,128)(2,1)}, f32[8,1024]{1,0:T(8,128)}, f32[256,128]{1,0:T(8,128)}, bf16[128,1024]{1,0:T(8,128)(2,1)}, bf16[128,1024]{1,0:...) custom-call(s32[1]{0:T(128)} %bitcast.11.first_ref.refs_0_, ...), custom_call_target="tpu_custom_call" | custom-call | tf_op jit(solution)/shard_map/late_back/pallas_call | solution.py:1057
  776.9 5.4 collective-permute-done.7
  (223 shorter events, 99.0 us)
Async XLA Ops:
  9.6 234.6 %copy-start.16 = (bf16[1,512,1024]{2,1,0:T(8,128)(2,1)S(1)}, bf16[1,512,1024]{2,1,0:T(8,128)(2,1)}, u32[]{:S(2)}) copy-start(bf16[1,512,1024]{2,1,0:T(8,128)(2,1)} %param.13) | copy-start | bytes 3145732
  243.5 9.5 %copy-start = (bf16[1,1024,4096]{2,1,0:T(8,128)(2,1)}, bf16[1,1024,4096]{2,1,0:T(8,128)(2,1)S(1)}, u32[]{:S(2)}) copy-start(bf16[1,1024,4096]{2,1,0:T(8,128)(2,1)S(1)} %get-tuple-element.47) | copy-start | bytes 25165828
  243.6 10.1 %copy-start.12 = (bf16[1,1024,1024]{2,1,0:T(8,128)(2,1)}, bf16[1,1024,1024]{2,1,0:T(8,128)(2,1)S(1)}, u32[]{:S(2)}) copy-start(bf16[1,1024,1024]{2,1,0:T(8,128)(2,1)S(1)} %get-tuple-element.52) | copy-start | bytes 6291460
  243.6 41.5 %copy-start.1 = (bf16[3,1024,1024]{2,1,0:T(8,128)(2,1)}, bf16[3,1024,1024]{2,1,0:T(8,128)(2,1)S(1)}, u32[]{:S(2)}) copy-start(bf16[3,1024,1024]{2,1,0:T(8,128)(2,1)S(1)} %get-tuple-element.49.refs_12_) | copy-start | bytes 18874372
  243.6 73.1 %copy-start.4 = (bf16[1,1024,1024]{2,1,0:T(8,128)(2,1)}, bf16[1,1024,1024]{2,1,0:T(8,128)(2,1)S(1)}, u32[]{:S(2)}) copy-start(bf16[1,1024,1024]{2,1,0:T(8,128)(2,1)S(1)} %get-tuple-element.50) | copy-start | bytes 6291460
  244.3 9.4 %copy-start.17 = (bf16[1,4096,1024]{2,1,0:T(8,128)(2,1)S(1)}, bf16[1,4096,1024]{2,1,0:T(8,128)(2,1)}, u32[]{:S(2)}) copy-start(bf16[1,4096,1024]{2,1,0:T(8,128)(2,1)} %get-tuple-element.48) | copy-start | bytes 25165828
  267.8 21.0 %collective-permute-start.3 = (bf16[1,8,1024]{2,1,0:T(8,128)(2,1)}, bf16[1,8,1024]{2,1,0:T(8,128)(2,1)}, u32[]{:S(2)}, u32[]{:S(2)}) collective-permute-start(bf16[1,8,1024]{2,1,0:T(8,128)(2,1)} %slice.514), channel_id=1, source_target_pairs={{16,0},{17,1},{18,2},{19,3},{20,4},{21,5},{22,6},{23,7},{24,8},{25... | collective-permute-start | bytes 49160 | tf_op jit(solution)/shard_map/ppermute | solution.py:31
  269.8 19.1 %collective-permute-start.2 = (bf16[1,64,1024]{2,1,0:T(8,128)(2,1)}, bf16[1,64,1024]{2,1,0:T(8,128)(2,1)S(1)}, u32[]{:S(2)}, u32[]{:S(2)}) collective-permute-start(bf16[1,64,1024]{2,1,0:T(8,128)(2,1)} %slice.513), channel_id=1, source_target_pairs={{0,16},{1,17},{2,18},{3,19},{4,20},{5,21},{6,22},{7,23},{8,24},{9,... | collective-permute-start | bytes 393224 | tf_op jit(solution)/shard_map/ppermute | solution.py:31
  276.6 10.7 %copy-start.25 = (bf16[1,512,1024]{2,1,0:T(8,128)(2,1)}, bf16[1,512,1024]{2,1,0:T(8,128)(2,1)S(1)}, u32[]{:S(2)}) copy-start(bf16[1,512,1024]{2,1,0:T(8,128)(2,1)S(1)} %fusion.91) | copy-start | bytes 3145732
  277.3 11.6 %collective-permute-start.1 = (bf16[1,8,1024]{2,1,0:T(8,128)(2,1)}, bf16[1,8,1024]{2,1,0:T(8,128)(2,1)}, u32[]{:S(2)}, u32[]{:S(2)}) collective-permute-start(bf16[1,8,1024]{2,1,0:T(8,128)(2,1)} %slice.512), channel_id=1, source_target_pairs={{16,0},{17,1},{18,2},{19,3},{20,4},{21,5},{22,6},{23,7},{24,8},{25... | collective-permute-start | bytes 49160 | tf_op jit(solution)/shard_map/ppermute | solution.py:31
  279.2 9.6 %collective-permute-start = (bf16[1,64,1024]{2,1,0:T(8,128)(2,1)}, bf16[1,64,1024]{2,1,0:T(8,128)(2,1)}, u32[]{:S(2)}, u32[]{:S(2)}) collective-permute-start(bf16[1,64,1024]{2,1,0:T(8,128)(2,1)} %slice.511), channel_id=1, source_target_pairs={{0,16},{1,17},{2,18},{3,19},{4,20},{5,21},{6,22},{7,23},{8,24},{9,... | collective-permute-start | bytes 393224 | tf_op jit(solution)/shard_map/ppermute | solution.py:31
  320.7 20.5 %copy-start.18 = (f32[512,1024]{1,0:T(8,128)}, f32[512,1024]{1,0:T(8,128)S(1)}, u32[]{:S(2)}) copy-start(f32[512,1024]{1,0:T(8,128)S(1)} %get-tuple-element.132) | copy-start | bytes 6291460
  325.9 4.6 collective-permute-start.4
  344.7 7.7 copy-start.22
  377.8 12.2 %copy-start.23 = (f32[512,1024]{1,0:T(8,128)S(1)}, f32[512,1024]{1,0:T(8,128)}, u32[]{:S(2)}) copy-start(f32[512,1024]{1,0:T(8,128)} %copy-done.22) | copy-start | bytes 6291460
  462.2 6.2 collective-permute-start.5
  482.6 290.1 %copy-start.43 = (f32[1024]{0:T(1024)S(1)}, f32[1024]{0:T(1024)}, u32[]{:S(2)}) copy-start(f32[1024]{0:T(1024)} %get-tuple-element.117) | copy-start | bytes 12292
  767.6 17.5 %copy-start.27 = (bf16[128,4096]{1,0:T(8,128)(2,1)S(1)}, bf16[128,4096]{1,0:T(8,128)(2,1)}, u32[]{:S(2)}) copy-start(bf16[128,4096]{1,0:T(8,128)(2,1)} %get-tuple-element.56) | copy-start | bytes 3145732
  773.1 1.5 collective-permute-start.6
  774.7 7.6 collective-permute-start.7
  782.3 7.4 collective-permute-start.8
  789.7 5.8 collective-permute-start.9
  795.6 10.0 %collective-permute-start.10 = (f32[42,1024]{1,0:T(8,128)S(1)}, f32[42,1024]{1,0:T(8,128)S(1)}, u32[]{:S(2)}, u32[]{:S(2)}) collective-permute-start(f32[42,1024]{1,0:T(8,128)S(1)} %add.449), channel_id=1, source_target_pairs={{0,8},{2,10},{4,12},{6,14},{8,0},{10,2},{12,4},{14,6},{1,9},{3,11}... | collective-permute-start | bytes 516104 | tf_op jit(solution)/shard_map/ppermute | solution.py:365
  801.6 6.8 copy-start.26
  (43 other events, 131.7 us)

commit v4 on v3

--- a/solution.py
+++ b/solution.py
@@ -193,10 +193,11 @@
 
 
 class Gather:
-    def __init__(self, source, target, cut, low, high, rows, sends, recvs, at):
+    def __init__(self, source, target, cut, low, left, rows, size, sends, recvs, at):
         depth = depth_of()
         self.source, self.target, self.cut, self.low, self.rows = (source, target, cut, low, rows)
-        self.piece = (high - low) // (1, 2, 4)[cut]
+        self.piece = size[0] // (1, 2, 4)[cut]
+        self.columns = pl.ds(left, size[1])
         self.sends, self.recvs, self.at = (sends, recvs, at)
         self.z, self.x, self.seq, self.replica = place()
         self.deep, self.across, self.beside, self.twin = neighbours()
@@ -211,7 +212,7 @@
         if self.cut == 2:
             part = part + 2 * ((self.seq + dy) % 2)
         first = pl.multiple_of(owner * self.rows + self.low + part * self.piece, self.piece)
-        return ref.at[:, pl.ds(first, self.piece)]
+        return ref.at[pl.ds(first, self.piece), self.columns]
 
     def owner(self, steps, dx):
         return (self.z + self.depth - steps) % self.depth * 2 + (self.x + dx) % 2
@@ -283,12 +284,12 @@
             copy.wait_send()
 
 
-def gather_kernel(plan, count, *refs):
-    ins, outs = (refs[:count], refs[count : count + len(plan)])
-    helds, (sends, recvs, local) = (refs[count + len(plan) : -3], refs[-3:])
+def gather_kernel(plan, sources, count, *refs):
+    ins, outs = (refs[:count], refs[count : count + len(sources)])
+    helds, (sends, recvs, local) = (refs[count + len(sources) : -3], refs[-3:])
     deep, across, beside, twin = neighbours()
     peers = deep + [across, twin]
-    if any(cut == 2 for _, _, cut, _ in plan):
+    if any(member[-1] == 2 for member in plan):
         peers.append(beside)
     greet(peers)
     loads = [
@@ -296,37 +297,32 @@
     ]
     for load in loads:
         load.start()
-    jobs, stores, at = ([], [], 0)
-    for number, (source, layers, cut, chunks) in enumerate(plan):
-        ref = ins[source].at[pl.ds(layers[0], layers[1])]
+    jobs, at = ([], 0)
+    for number, layer, low, left, size, cut in plan:
+        source, first = sources[number]
+        ref = ins[source].at[first + layer]
         rows = ins[source].shape[1]
-        for chunk in range(chunks):
-            low, high = (rows * chunk // chunks, rows * (chunk + 1) // chunks)
-            jobs.append(Gather(ref, outs[number], cut, low, high, rows, sends, recvs, at))
-            at += (2, 6, 8)[cut] * depth_of()
+        target = outs[number].at[layer]
+        jobs.append(Gather(ref, target, cut, low, left, rows, size, sends, recvs, at))
+        at += (2, 6, 8)[cut] * depth_of()
     z, x, _, _ = place()
-    ready = set()
-    for tick in range(len(jobs) + 4):
-        if tick < len(jobs):
-            jobs[tick].open()
-        if 1 <= tick < len(jobs) + 1:
-            jobs[tick - 1].forward_deep()
-        if 2 <= tick < len(jobs) + 2:
-            jobs[tick - 2].forward_across()
-        if 3 <= tick < len(jobs) + 3:
-            jobs[tick - 3].forward_beside()
-        if 4 <= tick:
-            jobs[tick - 4].close()
-        if tick < len(plan):
-            source, layers, _, _ = plan[tick]
+    ready, stores = (set(), [])
+    for tick in range(len(jobs) + 8):
+        for lag, name in enumerate(
+            ("open", "forward_deep", "forward_across", "forward_beside", "close")
+        ):
+            if 0 <= tick - 2 * lag < len(jobs):
+                getattr(jobs[tick - 2 * lag], name)()
+        if tick < len(sources):
+            source, first = sources[tick]
             if source not in ready:
                 loads[source].wait()
                 ready.add(source)
             rows = ins[source].shape[1]
-            first = pl.multiple_of((z * 2 + x) * rows, rows)
+            start = pl.multiple_of((z * 2 + x) * rows, rows)
             store = pltpu.make_async_copy(
-                helds[source].at[pl.ds(layers[0], layers[1])],
-                outs[tick].at[:, pl.ds(first, rows)],
+                helds[source].at[pl.ds(first, outs[tick].shape[0])],
+                outs[tick].at[:, pl.ds(start, rows)],
                 local.at[1, tick],
             )
             store.start()
@@ -335,24 +331,35 @@
         store.wait()
 
 
-def gather_weights(shards, plan):
+def gather_weights(shards, sources, halve):
     groups = lax.axis_size("group")
-    total = sum((2, 6, 8)[cut] * depth_of() * chunks for _, _, cut, chunks in plan)
+    width = shards[1].shape[1] * groups
+    part = width // groups
+    plan = [(0, 0, 0, 0, shards[0].shape[1:], 0)]
+    for number, (source, first, layers) in enumerate(sources):
+        for layer in range(layers if source else 0):
+            for low in range(0, shards[source].shape[1], part):
+                for left in range(0, shards[source].shape[2], width):
+                    cut = 2 if halve and len(plan) % 3 else 1
+                    plan.append((number, layer, low, left, (part, width), cut))
+    total = sum((2, 6, 8)[member[-1]] * depth_of() for member in plan)
     return pl.pallas_call(
-        functools.partial(gather_kernel, plan, len(shards)),
+        functools.partial(
+            gather_kernel, plan, [(source, first) for source, first, _ in sources], len(shards)
+        ),
         in_specs=[pl.BlockSpec(memory_space=pl.ANY)] * len(shards),
-        out_specs=[pl.BlockSpec(memory_space=pl.ANY)] * len(plan),
+        out_specs=[pl.BlockSpec(memory_space=pl.ANY)] * len(sources),
         out_shape=[
             jax.ShapeDtypeStruct(
-                (layers[1], groups * shards[source].shape[1], shards[source].shape[2]), jnp.bfloat16
+                (layers, groups * shards[source].shape[1], shards[source].shape[2]), jnp.bfloat16
             )
-            for source, layers, _, _ in plan
+            for source, _, layers in sources
         ],
         scratch_shapes=[pltpu.VMEM(shard.shape, jnp.bfloat16) for shard in shards]
         + [
             pltpu.SemaphoreType.DMA((total,)),
             pltpu.SemaphoreType.DMA((total,)),
-            pltpu.SemaphoreType.DMA((2, len(plan))),
+            pltpu.SemaphoreType.DMA((2, len(sources))),
         ],
         compiler_params=pltpu.CompilerParams(
             collective_id=1, has_side_effects=True, vmem_limit_bytes=24 << 20
@@ -363,12 +370,6 @@
 
 def swap(value, axis, bit=1):
     return lax.ppermute(value, axis, [(i, i ^ bit) for i in range(lax.axis_size(axis))])
-
-
-def along_depth(value, steps):
-    depth = depth_of()
-    pairs = [(i, (i // 2 + steps) % depth * 2 + i % 2) for i in range(2 * depth)]
-    return lax.ppermute(value, "group", pairs)
 
 
 def butterfly(value):
@@ -392,13 +393,14 @@
 
 
 class Reduce:
-    def __init__(self, pool, number, source, target, low, left, cut):
-        self.pool, self.number, self.cut = (pool, number, cut)
-        self.source, self.target, self.low, self.left = (source, target, low, left)
-        self.depth, self.span = (depth_of(), lax.axis_size("seq"))
-        self.width = pool.width
-        self.piece = pool.rows // (2 * cut)
-        self.last = 4 + self.depth
+    def __init__(self, pool, number, target, low, left):
+        self.pool, self.number = (pool, number)
+        self.target, self.low, self.left = (target, low, left)
+        self.source = pool.kept.at[number]
+        self.stage = pool.stage.at[number % 2]
+        self.kept = False
+        self.depth, self.width = (depth_of(), pool.width)
+        self.half, self.unit = (pool.rows // 2, pool.rows // 8)
         self.started = []
         self.stages = [
             self.exchange_twin,
@@ -410,36 +412,34 @@
             self.close,
         ]
         self.done_stages = 0
-        self.ready = source is not None
-        self.turn = pool.cuts.setdefault(cut, [])
-        self.rank = len(self.turn)
-        self.turn.append(self)
-        self.own = pool.own.at[number % pool.ring]
-        self.came = pool.came.at[number % pool.ring]
-        self.from_x = pool.from_x.at[number % pool.ring, :, pl.ds(0, self.piece)]
-        self.from_z = pool.from_z.at[number, :, pl.ds(0, self.piece)]
-        self.finished = pool.finished.at[number % pool.ring, pl.ds(0, self.piece)]
-        if cut == 2:
-            self.from_seq = pool.from_seq.at[self.rank % pool.ring]
-        else:
-            self.shared = pool.shared.at[self.rank]
+        slot = number % pool.ring
+        self.own, self.came = (pool.own.at[slot], pool.came.at[slot])
+        self.from_x, self.from_seq = (pool.from_x.at[slot], pool.from_seq.at[slot])
+        self.from_z, self.shared = (pool.from_z.at[number], pool.shared.at[number])
+        self.alone = pool.finished.at[slot, pl.ds(0, self.unit)]
+        self.joint = pool.finished.at[slot, pl.ds(self.unit, 2 * self.unit)]
 
     def locate(self):
         self.z, self.x, self.seq, self.replica = place()
         self.deep, self.across, self.beside, self.twin = neighbours()
 
-    def part(self, dy, dc):
-        part = (self.replica + dc) % 2
-        if self.cut == 2:
-            part = part + 2 * ((self.seq + dy) % 2)
-        return part
-
-    def row(self, dy, dc, low=0):
-        first = pl.multiple_of(low + self.part(dy, dc) * self.piece, self.piece)
-        return pl.ds(first, self.piece)
-
-    def half(self, dy):
-        return pl.ds(dy * self.piece, self.piece)
+    def rows(self, first, count):
+        return pl.ds(pl.multiple_of(first, self.unit), count * self.unit)
+
+    def near(self):
+        return self.rows(self.seq * self.unit, 3)
+
+    def lone(self):
+        return self.rows(3 * self.unit * self.seq, 1)
+
+    def far(self):
+        return self.rows(3 * self.unit * (1 - self.seq), 1)
+
+    def both(self):
+        return pl.ds(self.unit, 2 * self.unit)
+
+    def side(self, replica):
+        return pl.ds(pl.multiple_of(replica * self.half, self.half), self.half)
 
     def remote(self, source, target, slot, peer):
         return pltpu.make_async_remote_copy(
@@ -459,131 +459,133 @@
     def wait(self, target, slot):
         self.remote(target, target, slot, self.twin).wait_recv()
 
-    def load(self, dy):
-        source = self.source.at[:, :, self.row(dy, 0, self.low), pl.ds(self.left, self.width)]
-        target = self.own.at[:, :, self.row(dy, 0)]
-        return pltpu.make_async_copy(source, target, self.pool.local.at[self.number, dy])
-
-    def credit(self, kind, behind, peer):
-        if behind >= self.pool.ring:
+    def keep(self):
+        return pltpu.make_async_copy(self.stage, self.source, self.pool.local.at[self.number, 0])
+
+    def await_kept(self):
+        if not self.kept:
+            self.keep().wait()
+            self.kept = True
+
+    def load(self):
+        source = self.source.at[:, :, self.side(self.replica)]
+        return pltpu.make_async_copy(source, self.own, self.pool.local.at[self.number, 1])
+
+    def credit(self, kind):
+        if self.number >= self.pool.ring:
             pl.semaphore_wait(self.pool.credits.at[kind], 1)
 
-    def release(self, kind, ahead, peer):
-        if ahead:
+    def release(self, kind, peer):
+        if self.number + self.pool.ring < self.pool.total:
             pl.semaphore_signal(
                 self.pool.credits.at[kind], inc=1, device_id=peer, device_id_type=MESH
             )
 
     def exchange_twin(self):
-        self.credit(0, self.number, self.twin)
-        for dy in reversed(range(self.cut)):
-            if self.source is None:
-                ends = lambda dy=dy: (
-                    self.own.at[:, :, self.row(dy, 1)],
-                    self.came.at[:, :, self.half(dy)],
-                )
-            else:
-                ends = lambda dy=dy: (
-                    self.source.at[:, :, self.row(dy, 1, self.low), pl.ds(self.left, self.width)],
-                    self.came.at[:, :, self.half(dy)],
-                )
-                self.load(dy).start()
-            self.send(ends, dy, self.twin)
+        self.await_kept()
+        self.credit(0)
+        self.load().start()
+        ends = lambda: (self.source.at[:, :, self.side(1 - self.replica)], self.came)
+        self.send(ends, 0, self.twin)
 
     def exchange_seq(self):
-        if self.cut == 2:
-            if self.source is not None:
-                self.load(1).wait()
-            self.wait(self.came.at[:, :, self.half(1)], 1)
-            own = lambda at: self.own.at[at // 2, at % 2, self.row(1, 0)]
-            came = lambda at: self.came.at[at // 2, at % 2, self.half(1)]
-            add_slabs(2 * self.depth, own, own, came)
-            self.credit(1, self.rank, self.beside)
-            self.send(lambda: (self.own.at[:, :, self.row(1, 0)], self.from_seq), 2, self.beside)
-
-    def spots(self, x):
-        sources = [
-            lambda at: self.own.at[at, x, self.row(0, 0)],
-            lambda at: self.came.at[at, x, self.half(0)],
-        ]
-        if self.cut == 2:
-            sources.append(lambda at: self.from_seq.at[at, x])
-        return sources
+        self.load().wait()
+        self.wait(self.came, 0)
+        far = self.far()
+        own = lambda at: self.own.at[at // 2, at % 2, far]
+        add_slabs(2 * self.depth, own, own, lambda at: self.came.at[at // 2, at % 2, far])
+        self.credit(1)
+        self.send(lambda: (self.own.at[:, :, self.far()], self.from_seq), 1, self.beside)
+
+    def gather(self, x, arrived):
+        both, lone = (self.both(), self.lone())
+        refs = [self.own.at[:, x], self.came.at[:, x]]
+        pick = lambda rows: [lambda at, ref=ref: ref.at[at, rows] for ref in refs]
+        shared, alone = (pick(both), pick(lone))
+        alone.append(lambda at: self.from_seq.at[at, x])
+        if arrived:
+            both_here = self.rows(self.unit * (1 - self.seq), 2)
+            lone_here = self.rows(2 * self.unit * self.seq, 1)
+            shared.append(lambda at: self.from_x.at[at, both_here])
+            alone.append(lambda at: self.from_x.at[at, lone_here])
+        add_slabs(self.depth, shared[0], *shared)
+        add_slabs(self.depth, alone[0], *alone)
 
     def exchange_across(self):
-        if self.source is not None:
-            self.load(0).wait()
-        self.wait(self.came.at[:, :, self.half(0)], 0)
-        if self.cut == 2:
-            self.wait(self.from_seq, 2)
-        sources = self.spots(1 - self.x)
-        add_slabs(self.depth, sources[0], *sources)
-        self.credit(2, self.number, self.across)
-        ends = lambda: (self.own.at[:, 1 - self.x, self.row(0, 0)], self.from_x)
-        self.send(ends, 3, self.across)
+        self.wait(self.from_seq, 1)
+        self.gather(1 - self.x, False)
+        self.credit(2)
+        self.send(lambda: (self.own.at[:, 1 - self.x, self.near()], self.from_x), 2, self.across)
 
     def exchange_deep(self):
-        self.wait(self.from_x, 3)
-        sources = self.spots(self.x)
-        add_slabs(self.depth, sources[0], lambda at: self.from_x.at[at], *sources)
+        self.wait(self.from_x, 2)
+        self.gather(self.x, True)
         for steps, peer in enumerate(self.deep, 1):
             ends = lambda steps=steps: (
-                self.own.at[(self.z + steps) % self.depth, self.x, self.row(0, 0)],
+                self.own.at[(self.z + steps) % self.depth, self.x, self.near()],
                 self.from_z.at[steps - 1],
             )
-            self.send(ends, 3 + steps, peer)
-        total = self.pool.total
-        self.release(0, self.number + self.pool.ring < total, self.twin)
-        self.release(2, self.number + self.pool.ring < total, self.across)
-        if self.cut == 2:
-            self.release(1, self.rank + self.pool.ring < self.pool.pairs, self.beside)
+            self.send(ends, 2 + steps, peer)
+        self.release(0, self.twin)
+        self.release(1, self.beside)
+        self.release(2, self.across)
 
     def settle(self):
         for steps in range(1, self.depth):
-            self.wait(self.from_z.at[steps - 1], 3 + steps)
+            self.wait(self.from_z.at[steps - 1], 2 + steps)
         self.flush()
-        sources = [lambda at: self.own.at[self.z, self.x, self.row(0, 0)]]
-        sources += [lambda at, steps=steps: self.from_z.at[steps - 1] for steps in range(1, self.depth)]
-        if self.cut == 2:
-            add_slabs(1, lambda at: self.finished, *sources)
-            self.publish()
-            self.send(lambda: (self.finished, self.spot(0, 0)), self.last, self.beside)
-        else:
-            add_slabs(1, lambda at: self.shared.at[self.seq], *sources)
-            for steps in range(1, self.span):
-                peer = {"seq": (self.seq + steps) % self.span}
-                ends = lambda: (self.shared.at[self.seq], self.shared.at[self.seq])
-                self.send(ends, self.last + 2 + steps, peer)
-
-    def spot(self, dy, dc):
-        return self.target.at[self.row(dy, dc, self.low), pl.ds(self.left, self.width)]
-
-    def store(self):
-        return pltpu.make_async_copy(
-            self.finished, self.spot(0, 0), self.pool.local.at[self.number, 2]
-        )
-
-    def publish(self):
-        self.store().start()
-        self.send(lambda: (self.finished, self.spot(0, 0)), self.last + 1, self.twin)
+        both_here = self.rows(self.unit * (1 - self.seq), 2)
+        lone_here = self.rows(2 * self.unit * self.seq, 1)
+        for target, own, here in (
+            (self.shared.at[self.seq], self.both(), both_here),
+            (self.alone, self.lone(), lone_here),
+        ):
+            sources = [lambda at, own=own: self.own.at[self.z, self.x, own]]
+            sources += [
+                lambda at, steps=steps, here=here: self.from_z.at[steps, here]
+                for steps in range(self.depth - 1)
+            ]
+            add_slabs(1, lambda at, target=target: target, *sources)
+        self.last = 2 + self.depth
+        ends = lambda: (self.shared.at[self.seq], self.shared.at[self.seq])
+        self.send(ends, self.last, self.beside)
+        self.store(0).start()
+        self.send(lambda: (self.alone, self.spot(self.lone_out())), self.last + 1, self.beside)
+        self.send(lambda: (self.alone, self.spot(self.lone_out())), self.last + 2, self.twin)
+
+    def spot(self, first, count=1):
+        return self.target.at[self.rows(first, count), pl.ds(self.left, self.width)]
+
+    def lone_out(self, dy=0, dc=0):
+        seq = self.seq if dy == 0 else 1 - self.seq
+        replica = self.replica if dc == 0 else 1 - self.replica
+        return self.low + replica * self.half + 3 * self.unit * seq
+
+    def both_out(self, dc=0):
+        replica = self.replica if dc == 0 else 1 - self.replica
+        return self.low + replica * self.half + self.unit
+
+    def store(self, kind):
+        source = self.joint if kind else self.alone
+        target = self.spot(self.both_out(), 2) if kind else self.spot(self.lone_out())
+        return pltpu.make_async_copy(source, target, self.pool.local.at[self.number, 2 + kind])
 
     def hand_over(self):
-        if self.cut == 2:
-            self.wait(self.spot(1, 0), self.last)
-            self.send(lambda: (self.spot(1, 0), self.spot(1, 0)), self.last + 2, self.twin)
-        else:
-            for steps in range(1, self.span):
-                turn = (self.seq + self.span - steps) % self.span
-                self.wait(self.shared.at[turn], self.last + 2 + steps)
-            sources = [lambda at, turn=turn: self.shared.at[turn] for turn in range(self.span)]
-            add_slabs(1, lambda at: self.finished, *sources)
-            self.publish()
+        self.wait(self.spot(self.lone_out(1)), self.last + 1)
+        spot = lambda: self.spot(self.lone_out(1))
+        self.send(lambda: (spot(), spot()), self.last + 3, self.twin)
+        self.wait(self.shared.at[1 - self.seq], self.last)
+        sources = [lambda at, turn=turn: self.shared.at[turn] for turn in range(2)]
+        add_slabs(1, lambda at: self.joint, *sources)
+        self.store(1).start()
+        self.send(lambda: (self.joint, self.spot(self.both_out(), 2)), self.last + 4, self.twin)
 
     def close(self):
-        self.wait(self.spot(0, 1), self.last + 1)
-        if self.cut == 2:
-            self.wait(self.spot(1, 1), self.last + 2)
-        self.store().wait()
+        self.wait(self.spot(self.lone_out(0, 1)), self.last + 2)
+        self.wait(self.spot(self.lone_out(1, 1)), self.last + 3)
+        self.wait(self.spot(self.both_out(1), 2), self.last + 4)
+        self.store(0).wait()
+        self.store(1).wait()
         self.flush()
 
     def flush(self):
@@ -598,63 +600,58 @@
 
 
 class Pool:
-    def __init__(self, rows, width, plan, refs):
-        self.ring = Pool.slots()
-        self.rows, self.width, self.plan = (rows, width, plan)
-        self.total = len(plan)
-        self.pairs = sum(cut == 2 for cut in plan)
-        names = list(Pool.shapes(rows, width, plan))
+    ring = 7
+
+    def __init__(self, rows, width, total, kept, refs):
+        self.rows, self.width, self.total, self.kept = (rows, width, total, kept)
+        names = list(Pool.shapes(rows, width, total))
         for name, ref in zip(names, refs):
             setattr(self, name, ref)
         self.sends, self.recvs, self.local, self.credits = refs[len(names) :]
-        self.cuts, self.jobs, self.next = ({}, [], 0)
+        self.jobs = []
 
     @staticmethod
-    def slots():
-        return 6 if lax.axis_size("seq") == 2 else 4
+    def shapes(rows, width, total):
+        depth, ring = (depth_of(), Pool.ring)
+        unit = rows // 8
+        return {
+            "own": (ring, depth, 2, rows // 2, width),
+            "came": (ring, depth, 2, rows // 2, width),
+            "from_x": (ring, depth, 3 * unit, width),
+            "from_seq": (ring, depth, 2, unit, width),
+            "from_z": (total, depth - 1, 3 * unit, width),
+            "shared": (total, 2, 2 * unit, width),
+            "finished": (ring, 3 * unit, width),
+            "stage": (2, depth, 2, rows, width),
+        }
 
     @staticmethod
-    def shapes(rows, width, plan):
-        depth, span = (depth_of(), lax.axis_size("seq"))
-        ring = min(Pool.slots(), len(plan))
-        pairs = sum(cut == 2 for cut in plan)
-        shapes = {
-            "own": (ring, depth, 2, rows, width),
-            "came": (ring, depth, 2, rows // 2, width),
-            "from_x": (ring, depth, rows // 2, width),
-            "from_z": (len(plan), depth - 1, rows // 2, width),
-            "finished": (ring, rows // 2, width),
-        }
-        if pairs:
-            shapes["from_seq"] = (min(ring, pairs), depth, 2, rows // 4, width)
-        if pairs < len(plan):
-            shapes["shared"] = (len(plan) - pairs, span, rows // 2, width)
-        return shapes
-
-    @staticmethod
-    def scratch(rows, width, plan):
-        slots = 7 + depth_of() + lax.axis_size("seq")
-        shapes = Pool.shapes(rows, width, plan).values()
-        return [pltpu.VMEM(shape, jnp.bfloat16) for shape in shapes] + [
-            pltpu.SemaphoreType.DMA((len(plan), slots)),
-            pltpu.SemaphoreType.DMA((len(plan), slots)),
-            pltpu.SemaphoreType.DMA((len(plan), 3)),
+    def scratch(rows, width, total):
+        slots = 7 + depth_of()
+        return [pltpu.VMEM(shape, jnp.bfloat16) for shape in Pool.shapes(rows, width, total).values()] + [
+            pltpu.SemaphoreType.DMA((total, slots)),
+            pltpu.SemaphoreType.DMA((total, slots)),
+            pltpu.SemaphoreType.DMA((total, 4)),
             pltpu.SemaphoreType.REGULAR((3,)),
         ]
 
-    def add(self, target, low, left, source=None):
+    def add(self, target, low, left):
         number = len(self.jobs)
-        while number >= self.ring and self.jobs[number - self.ring].done_stages < 5:
-            self.pump()
-        job = Reduce(self, number, source, target, low, left, self.plan[number])
+        if number >= 2:
+            self.jobs[number - 2].await_kept()
+        job = Reduce(self, number, target, low, left)
         self.jobs.append(job)
         return job
 
+    def free(self, number):
+        return number < self.ring or self.jobs[number - self.ring].done_stages >= 5
+
     def pump(self):
-        active = [job for job in self.jobs if job.ready and 0 < job.done_stages < 7]
-        fresh = [job for job in self.jobs if job.ready and job.done_stages == 0]
-        for job in fresh[:1]:
-            job.step()
+        active = [job for job in self.jobs if 0 < job.done_stages < 7]
+        fresh = [job for job in self.jobs if job.done_stages == 0][:1]
+        for job in fresh:
+            if self.free(job.number):
+                job.step()
         for job in reversed(active):
             job.step()
 
@@ -724,17 +721,17 @@
 
 
 def gradient_into(job, left, right):
-    depth, _, rows, width = job.own.shape
+    depth, _, rows, width = job.stage.shape
 
     def step(z, carry):
         cols = pl.ds(pl.multiple_of(z * 2 * rows, 2 * rows), 2 * rows)
         value = tn(left[:, cols], right[...]).astype(jnp.bfloat16)
-        job.own[z, 0] = value[:rows]
-        job.own[z, 1] = value[rows:]
+        job.stage[z, 0] = value[:rows]
+        job.stage[z, 1] = value[rows:]
         return carry
 
     lax.fori_loop(0, depth, step, 0)
-    job.ready = True
+    job.keep().start()
 
 
 class Stream:
@@ -803,7 +800,8 @@
     ]
 
 
-def module_back(pool, pump, weights, saved, buffers, chunks, outs):
+def module_back(pool, weights, saved, buffers, chunks, outs, often):
+    pump = pool.pump
     entry, low, hidden, grad_hidden, total = buffers
     grad_in, grad_out = outs
     width = total.shape[1]
@@ -823,73 +821,173 @@
         row_blocks(width, 256, body)
         job = pool.add(grad_out, chunk * pool.rows, 0)
         gradient_into(job, hidden, low)
-        pump()
         job = pool.add(grad_in, 0, chunk * width)
         gradient_into(job, entry, grad_hidden)
-        pump()
+        if often:
+            pump()
         add_transposed(grad_hidden, weights.take(), total)
         pump()
-def late_back_kernel(settings, *refs):
-    plan, early, count, clips, rows, limit = settings
-    first_ref, table_ref, gains = refs[:3]
-    grad, x1, x0, u0, mixed, query, keys, values, a_out, qkv, w_in, w_out = refs[3:15]
-    refs = refs[15:]
-    sources, refs = (refs[:count], refs[count:])
-    grad_x, gain_sums, dt_ref, to_attn, to_q, to_k, to_v, to_out, to_in = refs[:9]
-    refs = refs[9:]
-    targets, refs = (refs[:count], refs[count:])
-    resid, total, resid_in, low, entry, mixed_grad, q_ref, dq_ref = refs[:8]
+def middle_rows(source, gain, grads, entry, sums, line):
+    sums[pl.ds(line, 1), :] = jnp.zeros_like(sums[pl.ds(line, 1), :])
+
+    def body(rows):
+        normal, inverse = norm_parts(source[rows, :])
+        middle = normal * gain
+        logistic = jax.nn.sigmoid(middle)
+        entry[rows, :] = (middle * logistic).astype(jnp.bfloat16)
+        grad = grads[rows, :] * (logistic + middle * logistic * (1.0 - logistic))
+        grad_normal = grad * gain
+        grads[rows, :] = inverse * (
+            grad_normal
+            - jnp.mean(grad_normal, -1, keepdims=True)
+            - normal * jnp.mean(grad_normal * normal, -1, keepdims=True)
+        )
+        sums[pl.ds(line, 1), :] += jnp.sum(grad * normal, 0, keepdims=True)
+
+    row_blocks(source.shape[0], 64, body)
+
+
+def depthwise_back(grads, taps, value, gate, grad_value, grad_gate, tap_sums, pump):
+    total, width = value.shape
+    tap_sums[...] = jnp.zeros_like(tap_sums)
+    for column in range(width // LANES):
+        lanes = pl.ds(column * LANES, LANES)
+
+        def body(at, carry):
+            first = pl.multiple_of(at * LANES, LANES)
+            rows = pl.ds(first, LANES)
+            held = value[rows, lanes].astype(jnp.float32)
+            opened = jax.nn.sigmoid(gate[rows, lanes].astype(jnp.float32))
+            glu = (held * opened).astype(jnp.bfloat16).astype(jnp.float32)
+            grad = jnp.zeros((LANES, LANES), jnp.float32)
+            window = grads[pl.ds(first, LANES + 32), lanes]
+            for tap in range(KERNEL):
+                ahead = KERNEL - 1 - tap
+                moved = window[ahead : ahead + LANES]
+                grad = grad + moved * taps[pl.ds(tap, 1), lanes]
+                tap_sums[pl.ds(tap, 1), lanes] += jnp.sum(glu * moved, 0, keepdims=True)
+            grad_value[rows, lanes] = (grad * opened).astype(jnp.bfloat16)
+            grad_gate[rows, lanes] = (grad * held * opened * (1.0 - opened)).astype(jnp.bfloat16)
+            return carry
+
+        lax.fori_loop(0, total // LANES, body, 0)
+        if column % 2:
+            pump()
+
+
+def fetch(source, target, sem):
+    copy = pltpu.make_async_copy(source, target, sem)
+    copy.start()
+    return copy
+
+
+def back_kernel(settings, *refs):
+    count, clips, rows, limit = settings
+    first_ref, table_ref, gains, taps = refs[:4]
+    cot, x4, x3, x2, x1, x0, u1, u0, joined, summed = refs[4:14]
+    mixed, query, keys, values, c_in, c_out, a_out, qkv = refs[14:22]
+    second_in, second_out, w_in, w_out = refs[22:26]
+    grad_x, gain_sums, dt_ref, tap_sums = refs[26:30]
+    to_second_out, to_second_in, to_conv_out, to_conv_in = refs[30:34]
+    to_attn, to_q, to_k, to_v, to_out, to_in, kept = refs[34:41]
+    refs = refs[41:]
+    resid, total_ext, resid_in, low, entry, mixed_grad, q_ref, dq_ref = refs[:8]
     k_ref, v_ref, dk_ref, dv_ref, later, earlier, dk_sum, dv_sum, slots = refs[8:17]
     local, slot_sems, saved_sems, halo_sems = refs[17:21]
-    width = total.shape[1]
+    width = resid.shape[1]
+    total = total_ext.at[pl.ds(0, rows)]
     groups = lax.axis_size("group")
     part = width // groups
     span = lax.axis_size("seq")
     chunks = w_out.shape[1]
     reduce_greet()
-    pool = Pool(part, width, plan, refs[21:])
+    pool = Pool(part, width, count, kept, refs[21:])
+    pump = pool.pump
+    copies = module_copies(second_in, second_out, groups)
+    copies += [lambda slot: [(c_out, slot)]]
+    copies += [
+        lambda slot, at=at: [(c_in.at[:, pl.ds(at * width, width)], slot)] for at in range(2)
+    ]
+    copies += [lambda slot: [(a_out, slot)]]
+    copies += [lambda slot, at=at: [(qkv.at[at], slot)] for at in range(3)]
+    copies += module_copies(w_in, w_out, groups)
+    load = fetch(x4, resid_in, local.at[0])
+    arrival = fetch(cot, low, local.at[1])
+    weights = Stream([slots.at[at] for at in range(3)], slot_sems, copies)
+    free = [ref.at[0, pl.ds(0, rows)] for ref in (k_ref, v_ref)]
+    saved = Stream(free, saved_sems, saved_copies(u1, groups, part))
+    halves = [ref.at[0, pl.ds(0, rows)] for ref in (dk_ref, dv_ref)]
+    opening = [
+        fetch(joined.at[:, pl.ds(at * width, width)], half, local.at[2 + at])
+        for at, half in enumerate(halves)
+    ]
+    resid[...] = jnp.zeros_like(resid)
+    arrival.wait()
+    load.wait()
+
+    def widen(at):
+        total[at, :] = low[at, :].astype(jnp.float32)
+
+    row_blocks(rows, 64, widen)
+    norm_back_rows(resid_in, gains[pl.ds(5, 1), :], total, resid, gain_sums, 5)
+    load = fetch(x3, resid_in, local.at[0])
+    cast_rows(resid, low, 0.5)
+    load.wait()
+    norm_rows(resid_in, gains[pl.ds(4, 1), :], entry)
+    buffers = (entry, low, mixed_grad, q_ref, total)
+    module_back(
+        pool, weights, saved, buffers, chunks, (to_second_in, to_second_out), False
+    )
+    norm_back_rows(resid_in, gains[pl.ds(4, 1), :], total, resid, gain_sums, 4)
+    load = fetch(summed, resid_in, local.at[0])
+    cast_rows(resid, low)
+    transposed_rows(low, weights.take(), total)
+    load.wait()
+    middle_rows(resid_in, gains[pl.ds(3, 1), :], total, entry, gain_sums, 3)
+    _, _, seq, _ = place()
+    halo = pltpu.make_async_remote_copy(
+        src_ref=total_ext.at[pl.ds(0, 32)],
+        dst_ref=total_ext.at[pl.ds(rows, 32)],
+        send_sem=halo_sems.at[0, 4],
+        recv_sem=halo_sems.at[1, 4],
+        device_id={"seq": (seq + span - 1) % span},
+        device_id_type=MESH,
+    )
+    halo.start()
+    load = fetch(x2, resid_in, local.at[0])
+    job = pool.add(to_conv_out, 0, 0)
+    gradient_into(job, entry, low)
+    pump()
+    for copy in opening:
+        copy.wait()
+    load.wait()
+    norm_rows(resid_in, gains[pl.ds(2, 1), :], entry)
+    halo.wait()
+    beyond = pl.ds(rows, 32)
+    nothing = jnp.zeros((32, width), jnp.float32)
+    total_ext[beyond, :] = jnp.where(seq < span - 1, total_ext[beyond, :], nothing)
+    depthwise_back(total_ext, taps, *halves, mixed_grad, q_ref, tap_sums, pump)
+    total[...] = jnp.zeros_like(total)
+    for at, flat in enumerate((mixed_grad, q_ref)):
+        job = pool.add(to_conv_in, 0, at * width)
+        gradient_into(job, entry, flat)
+        pump()
+        add_transposed(flat, weights.take(), total)
+        pump()
+    norm_back_rows(resid_in, gains[pl.ds(2, 1), :], total, resid, gain_sums, 2)
     loads = [
-        pltpu.make_async_copy(source, target, local.at[at])
+        fetch(source, target, local.at[at])
         for at, (source, target) in enumerate(
-            (
-                (grad, resid),
-                (mixed, entry),
-                (query, q_ref),
-                (keys, k_ref),
-                (values, v_ref),
-                (x1, resid_in),
-            )
+            ((mixed, entry), (query, q_ref), (keys, k_ref), (values, v_ref), (x1, resid_in))
         )
     ]
-    for load in loads:
-        load.start()
-    copies = [lambda slot: [(a_out, slot)]]
-    copies += [lambda slot, at=at: [(qkv.at[at], slot)] for at in range(3)]
-    copies += module_copies(w_in, w_out, groups)
-    weights = Stream([slots.at[at] for at in range(3)], slot_sems, copies)
-    waiting = list(early)
-
-    def feed():
-        number = len(pool.jobs)
-        free = number < pool.ring or pool.jobs[number - pool.ring].done_stages >= 5
-        if waiting and free and not any(job.done_stages == 0 for job in pool.jobs):
-            source, low_row, left = waiting.pop(0)
-            pool.add(targets[source], low_row, left, sources[source])
-
-    def pump():
-        feed()
-        pool.pump()
-
-    pump()
+    cast_rows(resid, low)
+    transposed_rows(low, weights.take(), mixed_grad)
     loads[0].wait()
-    cast_rows(resid, low)
-    loads[1].wait()
     job = pool.add(to_attn, 0, 0)
     gradient_into(job, entry, low)
     pump()
-    transposed_rows(low, weights.take(), mixed_grad)
-    pump()
-    for load in loads[2:]:
+    for load in loads[1:]:
         load.wait()
     table = table_ref[...]
     zero = jnp.zeros((BLOCK, LANES), jnp.bfloat16)
@@ -930,13 +1028,11 @@
             dq_ref[here, lanes] = (both * HEAD_DIM**-0.5).astype(jnp.bfloat16)
             return carry
 
-        lax.fori_loop(0, clips * blocks, attend_block, 0)
+        lax.fori_loop(0, clips * blocks, attend_block, 0, unroll=2)
         dk_ref[:, :, lanes] = (dk_sum[...] * HEAD_DIM**-0.5).astype(jnp.bfloat16)
         dv_ref[:, :, lanes] = dv_sum[...].astype(jnp.bfloat16)
         pump()
 
-    _, _, seq, _ = place()
-    free = [ref.at[0, pl.ds(0, rows)] for ref in (k_ref, v_ref)]
     saved = Stream(free, saved_sems, saved_copies(u0, groups, part))
     edges = []
     for at, ref in enumerate((dk_ref, dv_ref)):
@@ -990,9 +1086,7 @@
     gain = gains[pl.ds(0, 1), :]
     norm_rows(dq_ref, gain, entry)
     buffers = (entry, low, mixed_grad, q_ref, total)
-    module_back(pool, pump, weights, saved, buffers, chunks, (to_in, to_out))
-    while waiting:
-        pump()
+    module_back(pool, weights, saved, buffers, chunks, (to_in, to_out), True)
     norm_back_rows(dq_ref, gain, total, resid, gain_sums, 0)
     cast_rows(resid, low)
     store = pltpu.make_async_copy(low, grad_x, local.at[1])
@@ -1001,20 +1095,6 @@
     store.wait()
 
 
-def reduce_views(grads):
-    groups = lax.axis_size("group")
-    return [grad.reshape(groups // 2, 2, grad.shape[0] // groups, grad.shape[1]) for grad in grads]
-
-
-def early_list(views, rows, width):
-    return [
-        (source, low, left)
-        for source, view in enumerate(views)
-        for low in range(0, view.shape[2], rows)
-        for left in range(0, view.shape[3], width)
-    ]
-
-
 def reduce_greet():
     deep, across, _, twin = neighbours()
     span = lax.axis_size("seq")
@@ -1022,26 +1102,23 @@
     greet(deep + [across, twin] + [{"seq": (seq + steps) % span} for steps in range(1, span)])
 
 
-def late_back(grad, x1, x0, u0, kept, table, gains, weights, grads, rows, halve):
+def back(cot, resids, saved, kept, table, gains, taps, weights, rows):
+    joined, summed, u1, u0 = saved
     query, keys, values, mixed = kept
-    a_out, qkv, w_in, w_out = weights
+    c_in, c_out, a_out, qkv, second_in, second_out, w_in, w_out = weights
     clips, ext, width = keys.shape
-    flat = clips * rows
     groups = lax.axis_size("group")
     part = width // groups
     chunks = w_out.shape[0] // width
-    views = reduce_views(grads)
-    early = early_list(views, part, width)
-    count = len(early) + 4 + 2 * chunks
-    plan = [2 if halve and at % 2 == 0 else 1 for at in range(count)]
+    count = 7 + 4 * chunks
     first = lax.axis_index("seq").astype(jnp.int32)[None] * rows
     limit = rows * lax.axis_size("seq")
     hbm = pl.BlockSpec(memory_space=pl.ANY)
     vmem = pl.BlockSpec(memory_space=pltpu.VMEM)
     low = lambda *shape: jax.ShapeDtypeStruct(shape, jnp.bfloat16)
     wide = lambda *shape: jax.ShapeDtypeStruct(shape, jnp.float32)
-    holds = [pltpu.VMEM((flat, width), jnp.float32)] * 3
-    holds += [pltpu.VMEM((flat, width), jnp.bfloat16)] * 5
+    holds = [pltpu.VMEM((rows + more, width), jnp.float32) for more in (0, 32, 0)]
+    holds += [pltpu.VMEM((rows, width), jnp.bfloat16)] * 5
     holds += [pltpu.VMEM((clips, ext, width), jnp.bfloat16)] * 4
     holds += [
         pltpu.VMEM((2, clips, LEFT, width), jnp.bfloat16),
@@ -1052,42 +1129,51 @@
         pltpu.SemaphoreType.DMA((6,)),
         pltpu.SemaphoreType.DMA((3, groups)),
         pltpu.SemaphoreType.DMA((2, groups)),
-        pltpu.SemaphoreType.DMA((2, 4)),
+        pltpu.SemaphoreType.DMA((2, 5)),
     ]
+    grad_out = low(chunks * part, width)
+    grad_in = low(part, chunks * width)
+    by_chunk = lambda weight: weight.reshape(groups, chunks, part, width)
     results = pl.pallas_call(
-        functools.partial(late_back_kernel, (plan, early, len(views), clips, rows, limit)),
-        in_specs=[pl.BlockSpec(memory_space=pltpu.SMEM), vmem, vmem] + [hbm] * (12 + len(views)),
-        out_specs=[hbm, vmem, vmem] + [hbm] * (6 + len(views)),
-        out_shape=[low(flat, width), wide(8, width), wide(SPAN, LANES)]
+        functools.partial(back_kernel, (count, clips, rows, limit)),
+        in_specs=[pl.BlockSpec(memory_space=pltpu.SMEM)] + [vmem] * 3 + [hbm] * 22,
+        out_specs=[hbm] + [vmem] * 3 + [hbm] * 11,
+        out_shape=[low(rows, width), wide(8, width), wide(SPAN, LANES), wide(32, width)]
+        + [grad_out, grad_in, low(part, width), low(part, 2 * width)]
         + [low(part, width)] * 4
-        + [low(chunks * part, width), low(part, chunks * width)]
-        + [low(*view.shape[2:]) for view in views],
-        scratch_shapes=holds + Pool.scratch(part, width, plan),
+        + [grad_out, grad_in, low(count, groups // 2, 2, part, width)],
+        scratch_shapes=holds + Pool.scratch(part, width, count),
         compiler_params=pltpu.CompilerParams(
-            collective_id=3, has_side_effects=True, vmem_limit_bytes=62 << 20
+            collective_id=3, has_side_effects=True, vmem_limit_bytes=63 << 20
         ),
-        name="late_back",
+        name="back",
     )(
         first,
         wide_table(table),
         gains,
-        grad,
-        x1,
-        x0,
+        taps,
+        cot,
+        *resids,
+        u1,
         u0,
+        joined,
+        summed,
         mixed,
-        query.reshape(flat, width),
+        query.reshape(rows, width),
         keys,
         values,
+        c_in,
+        c_out,
         a_out,
         qkv,
+        second_in,
+        by_chunk(second_out),
         w_in,
-        w_out.reshape(groups, chunks, part, width),
-        *views,
-    )
-    grad_x, gain_sums, dt = results[:3]
+        by_chunk(w_out),
+    )
+    grad_x, gain_sums, dt, tap_sums = results[:4]
     dt = (dt[:WIN, :HEAD_DIM] + dt[:WIN, HEAD_DIM:]) * HEAD_DIM**-0.5
-    return grad_x, gain_sums, dt, results[3:9], results[9:]
+    return grad_x, gain_sums, dt, tap_sums, results[4:]
 
 
 def unmix(grad, groups):
@@ -1185,7 +1271,7 @@
         mid_inverse,
         swished,
     )
-    return (matmul(swished, conv_out), kept)
+    return (matmul(swished, conv_out), summed.reshape(clips * rows, width), kept)
 
 
 def conv_back(grad_branch, kept, gain_in, gain_mid, conv_in, depthwise, conv_out, shape):
@@ -1248,19 +1334,18 @@
     small = jnp.concatenate([gains, depthwise], 0)
     small = jnp.pad(small, ((0, lines - norms - taps), (0, 0)))[None]
     shards = (small, ffn_in, ffn_out, qkv, attn_out[None], conv_in[None], conv_out[None])
-    cut = 2 if halve else 1
-    plan = (
-        (0, (0, 1), 0, 1),
-        (1, (0, 1), cut, 2),
-        (2, (0, 1), cut, 2),
-        (3, (0, 3), 1, 1),
-        (4, (0, 1), 1, 1),
-        (5, (0, 1), 1, 1),
-        (6, (0, 1), 1, 1),
-        (1, (1, 1), cut, 2),
-        (2, (1, 1), cut, 2),
-    )
-    gathered = gather_weights(shards, plan)
+    sources = (
+        (0, 0, 1),
+        (1, 0, 1),
+        (2, 0, 1),
+        (3, 0, 3),
+        (4, 0, 1),
+        (5, 0, 1),
+        (6, 0, 1),
+        (1, 1, 1),
+        (2, 1, 1),
+    )
+    gathered = gather_weights(shards, sources, halve)
     small = gathered[0].reshape(-1, lines, gains.shape[1]).transpose(1, 0, 2).reshape(lines, width)
     gain_f = small[:norms].astype(jnp.float32)
     depth = small[norms : norms + taps]
@@ -1274,7 +1359,7 @@
         after_first, gain_f[1], proj, a_out, rel_table, shape
     )
     after_attn = after_first + attn_branch
-    conv_branch, conv_kept = conv_forward(
+    conv_branch, summed, conv_kept = conv_forward(
         after_attn, gain_f[2], gain_f[3], c_in, depth, c_out, shape
     )
     after_conv = after_attn + conv_branch
@@ -1287,36 +1372,41 @@
             for member in (final, first_branch, attn_branch, conv_branch, second_branch)
         ]
     )
-    grad = cotangent.reshape(flat_rows, width).astype(jnp.float32)
-    grad, grad_gain_final = norm_backward(grad, final_normal, final_inverse, gain_f[5])
-    back_in, grad_gain_second, grad_in_second, grad_out_second = feed_back(
-        0.5 * grad, second_kept, gain_f[4], f_in[1], f_out[1]
-    )
-    grad = grad + back_in
-    back_in, grad_gain_conv, grad_gain_mid, grad_conv_in, grad_taps, grad_conv_out = conv_back(
-        grad, conv_kept, gain_f[2], gain_f[3], c_in, depth, c_out, shape
-    )
-    grad = grad + back_in
     if halve and clips == 1 and gains.shape[1] % LANES == 0:
-        early = [grad_out_second, grad_in_second, grad_conv_out, grad_conv_in]
-        grad, gain_sums, grad_table, mine, early = late_back(
-            grad,
-            after_first,
-            tokens.reshape(flat_rows, width),
-            first_kept[3].astype(jnp.bfloat16),
+        grad, gain_sums, grad_table, grad_taps, shares = back(
+            cotangent.reshape(flat_rows, width),
+            (final, after_conv, after_attn, after_first, tokens.reshape(flat_rows, width)),
+            (
+                conv_kept[3].astype(jnp.bfloat16),
+                summed,
+                second_kept[3].astype(jnp.bfloat16),
+                first_kept[3].astype(jnp.bfloat16),
+            ),
             attn_kept[3:],
             rel_table,
             small[:8].astype(jnp.float32),
-            (a_out, proj, f_in[0], f_out[0]),
-            early,
+            jnp.pad(depth.astype(jnp.float32), ((0, 32 - taps), (0, 0))),
+            (c_in, c_out, a_out, proj, f_in[1], f_out[1], f_in[0], f_out[0]),
             rows,
-            halve,
         )
-        grad_gain_first, grad_gain_attn = (gain_sums[0], gain_sums[1])
-        grad_attn_out, grad_out_first = (mine[0], mine[4])
-        grad_qkv, grad_in_first = (mine[1:4], unmix(mine[5], lax.axis_size("group")))
-        grad_out_second, grad_in_second, grad_conv_out, grad_conv_in = early
+        gain_grads = gain_sums[:norms]
+        grad_taps = grad_taps[:taps]
+        groups = lax.axis_size("group")
+        grad_in_first, grad_in_second = (unmix(shares[9], groups), unmix(shares[1], groups))
+        grad_out_first, grad_out_second = (shares[8], shares[0])
+        grad_conv_out, grad_conv_in, grad_attn_out = shares[2:5]
+        grad_qkv = shares[5:8]
     else:
+        grad = cotangent.reshape(flat_rows, width).astype(jnp.float32)
+        grad, grad_gain_final = norm_backward(grad, final_normal, final_inverse, gain_f[5])
+        back_in, grad_gain_second, grad_in_second, grad_out_second = feed_back(
+            0.5 * grad, second_kept, gain_f[4], f_in[1], f_out[1]
+        )
+        grad = grad + back_in
+        back_in, grad_gain_conv, grad_gain_mid, grad_conv_in, grad_taps, grad_conv_out = conv_back(
+            grad, conv_kept, gain_f[2], gain_f[3], c_in, depth, c_out, shape
+        )
+        grad = grad + back_in
         back_in, grad_gain_attn, grad_qkv, grad_attn_out, grad_table = attention_back(
             grad, attn_kept, gain_f[1], proj, a_out, rel_table, shape
         )
@@ -1334,16 +1424,16 @@
         grad_in_first, grad_in_second, grad_out_first, grad_out_second = matrices[:4]
         grad_attn_out, grad_conv_in, grad_conv_out = matrices[4:7]
         grad_qkv = matrices[7:]
-    gain_grads = jnp.stack(
-        [
-            grad_gain_first,
-            grad_gain_attn,
-            grad_gain_conv,
-            grad_gain_mid,
-            grad_gain_second,
-            grad_gain_final,
-        ]
-    )
+        gain_grads = jnp.stack(
+            [
+                grad_gain_first,
+                grad_gain_attn,
+                grad_gain_conv,
+                grad_gain_mid,
+                grad_gain_second,
+                grad_gain_final,
+            ]
+        )
     loose = jnp.concatenate([grad_table.reshape(-1), squares])
     lines = -(-loose.shape[0] // width)
     loose = jnp.pad(loose, (0, lines * width - loose.shape[0])).reshape(lines, width)

time: 818 us -> 766 us (0.936)
  Pallas kernels: 541 us -> 599 us
  matrix products: 104 us -> 52.5 us
  other arithmetic: 87.5 us -> 41.2 us
    pallas_call x2, Pallas kernels: 517 us -> 575 us  [the longest x1 363 us: back(): pl.pallas_call(functools.partial(back_kernel, (count, clips, rows, limit)...]
    dot_general x8 -> x0, matrix products: 53.9 us -> none  [the longest x4 27.1 us: matmul_right_t(): lax.dot_general(left, right, (((1,), (1,)), ((), ())), preferred_element_...]
    add x3 -> x0, other arithmetic: 23.5 us -> none  [the longest x1 18.7 us: conv_back(): grad_padded + jnp.pad(grad_summed * taps[tap], ((0, 0), (tap, KERNEL - 1...]
    mul x3 -> x1, other arithmetic: 18.8 us -> 0.97 us  [back(): dt = (dt[:WIN, :HEAD_DIM] + dt[:WIN, HEAD_DIM:]) * HEAD_DIM ** (-0.5)]
    reduce_sum x3 -> x1, other arithmetic: 12.4 us -> 2.85 us  [on_device(): jnp.sum(member * member)]
    ppermute x6 -> x5, starting transfers between devices: 18.1 us -> 13.6 us  [from_behind(): lax.ppermute(value, axis, [(source, source + steps) for source in range(i...]
  transfers between devices with their start and end apart: 11 -> 10, of which waited for: 7 -> 6; matrix products, arithmetic and copies ran while one was open for 2% -> 3% of each run, Pallas kernels for 0% -> 0%
where the time goes in v4:
time: 766 us; the launch traced here: 757 us
  Pallas kernels  599 us (78%)
  matrix products  52.5 us (7%)
  other arithmetic  41.2 us (5%)
  local copies, waits for them, and re-layouts  27.3 us (4%)
  starting transfers between devices  21.6 us (3%)
  waiting for transfers between devices  13.4 us (2%)
    pallas_call x1, Pallas kernels, back(): pl.pallas_call(functools.partial(back_kernel, (count, clips, rows, limit)...  363 us
    pallas_call x1, Pallas kernels, gather_weights(): pl.pallas_call(functools.partial(gather_kernel, plan, [(source, first) fo...  211 us
    dot_general x10, matrix products, matmul(): return jnp.dot(left, right, preferred_element_type=jnp.float32)  52.5 us
    pallas_call x1, Pallas kernels, attend(): pl.pallas_call(functools.partial(attend_kernel, limit), grid=grid, in_spe...  24.5 us
    reduce_sum x2, other arithmetic, norm_forward(): centered = values - jnp.mean(values, -1, keepdims=True)  18.7 us
  transfers between devices with their start and end apart: 10, of which 6 were waited for; matrix products, arithmetic and copies ran while one was open for 3% of the time, Pallas kernels for 0%

profile of v4, /device:TPU:0, one launch (start us, length us, event | category | flops | bytes accessed | tf_op | source)
XLA Modules:
  0.0 756.9 jit_solution(16413664833431232748)
XLA Ops:
  8.6 211.5 %gather_weights.1 = (bf16[1,384,128]{2,1,0:T(8,128)(2,1)S(1)}, bf16[1,1024,4096]{2,1,0:T(8,128)(2,1)S(1)}, bf16[1,4096,1024]{2,1,0:T(8,128)(2,1)}, bf16[3,1024,1...) custom-call(bf16[1,48,128]{2,1,0:T(8,128)(2,1)S(1)} %fusion.91.refs_, ...), custom_call_target="tpu_custom_call" | custom-call | tf_op jit(solution)/shard_map/gather_weights/pallas_call | solution.py:346
  221.6 8.5 %fusion.111 = (bf16[512,4096]{1,0:T(8,128)(2,1)}, f32[512,4096]{1,0:T(8,128)}) fusion(bf16[1,1024,4096]{2,1,0:T(8,128)(2,1)S(1)} %get-tuple-element.36, bf16[1,512,1024]{2,1,0:T(8,128)(2,1)S(1)} %copy-done.16, f32[1024]{0:T(1024)S(1)} %get-tuple-element.122, f32[512]{0:T(512)S(1)} %add_rsqrt_fusion.5, f32[512]{0:T(512)S(1)} %broadcast_multiply_fusion.5), kind=kOutput, calls=%fused_computation.218 | convolution fusion | flops 4299685888 | bytes 22028288 | tf_op jit(solution)/shard_map/dot_general | solution.py:53
  230.1 11.3 %fusion.109 = (f32[512]{0:T(512)S(1)}, f32[512,1024]{1,0:T(8,128)S(1)}, f32[]{:T(128)}) fusion(bf16[1,512,1024]{2,1,0:T(8,128)(2,1)S(1)} %copy-done.16, bf16[1,4096,1024]{2,1,0:T(8,128)(2,1)} %get-tuple-element.37, f32[512,4096]{1,0:T(8,128)} %get-tuple-element.128), kind=kOutput, calls=%fused_computation.216 | convolution fusion | flops 4308598272 | bytes 19924996 | tf_op jit(solution)/shard_map/dot_general | solution.py:53
  250.5 5.2 collective-permute-start.2
  257.8 2.2 fusion.52.refs_15_
  262.3 3.3 maximum_maximum_fusion.1
  265.6 24.5 %attend.1 = bf16[1,512,1024]{2,1,0:T(8,128)(2,1)} custom-call(s32[1]{0:T(128)} %bitcast.11.first_ref.refs_0_, bf16[1,512,1024]{2,1,0:T(8,128)(2,1)} %bitcast.225, bf16[1,640,1024]{2,1,0:T(8,128)(2,1)} %get-tuple-element.124.k_ref.refs_16_, bf16[1,640,1024]{2,1,0:T(8,128)(2,1)} %get-tuple-element.123.v_ref.refs_17_, bf16[256,128]{1,0:T(8,128)(2,1)} %copy.29.t_ref.refs_1_), custom_call_target="tpu_custom_call" | custom-call | tf_op jit(solution)/shard_map/attend/pallas_call | solution.py:153
  290.1 4.1 fusion.108
  294.9 3.8 fusion.112
  299.3 3.8 collective-permute-start.4
  305.4 18.5 %fusion.106 = (f32[512]{0:T(512)S(1)}, f32[1,512,1024]{2,1,0:T(8,128)S(1)}) fusion(f32[1,542,1024]{2,1,0:T(8,128)S(1)} %maximum_convert_fusion.2, f32[1024]{0:T(1024)S(1)} %get-tuple-element.87, f32[1024]{0:T(1024)S(1)} %get-tuple-element.88, f32[1024]{0:T(1024)S(1)} %get-tuple-element.89, f32[1024]{0:T(1024)S(1)} %get-tuple-element.90, ...), kind=kLoop, calls=%fused_computation.214 | loop fusion | flops 32505344 | bytes 67237888 | tf_op jit(solution)/shard_map/reduce_sum | solution.py:35
  324.3 1.9 copy-done.8
  326.2 2.3 fusion.105
  330.3 7.7 %fusion.110 = (bf16[512,4096]{1,0:T(8,128)(2,1)}, f32[512,4096]{1,0:T(8,128)}) fusion(bf16[1,1024,4096]{2,1,0:T(8,128)(2,1)S(1)} %bitcast.221, f32[512,1024]{1,0:T(8,128)S(1)} %get-tuple-element.75.refs_6_, f32[1024]{0:T(1024)S(1)} %copy-done.45, f32[512]{0:T(512)S(1)} %add_rsqrt_fusion.1, f32[512]{0:T(512)S(1)} %broadcast_multiply_fusion.1), kind=kOutput, calls=%fused_computation.217 | convolution fusion | flops 4299161600 | bytes 23076864 | tf_op jit(solution)/shard_map/dot_general | solution.py:53
  338.1 10.0 %fusion.104 = (f32[512]{0:T(512)S(1)}, f32[512,1024]{1,0:T(8,128)}, f32[]{:T(128)}) fusion(f32[512,1024]{1,0:T(8,128)S(1)} %get-tuple-element.75.refs_6_, bf16[1,4096,1024]{2,1,0:T(8,128)(2,1)S(1)} %bitcast.224, f32[512,4096]{1,0:T(8,128)} %get-tuple-element.126), kind=kOutput, calls=%fused_computation.212 | convolution fusion | flops 4308073984 | bytes 20973572 | tf_op jit(solution)/shard_map/dot_general | solution.py:53
  348.1 363.1 %back.1 = (bf16[512,1024]{1,0:T(8,128)(2,1)}, f32[8,1024]{1,0:T(8,128)}, f32[256,128]{1,0:T(8,128)}, f32[32,1024]{1,0:T(8,128)}, bf16[512,1024]{1,0:T(8,128)(2,1...) custom-call(s32[1]{0:T(128)} %bitcast.11.first_ref.refs_0_, ...), custom_call_target="tpu_custom_call" | custom-call | tf_op jit(solution)/shard_map/back/pallas_call | solution.py:1137
  712.3 2.9 multiply_reduce_fusion.4
  715.2 3.3 concatenate.30
  723.0 2.5 collective-permute-start.6
  725.5 2.3 maximum_convert_fusion
  727.8 2.9 collective-permute-done.6
  732.0 5.3 collective-permute-done.7
  740.5 2.5 collective-permute-done.8
  745.0 2.3 maximum_convert_fusion.1
  (194 shorter events, 49.2 us)
Async XLA Ops:
  8.6 212.3 %copy-start.16 = (bf16[1,512,1024]{2,1,0:T(8,128)(2,1)S(1)}, bf16[1,512,1024]{2,1,0:T(8,128)(2,1)}, u32[]{:S(2)}) copy-start(bf16[1,512,1024]{2,1,0:T(8,128)(2,1)} %param.11) | copy-start | bytes 3145732
  220.1 10.0 %copy-start = (bf16[1,1024,4096]{2,1,0:T(8,128)(2,1)}, bf16[1,1024,4096]{2,1,0:T(8,128)(2,1)S(1)}, u32[]{:S(2)}) copy-start(bf16[1,1024,4096]{2,1,0:T(8,128)(2,1)S(1)} %get-tuple-element.36) | copy-start | bytes 25165828
  220.1 10.0 %copy-start.2 = (bf16[1,1024,2048]{2,1,0:T(8,128)(2,1)}, bf16[1,1024,2048]{2,1,0:T(8,128)(2,1)S(1)}, u32[]{:S(2)}) copy-start(bf16[1,1024,2048]{2,1,0:T(8,128)(2,1)S(1)} %get-tuple-element.40) | copy-start | bytes 12582916
  220.1 10.0 %copy-start.7 = (bf16[1,1024,1024]{2,1,0:T(8,128)(2,1)}, bf16[1,1024,1024]{2,1,0:T(8,128)(2,1)S(1)}, u32[]{:S(2)}) copy-start(bf16[1,1024,1024]{2,1,0:T(8,128)(2,1)S(1)} %get-tuple-element.41) | copy-start | bytes 6291460
  220.1 37.6 %copy-start.1 = (bf16[3,1024,1024]{2,1,0:T(8,128)(2,1)}, bf16[3,1024,1024]{2,1,0:T(8,128)(2,1)S(1)}, u32[]{:S(2)}) copy-start(bf16[3,1024,1024]{2,1,0:T(8,128)(2,1)S(1)} %get-tuple-element.38.refs_21_) | copy-start | bytes 18874372
  220.1 70.0 %copy-start.6 = (bf16[1,1024,1024]{2,1,0:T(8,128)(2,1)}, bf16[1,1024,1024]{2,1,0:T(8,128)(2,1)S(1)}, u32[]{:S(2)}) copy-start(bf16[1,1024,1024]{2,1,0:T(8,128)(2,1)S(1)} %get-tuple-element.39) | copy-start | bytes 6291460
  244.7 17.6 %collective-permute-start = (bf16[1,64,1024]{2,1,0:T(8,128)(2,1)}, bf16[1,64,1024]{2,1,0:T(8,128)(2,1)}, u32[]{:S(2)}, u32[]{:S(2)}) collective-permute-start(bf16[1,64,1024]{2,1,0:T(8,128)(2,1)} %slice.411), channel_id=1, source_target_pairs={{0,16},{1,17},{2,18},{3,19},{4,20},{5,21},{6,22},{7,23},{8,24},{9,... | collective-permute-start | bytes 393224 | tf_op jit(solution)/shard_map/ppermute | solution.py:31
  247.3 14.3 %collective-permute-start.1 = (bf16[1,8,1024]{2,1,0:T(8,128)(2,1)}, bf16[1,8,1024]{2,1,0:T(8,128)(2,1)S(1)}, u32[]{:S(2)}, u32[]{:S(2)}) collective-permute-start(bf16[1,8,1024]{2,1,0:T(8,128)(2,1)} %slice.412), channel_id=1, source_target_pairs={{16,0},{17,1},{18,2},{19,3},{20,4},{21,5},{22,6},{23,7},{24,8},{25... | collective-permute-start | bytes 49160 | tf_op jit(solution)/shard_map/ppermute | solution.py:31
  249.8 10.2 %copy-start.19 = (bf16[1,512,1024]{2,1,0:T(8,128)(2,1)}, bf16[1,512,1024]{2,1,0:T(8,128)(2,1)S(1)}, u32[]{:S(2)}) copy-start(bf16[1,512,1024]{2,1,0:T(8,128)(2,1)S(1)} %fusion.61) | copy-start | bytes 3145732
  250.5 11.8 %collective-permute-start.2 = (bf16[1,64,1024]{2,1,0:T(8,128)(2,1)}, bf16[1,64,1024]{2,1,0:T(8,128)(2,1)}, u32[]{:S(2)}, u32[]{:S(2)}) collective-permute-start(bf16[1,64,1024]{2,1,0:T(8,128)(2,1)} %slice.413), channel_id=1, source_target_pairs={{0,16},{1,17},{2,18},{3,19},{4,20},{5,21},{6,22},{7,23},{8,24},{9,... | collective-permute-start | bytes 393224 | tf_op jit(solution)/shard_map/ppermute | solution.py:31
  256.3 6.0 collective-permute-start.3
  294.2 30.1 %copy-start.17 = (f32[512,1024]{1,0:T(8,128)}, f32[512,1024]{1,0:T(8,128)S(1)}, u32[]{:S(2)}) copy-start(f32[512,1024]{1,0:T(8,128)S(1)} %get-tuple-element.79.refs_7_) | copy-start | bytes 6291460
  299.3 5.7 collective-permute-start.4
  326.2 11.8 %slice-start.2 = ((s8[8388608]{0:T(1024)(128)(4,1)}), s8[4194304]{0:T(1024)(128)(4,1)S(1)}, s32[]{:S(2)}) async-start(s8[8388608]{0:T(1024)(128)(4,1)} %bitcast.223), calls=%async_computation.2 | async-start | bytes 8388608
  328.6 9.5 %copy-start.18 = (f32[512,1024]{1,0:T(8,128)}, f32[512,1024]{1,0:T(8,128)S(1)}, u32[]{:S(2)}) copy-start(f32[512,1024]{1,0:T(8,128)S(1)} %get-tuple-element.75.refs_6_) | copy-start | bytes 6291460
  328.6 9.5 %slice-start.3 = ((s8[8388608]{0:T(1024)(128)(4,1)}), s8[4194304]{0:T(1024)(128)(4,1)S(1)}, s32[]{:S(2)}) async-start(s8[8388608]{0:T(1024)(128)(4,1)} %bitcast.223), calls=%async_computation.3 | async-start | bytes 8388608
  718.6 3.5 collective-permute-start.5
  723.0 7.7 %collective-permute-start.6 = (f32[42,1024]{1,0:T(8,128)S(1)}, f32[42,1024]{1,0:T(8,128)S(1)}, u32[]{:S(2)}, u32[]{:S(2)}) collective-permute-start(f32[42,1024]{1,0:T(8,128)S(1)} %fusion.103), channel_id=1, source_target_pairs={{0,16},{16,0},{1,17},{17,1},{2,18},{18,2},{3,19},{19,3},{4,20},{20... | collective-permute-start | bytes 516104 | tf_op jit(solution)/shard_map/ppermute | solution.py:372
  725.5 13.7 %copy-start.15 = (f32[512,1024]{1,0:T(8,128)S(1)}, f32[512,1024]{1,0:T(8,128)}, u32[]{:S(2)}) copy-start(f32[512,1024]{1,0:T(8,128)} %get-tuple-element.73.refs_5_) | copy-start | bytes 6291460
  730.8 6.5 collective-permute-start.7
  732.0 13.0 %copy-start.23 = (bf16[512,1024]{1,0:T(8,128)(2,1)S(1)}, bf16[512,1024]{1,0:T(8,128)(2,1)}, u32[]{:S(2)}) copy-start(bf16[512,1024]{1,0:T(8,128)(2,1)} %get-tuple-element.48) | copy-start | bytes 3145732
  732.0 13.0 %copy-start.24 = (bf16[512,1024]{1,0:T(8,128)(2,1)S(1)}, bf16[512,1024]{1,0:T(8,128)(2,1)}, u32[]{:S(2)}) copy-start(bf16[512,1024]{1,0:T(8,128)(2,1)} %get-tuple-element.47) | copy-start | bytes 3145732
  737.3 5.7 collective-permute-start.8
  743.1 9.7 %collective-permute-start.9 = (f32[42,1024]{1,0:T(8,128)S(1)}, f32[42,1024]{1,0:T(8,128)S(1)}, u32[]{:S(2)}, u32[]{:S(2)}) collective-permute-start(f32[42,1024]{1,0:T(8,128)S(1)} %add.240), channel_id=1, source_target_pairs={{0,8},{2,10},{4,12},{6,14},{8,0},{10,2},{12,4},{14,6},{1,9},{3,11}... | collective-permute-start | bytes 516104 | tf_op jit(solution)/shard_map/ppermute | solution.py:372
  (38 other events, 106.4 us)

commit v5 on v4

--- a/solution.py
+++ b/solution.py
@@ -284,9 +284,43 @@
             copy.wait_send()
 
 
-def gather_kernel(plan, sources, count, *refs):
-    ins, outs = (refs[:count], refs[count : count + len(sources)])
-    helds, (sends, recvs, local) = (refs[count + len(sources) : -3], refs[-3:])
+class Ticker:
+    def __init__(self, jobs, numbers, stores, loads):
+        self.jobs, self.numbers, self.stores, self.loads = (jobs, numbers, stores, loads)
+        self.tick, self.stored, self.loaded = (0, set(), set())
+
+    def advance(self):
+        names = ("open", "forward_deep", "forward_across", "forward_beside", "close")
+        if self.tick >= len(self.jobs) + 8:
+            return
+        for lag, name in enumerate(names):
+            if 0 <= self.tick - 2 * lag < len(self.jobs):
+                getattr(self.jobs[self.tick - 2 * lag], name)()
+        if self.tick < len(self.stores):
+            source, store = self.stores[self.tick]
+            if source not in self.loaded:
+                self.loads[source].wait()
+                self.loaded.add(source)
+            store.start()
+        self.tick += 1
+
+    def until(self, number):
+        last = max(at for at, owner in enumerate(self.numbers) if owner == number)
+        while self.tick <= max(last + 8, number):
+            self.advance()
+        if number not in self.stored:
+            self.stores[number][1].wait()
+            self.stored.add(number)
+
+    def finish(self):
+        while self.tick < len(self.jobs) + 8:
+            self.advance()
+        for number in range(len(self.stores)):
+            self.until(number)
+
+
+def gather_ticker(plan, sources, ins, outs, helds, sems):
+    sends, recvs, local = sems
     deep, across, beside, twin = neighbours()
     peers = deep + [across, twin]
     if any(member[-1] == 2 for member in plan):
@@ -306,32 +340,289 @@
         jobs.append(Gather(ref, target, cut, low, left, rows, size, sends, recvs, at))
         at += (2, 6, 8)[cut] * depth_of()
     z, x, _, _ = place()
-    ready, stores = (set(), [])
-    for tick in range(len(jobs) + 8):
-        for lag, name in enumerate(
-            ("open", "forward_deep", "forward_across", "forward_beside", "close")
+    stores = []
+    for number, (source, first) in enumerate(sources):
+        rows = ins[source].shape[1]
+        start = pl.multiple_of((z * 2 + x) * rows, rows)
+        store = pltpu.make_async_copy(
+            helds[source].at[pl.ds(first, outs[number].shape[0])],
+            outs[number].at[:, pl.ds(start, rows)],
+            local.at[1, number],
+        )
+        stores.append((source, store))
+    return Ticker(jobs, [member[0] for member in plan], stores, loads)
+
+
+def gather_kernel(plan, sources, count, *refs):
+    ins, outs = (refs[:count], refs[count : count + len(sources)])
+    ticker = gather_ticker(
+        plan, sources, ins, outs, refs[count + len(sources) : -3], refs[-3:]
+    )
+    ticker.finish()
+
+
+def product_rows(left, right, target, size=256):
+    def body(cols):
+        target[:, cols] = nn(left[...], right[:, cols]).astype(target.dtype)
+
+    row_blocks(right.shape[1], size, body)
+
+
+def join_rows(resid, branch, scale, squares, line):
+    squares[pl.ds(line, 1), :] = jnp.zeros_like(squares[pl.ds(line, 1), :])
+
+    def body(rows):
+        value = branch[rows, :]
+        resid[rows, :] += scale * value
+        squares[pl.ds(line, 1), :] += jnp.sum(value * value, 0, keepdims=True)
+
+    row_blocks(resid.shape[0], 64, body)
+
+
+def module_forward(ticker, weights, entry, hidden, total, helds, saved, sems, chunks):
+    width = total.shape[1]
+    total[...] = jnp.zeros_like(total)
+    stores = []
+    for chunk in range(chunks):
+        before = helds[chunk % 2]
+        if chunk > 1:
+            stores[chunk - 2].wait()
+        w_in = weights.take()
+
+        def body(cols):
+            value = nn(entry[...], w_in[:, cols])
+            before[:, cols] = value.astype(jnp.bfloat16)
+            hidden[:, cols] = (value * jax.nn.sigmoid(value)).astype(jnp.bfloat16)
+
+        row_blocks(width, 256, body)
+        target = saved.at[:, pl.ds(chunk * width, width)]
+        stores.append(fetch(before, target, sems.at[chunk]))
+        w_out = weights.take()
+
+        def gather(cols):
+            total[:, cols] += nn(hidden[...], w_out[:, cols])
+
+        row_blocks(width, 256, gather)
+        ticker.advance()
+    for store in stores[-2:]:
+        store.wait()
+
+
+def depthwise_rows(glu, taps, skip, target, ticker):
+    total, width = target.shape
+    for column in range(width // LANES):
+        lanes = pl.ds(column * LANES, LANES)
+
+        def body(at, carry):
+            first = pl.multiple_of(at * LANES, LANES)
+            window = glu[pl.ds(first, LANES + 32), lanes]
+            summed = jnp.zeros((LANES, LANES), jnp.float32)
+            for tap in range(KERNEL):
+                moved = window[tap + 2 : tap + 2 + LANES]
+                summed = summed + moved * taps[pl.ds(skip + tap, 1), lanes]
+            target[pl.ds(first, LANES), lanes] = summed
+            return carry
+
+        lax.fori_loop(0, total // LANES, body, 0)
+        if column % 4 == 3:
+            ticker.advance()
+
+
+def swish_rows(source, gain, target):
+    def body(rows):
+        normal, _ = norm_parts(source[rows, :])
+        middle = normal * gain
+        target[rows, :] = (middle * jax.nn.sigmoid(middle)).astype(jnp.bfloat16)
+
+    row_blocks(source.shape[0], 64, body)
+
+
+def forward_kernel(settings, *refs):
+    plan, sources, count, norms, rows, limit = settings
+    first_ref, table_ref, tokens = refs[:3]
+    ins, refs = (refs[3 : 3 + count], refs[3 + count :])
+    outs, refs = (refs[: len(sources)], refs[len(sources) :])
+    out, squares, x1, x2, x3, x4, u0, u1, q_out, k_out, v_out, mixed_out, joined, summed = refs[:14]
+    helds, refs = (refs[14 : 14 + count], refs[14 + count :])
+    resid, total, glu, low_gains, gains, entry, hidden, held_a, held_b, q_ref = refs[:10]
+    k_ref, v_ref, mixed, slots = refs[10:14]
+    local, slot_sems, saved_sems, halo_sems = refs[14:18]
+    ticker = gather_ticker(plan, sources, ins, outs, helds, refs[18:])
+    width = resid.shape[1]
+    chunks = u0.shape[1] // width
+    groups = lax.axis_size("group")
+    part = width // groups
+    lines = low_gains.shape[0]
+    load = fetch(tokens, entry, local.at[0])
+    spaces = [slots.at[at] for at in range(3)]
+
+    def stream(*weights):
+        return Stream(spaces, slot_sems, [lambda slot, ref=ref: [(ref, slot)] for ref in weights])
+
+    def module_stream(w_in, w_out):
+        parts = []
+        for chunk in range(chunks):
+            here = pl.ds(chunk * width, width)
+            parts += [w_in.at[0, :, here], w_out.at[0, here]]
+        return stream(*parts)
+
+    for _ in range(5):
+        ticker.advance()
+    ticker.until(0)
+    small = [
+        fetch(
+            outs[0].at[0, pl.ds(group * lines, lines)],
+            low_gains.at[:, pl.ds(group * part, part)],
+            slot_sems.at[0, group],
+        )
+        for group in range(groups)
+    ]
+    for copy in small:
+        copy.wait()
+    gains[...] = low_gains[...].astype(jnp.float32)
+    load.wait()
+
+    def widen(at):
+        resid[at, :] = entry[at, :].astype(jnp.float32)
+
+    row_blocks(rows, 64, widen)
+    norm_rows(resid, gains[pl.ds(0, 1), :], entry)
+    ticker.until(1)
+    ticker.until(2)
+    pair = (held_a, held_b)
+    weights = module_stream(outs[1], outs[2])
+    module_forward(ticker, weights, entry, hidden, total, pair, u0, saved_sems, chunks)
+    join_rows(resid, total, 0.5, squares, 1)
+    stored = fetch(resid, x1, local.at[0])
+    norm_rows(resid, gains[pl.ds(1, 1), :], entry)
+    ticker.until(3)
+    weights = stream(*[outs[3].at[at] for at in range(3)])
+    own = pl.ds(LEFT, rows)
+    spare = BACK_PAD - 2 * RIGHT
+    for ref in (k_ref, v_ref):
+        ref[0, pl.ds(LEFT + rows + 2 * RIGHT, spare), :] = jnp.zeros((spare, width), jnp.bfloat16)
+    product_rows(entry, weights.take(), q_ref)
+    product_rows(entry, weights.take(), k_ref.at[0, own])
+    product_rows(entry, weights.take(), v_ref.at[0, own])
+    _, _, seq, _ = place()
+    span = lax.axis_size("seq")
+    edges = []
+    for at, ref in enumerate((k_ref, v_ref)):
+        for way, (source, target, size, step) in enumerate(
+            ((rows, 0, LEFT, 1), (LEFT, LEFT + rows, 2 * RIGHT, span - 1))
         ):
-            if 0 <= tick - 2 * lag < len(jobs):
-                getattr(jobs[tick - 2 * lag], name)()
-        if tick < len(sources):
-            source, first = sources[tick]
-            if source not in ready:
-                loads[source].wait()
-                ready.add(source)
-            rows = ins[source].shape[1]
-            start = pl.multiple_of((z * 2 + x) * rows, rows)
-            store = pltpu.make_async_copy(
-                helds[source].at[pl.ds(first, outs[tick].shape[0])],
-                outs[tick].at[:, pl.ds(start, rows)],
-                local.at[1, tick],
+            edges.append(
+                pltpu.make_async_remote_copy(
+                    src_ref=ref.at[0, pl.ds(source, size)],
+                    dst_ref=ref.at[0, pl.ds(target, size)],
+                    send_sem=halo_sems.at[0, 2 * at + way],
+                    recv_sem=halo_sems.at[1, 2 * at + way],
+                    device_id={"seq": (seq + step) % span},
+                    device_id_type=MESH,
+                )
             )
-            store.start()
-            stores.append(store)
-    for store in stores:
-        store.wait()
-
-
-def gather_weights(shards, sources, halve):
+    for edge in edges:
+        edge.start()
+    ticker.advance()
+    for edge in edges:
+        edge.wait()
+    table = table_ref[...]
+    zero = jnp.zeros((BLOCK, LANES), jnp.bfloat16)
+    for pair_at in range(width // LANES):
+        lanes = pl.ds(pair_at * LANES, LANES)
+
+        def attend_block(block, carry):
+            here = pl.ds(pl.multiple_of(block * BLOCK, BLOCK), BLOCK)
+            near = pl.ds(pl.multiple_of(block * BLOCK, BLOCK), SPAN)
+            key, value = (k_ref[0, near, lanes], v_ref[0, near, lanes])
+            mask = block_mask(first_ref[0], block, limit)
+            both = []
+            for head in range(2):
+                query = jnp.where(head_lanes(head), q_ref[here, lanes], zero)
+                probs = block_probs(query, key, table, mask)
+                both.append(nn(probs.astype(jnp.bfloat16), value))
+            mixed[here, lanes] = jnp.where(head_lanes(0), both[0], both[1]).astype(jnp.bfloat16)
+            return carry
+
+        lax.fori_loop(0, rows // BLOCK, attend_block, 0)
+        if pair_at % 2:
+            ticker.advance()
+    keeps = [
+        fetch(source, target, local.at[1 + at])
+        for at, (source, target) in enumerate(
+            ((q_ref, q_out), (k_ref, k_out), (v_ref, v_out), (mixed, mixed_out))
+        )
+    ]
+    ticker.until(4)
+    product_rows(mixed, stream(outs[4].at[0]).take(), total)
+    stored.wait()
+    join_rows(resid, total, 1.0, squares, 2)
+    stored = fetch(resid, x2, local.at[0])
+    norm_rows(resid, gains[pl.ds(2, 1), :], entry)
+    ticker.until(5)
+    weights = stream(*[outs[5].at[0, :, pl.ds(at * width, width)] for at in range(2)])
+    value_part, gate_part = (weights.take(), weights.take())
+
+    def open_columns(cols):
+        value = nn(entry[...], value_part[:, cols])
+        gate = nn(entry[...], gate_part[:, cols])
+        held_a[:, cols] = value.astype(jnp.bfloat16)
+        held_b[:, cols] = gate.astype(jnp.bfloat16)
+        opened = (value * jax.nn.sigmoid(gate)).astype(jnp.bfloat16)
+        glu[pl.ds(32, rows), cols] = opened.astype(jnp.float32)
+
+    row_blocks(width, 256, open_columns)
+    halo = pltpu.make_async_remote_copy(
+        src_ref=glu.at[pl.ds(rows, 32)],
+        dst_ref=glu.at[pl.ds(0, 32)],
+        send_sem=halo_sems.at[0, 4],
+        recv_sem=halo_sems.at[1, 4],
+        device_id={"seq": (seq + 1) % span},
+        device_id_type=MESH,
+    )
+    halo.start()
+    keeps += [
+        fetch(held, joined.at[:, pl.ds(at * width, width)], local.at[5 + at])
+        for at, held in enumerate(pair)
+    ]
+    ticker.advance()
+    halo.wait()
+    ahead = pl.ds(0, 32)
+    glu[ahead, :] = jnp.where(seq > 0, glu[ahead, :], jnp.zeros((32, width), jnp.float32))
+    depthwise_rows(glu, gains, norms, total, ticker)
+    kept = fetch(total, summed, local.at[7])
+    swish_rows(total, gains[pl.ds(3, 1), :], entry)
+    ticker.until(6)
+    conv = glu.at[pl.ds(0, rows)]
+    product_rows(entry, stream(outs[6].at[0]).take(), conv)
+    stored.wait()
+    join_rows(resid, conv, 1.0, squares, 3)
+    stored = fetch(resid, x3, local.at[0])
+    norm_rows(resid, gains[pl.ds(4, 1), :], entry)
+    kept.wait()
+    for keep in keeps:
+        keep.wait()
+    ticker.until(7)
+    ticker.until(8)
+    weights = module_stream(outs[7], outs[8])
+    module_forward(ticker, weights, entry, hidden, total, pair, u1, saved_sems, chunks)
+    stored.wait()
+    join_rows(resid, total, 0.5, squares, 4)
+    stored = fetch(resid, x4, local.at[0])
+    squares[pl.ds(0, 1), :] = jnp.zeros((1, width), jnp.float32)
+
+    def tally(at):
+        squares[pl.ds(0, 1), :] += jnp.sum(resid[at, :] * resid[at, :], 0, keepdims=True)
+
+    row_blocks(rows, 64, tally)
+    norm_rows(resid, gains[pl.ds(5, 1), :], entry)
+    last = fetch(entry, out, local.at[1])
+    ticker.finish()
+    stored.wait()
+    last.wait()
+
+
+def gather_plan(shards, sources, halve):
     groups = lax.axis_size("group")
     width = shards[1].shape[1] * groups
     part = width // groups
@@ -342,30 +633,96 @@
                 for left in range(0, shards[source].shape[2], width):
                     cut = 2 if halve and len(plan) % 3 else 1
                     plan.append((number, layer, low, left, (part, width), cut))
+    return plan
+
+
+def gather_outputs(shards, sources):
+    groups = lax.axis_size("group")
+    return [
+        jax.ShapeDtypeStruct(
+            (layers, groups * shards[source].shape[1], shards[source].shape[2]), jnp.bfloat16
+        )
+        for source, _, layers in sources
+    ]
+
+
+def gather_scratch(plan, sources):
     total = sum((2, 6, 8)[member[-1]] * depth_of() for member in plan)
+    return [
+        pltpu.SemaphoreType.DMA((total,)),
+        pltpu.SemaphoreType.DMA((total,)),
+        pltpu.SemaphoreType.DMA((2, len(sources))),
+    ]
+
+
+def gather_weights(shards, sources, halve):
+    plan = gather_plan(shards, sources, halve)
     return pl.pallas_call(
         functools.partial(
             gather_kernel, plan, [(source, first) for source, first, _ in sources], len(shards)
         ),
         in_specs=[pl.BlockSpec(memory_space=pl.ANY)] * len(shards),
         out_specs=[pl.BlockSpec(memory_space=pl.ANY)] * len(sources),
-        out_shape=[
-            jax.ShapeDtypeStruct(
-                (layers, groups * shards[source].shape[1], shards[source].shape[2]), jnp.bfloat16
-            )
-            for source, _, layers in sources
-        ],
+        out_shape=gather_outputs(shards, sources),
         scratch_shapes=[pltpu.VMEM(shard.shape, jnp.bfloat16) for shard in shards]
-        + [
-            pltpu.SemaphoreType.DMA((total,)),
-            pltpu.SemaphoreType.DMA((total,)),
-            pltpu.SemaphoreType.DMA((2, len(sources))),
-        ],
+        + gather_scratch(plan, sources),
         compiler_params=pltpu.CompilerParams(
             collective_id=1, has_side_effects=True, vmem_limit_bytes=24 << 20
         ),
         name="gather_weights",
     )(*shards)
+
+
+def forward(tokens, shards, sources, norms, table, halve):
+    rows, width = tokens.shape
+    plan = gather_plan(shards, sources, halve)
+    groups = lax.axis_size("group")
+    first = lax.axis_index("seq").astype(jnp.int32)[None] * rows
+    limit = rows * lax.axis_size("seq")
+    ext = rows + LEFT + BACK_PAD
+    inner = shards[1].shape[2]
+    lines = shards[0].shape[1]
+    hbm = pl.BlockSpec(memory_space=pl.ANY)
+    vmem = pl.BlockSpec(memory_space=pltpu.VMEM)
+    low = lambda *shape: jax.ShapeDtypeStruct(shape, jnp.bfloat16)
+    wide = lambda *shape: jax.ShapeDtypeStruct(shape, jnp.float32)
+    settings = (plan, [member[:2] for member in sources], len(shards), norms, rows, limit)
+    results = pl.pallas_call(
+        functools.partial(forward_kernel, settings),
+        in_specs=[pl.BlockSpec(memory_space=pltpu.SMEM), vmem] + [hbm] * (1 + len(shards)),
+        out_specs=[hbm] * len(sources) + [hbm, vmem] + [hbm] * 12,
+        out_shape=gather_outputs(shards, sources)
+        + [low(rows, width), wide(8, width)]
+        + [wide(rows, width)] * 4
+        + [low(rows, inner)] * 2
+        + [low(rows, width), low(1, ext, width), low(1, ext, width), low(rows, width)]
+        + [low(rows, 2 * width), wide(rows, width)],
+        scratch_shapes=[pltpu.VMEM(shard.shape, jnp.bfloat16) for shard in shards]
+        + [
+            pltpu.VMEM((rows, width), jnp.float32),
+            pltpu.VMEM((rows, width), jnp.float32),
+            pltpu.VMEM((rows + 32, width), jnp.float32),
+            pltpu.VMEM((lines, width), jnp.bfloat16),
+            pltpu.VMEM((lines, width), jnp.float32),
+        ]
+        + [pltpu.VMEM((rows, width), jnp.bfloat16)] * 5
+        + [
+            pltpu.VMEM((1, ext, width), jnp.bfloat16),
+            pltpu.VMEM((1, ext, width), jnp.bfloat16),
+            pltpu.VMEM((rows, width), jnp.bfloat16),
+            pltpu.VMEM((3, width, width), jnp.bfloat16),
+            pltpu.SemaphoreType.DMA((8,)),
+            pltpu.SemaphoreType.DMA((3, groups)),
+            pltpu.SemaphoreType.DMA((inner // width,)),
+            pltpu.SemaphoreType.DMA((2, 5)),
+        ]
+        + gather_scratch(plan, sources),
+        compiler_params=pltpu.CompilerParams(
+            collective_id=5, has_side_effects=True, vmem_limit_bytes=56 << 20
+        ),
+        name="forward",
+    )(first, wide_table(table), tokens, *shards)
+    return results[: len(sources)], results[len(sources) :]
 
 
 def swap(value, axis, bit=1):
@@ -826,7 +1183,8 @@
         if often:
             pump()
         add_transposed(grad_hidden, weights.take(), total)
-        pump()
+        if often or chunk % 2:
+            pump()
 def middle_rows(source, gain, grads, entry, sums, line):
     sums[pl.ds(line, 1), :] = jnp.zeros_like(sums[pl.ds(line, 1), :])
 
@@ -871,7 +1229,7 @@
             return carry
 
         lax.fori_loop(0, total // LANES, body, 0)
-        if column % 2:
+        if column % 4 == 3:
             pump()
 
 
@@ -971,7 +1329,6 @@
     for at, flat in enumerate((mixed_grad, q_ref)):
         job = pool.add(to_conv_in, 0, at * width)
         gradient_into(job, entry, flat)
-        pump()
         add_transposed(flat, weights.take(), total)
         pump()
     norm_back_rows(resid_in, gains[pl.ds(2, 1), :], total, resid, gain_sums, 2)
@@ -1345,44 +1702,26 @@
         (1, 1, 1),
         (2, 1, 1),
     )
-    gathered = gather_weights(shards, sources, halve)
+    quick = halve and clips == 1 and gains.shape[1] % LANES == 0
+    if quick:
+        flat = tokens.reshape(flat_rows, width)
+        gathered, saved = forward(flat, shards, sources, norms, rel_table, halve)
+    else:
+        gathered = gather_weights(shards, sources, halve)
     small = gathered[0].reshape(-1, lines, gains.shape[1]).transpose(1, 0, 2).reshape(lines, width)
     gain_f = small[:norms].astype(jnp.float32)
     depth = small[norms : norms + taps]
     f_in = (gathered[1][0], gathered[7][0])
     f_out = (gathered[2][0], gathered[8][0])
     proj, a_out, c_in, c_out = (gathered[3], gathered[4][0], gathered[5][0], gathered[6][0])
-    start = tokens.reshape(flat_rows, width).astype(jnp.float32)
-    first_branch, first_kept = feed_forward(start, gain_f[0], f_in[0], f_out[0])
-    after_first = start + 0.5 * first_branch
-    attn_branch, attn_kept = attention_forward(
-        after_first, gain_f[1], proj, a_out, rel_table, shape
-    )
-    after_attn = after_first + attn_branch
-    conv_branch, summed, conv_kept = conv_forward(
-        after_attn, gain_f[2], gain_f[3], c_in, depth, c_out, shape
-    )
-    after_conv = after_attn + conv_branch
-    second_branch, second_kept = feed_forward(after_conv, gain_f[4], f_in[1], f_out[1])
-    final = after_conv + 0.5 * second_branch
-    result, final_normal, final_inverse = norm_forward(final, gain_f[5])
-    squares = jnp.stack(
-        [
-            jnp.sum(member * member)
-            for member in (final, first_branch, attn_branch, conv_branch, second_branch)
-        ]
-    )
-    if halve and clips == 1 and gains.shape[1] % LANES == 0:
+    if quick:
+        result, squares, x1, x2, x3, x4, u0, u1, query, keys, values, mixed, joined, summed = saved
+        squares = jnp.sum(squares[:5], 1)
         grad, gain_sums, grad_table, grad_taps, shares = back(
             cotangent.reshape(flat_rows, width),
-            (final, after_conv, after_attn, after_first, tokens.reshape(flat_rows, width)),
-            (
-                conv_kept[3].astype(jnp.bfloat16),
-                summed,
-                second_kept[3].astype(jnp.bfloat16),
-                first_kept[3].astype(jnp.bfloat16),
-            ),
-            attn_kept[3:],
+            (x4, x3, x2, x1, flat),
+            (joined, summed, u1, u0),
+            (query, keys, values, mixed),
             rel_table,
             small[:8].astype(jnp.float32),
             jnp.pad(depth.astype(jnp.float32), ((0, 32 - taps), (0, 0))),
@@ -1397,6 +1736,26 @@
         grad_conv_out, grad_conv_in, grad_attn_out = shares[2:5]
         grad_qkv = shares[5:8]
     else:
+        start = tokens.reshape(flat_rows, width).astype(jnp.float32)
+        first_branch, first_kept = feed_forward(start, gain_f[0], f_in[0], f_out[0])
+        after_first = start + 0.5 * first_branch
+        attn_branch, attn_kept = attention_forward(
+            after_first, gain_f[1], proj, a_out, rel_table, shape
+        )
+        after_attn = after_first + attn_branch
+        conv_branch, summed, conv_kept = conv_forward(
+            after_attn, gain_f[2], gain_f[3], c_in, depth, c_out, shape
+        )
+        after_conv = after_attn + conv_branch
+        second_branch, second_kept = feed_forward(after_conv, gain_f[4], f_in[1], f_out[1])
+        final = after_conv + 0.5 * second_branch
+        result, final_normal, final_inverse = norm_forward(final, gain_f[5])
+        squares = jnp.stack(
+            [
+                jnp.sum(member * member)
+                for member in (final, first_branch, attn_branch, conv_branch, second_branch)
+            ]
+        )
         grad = cotangent.reshape(flat_rows, width).astype(jnp.float32)
         grad, grad_gain_final = norm_backward(grad, final_normal, final_inverse, gain_f[5])
         back_in, grad_gain_second, grad_in_second, grad_out_second = feed_back(

time: 766 us -> 649 us (0.85)
  matrix products: 52.5 us -> 0 us
  other arithmetic: 41.2 us -> 15.1 us
  local copies, waits for them, and re-layouts: 27.3 us -> 10.1 us
  starting transfers between devices: 21.6 us -> 7.68 us
    dot_general x10 -> x0, matrix products: 52.5 us -> none  [matmul(): return jnp.dot(left, right, preferred_element_type=jnp.float32)]
    pallas_call x1, Pallas kernels: 363 us -> 331 us  [back(): pl.pallas_call(functools.partial(back_kernel, (count, clips, rows, limit)...]
    pallas_call x2 -> x1, Pallas kernels: 236 us -> 262 us  [forward(): pl.pallas_call(functools.partial(forward_kernel, settings), in_specs=[pl....]
    reduce_sum x8 -> x1, other arithmetic: 23.4 us -> 0.88 us  [on_device(): squares = jnp.sum(squares[:5], 1)]
    ppermute x5 -> x0, starting transfers between devices: 13.6 us -> none  [from_behind(): lax.ppermute(value, axis, [(source, source + steps) for source in range(i...]
    unnamed x111 -> x32, local copies, waits for them, and re-layouts: 14.5 us -> 3.82 us
  transfers between devices with their start and end apart: 10 -> 5, of which waited for: 6 -> 5; matrix products, arithmetic and copies ran while one was open for 3% -> 2% of each run, Pallas kernels for 0% -> 0%
where the time goes in v5:
time: 649 us; the launch traced here: 639 us
  Pallas kernels  593 us (91%)
  other arithmetic  15.1 us (2%)
  waiting for transfers between devices  12.1 us (2%)
  local copies, waits for them, and re-layouts  10.1 us (2%)
  starting transfers between devices  7.68 us (1%)
    pallas_call x1, Pallas kernels, back(): pl.pallas_call(functools.partial(back_kernel, (count, clips, rows, limit)...  331 us
    pallas_call x1, Pallas kernels, forward(): pl.pallas_call(functools.partial(forward_kernel, settings), in_specs=[pl....  262 us
  transfers between devices with their start and end apart: 5, of which 5 were waited for; matrix products, arithmetic and copies ran while one was open for 2% of the time, Pallas kernels for 0%

profile of v5, /device:TPU:0, one launch (start us, length us, event | category | flops | bytes accessed | tf_op | source)
XLA Modules:
  0.0 638.7 jit_solution(1924147040919949102)
XLA Ops:
  2.1 1.3 fusion.3.refs_3_
  3.4 261.5 %forward.1 = (bf16[1,384,128]{2,1,0:T(8,128)(2,1)}, bf16[1,1024,4096]{2,1,0:T(8,128)(2,1)}, bf16[1,4096,1024]{2,1,0:T(8,128)(2,1)}, bf16[3,1024,1024]{2,1,0:T(8,...) custom-call(s32[1]{0:T(128)} %bitcast.refs_0_, ...), custom_call_target="tpu_custom_call" | custom-call | tf_op jit(solution)/shard_map/forward/pallas_call | solution.py:690
  265.0 0.9 copy.40
  265.9 0.9 slice_reduce_fusion
  268.1 331.1 %back.1 = (bf16[512,1024]{1,0:T(8,128)(2,1)}, f32[8,1024]{1,0:T(8,128)}, f32[256,128]{1,0:T(8,128)}, f32[32,1024]{1,0:T(8,128)}, bf16[512,1024]{1,0:T(8,128)(2,1...) custom-call(s32[1]{0:T(128)} %bitcast.refs_0_, ...), custom_call_target="tpu_custom_call" | custom-call | tf_op jit(solution)/shard_map/back/pallas_call | solution.py:1494
  599.2 1.0 add_multiply_fusion
  600.4 0.9 pad_maximum_fusion
  601.7 1.1 collective-permute-done
  602.8 1.0 fusion.5
  603.8 2.4 collective-permute-start.1
  606.2 5.4 collective-permute-done.1
  615.1 3.2 collective-permute-done.2
  618.3 2.0 collective-permute-start.3
  620.3 2.3 maximum_convert_fusion
  622.6 1.5 collective-permute-done.3
  624.1 2.5 collective-permute-start.4
  626.7 2.3 maximum_convert_fusion.1
  629.0 0.8 convert_element_type.42
  629.8 0.8 convert_element_type.44
  630.6 1.1 convert_element_type.43
  631.7 1.3 maximum_convert_fusion.2
  633.0 0.8 collective-permute-done.4
  636.6 1.0 copy.44
  637.5 1.0 copy.45
  (56 shorter events, 9.5 us)
Async XLA Ops:
  599.2 12.8 %copy-start.3 = (bf16[128,4096]{1,0:T(8,128)(2,1)S(1)}, bf16[128,4096]{1,0:T(8,128)(2,1)}, u32[]{:S(2)}) copy-start(bf16[128,4096]{1,0:T(8,128)(2,1)} %get-tuple-element.72) | copy-start | bytes 3145732
  601.3 1.5 collective-permute-start
  603.8 7.8 %collective-permute-start.1 = (f32[42,1024]{1,0:T(8,128)S(1)}, f32[42,1024]{1,0:T(8,128)S(1)}, u32[]{:S(2)}, u32[]{:S(2)}) collective-permute-start(f32[42,1024]{1,0:T(8,128)S(1)} %fusion.5), channel_id=1, source_target_pairs={{0,16},{16,0},{1,17},{17,1},{2,18},{18,2},{3,19},{19,3},{4,20},{20... | collective-permute-start | bytes 516104 | tf_op jit(solution)/shard_map/ppermute | solution.py:729
  611.6 6.7 %collective-permute-start.2 = (f32[42,1024]{1,0:T(8,128)S(1)}, f32[42,1024]{1,0:T(8,128)S(1)}, u32[]{:S(2)}, u32[]{:S(2)}) collective-permute-start(f32[42,1024]{1,0:T(8,128)S(1)} %add.31), channel_id=1, source_target_pairs={{0,2},{2,0},{4,6},{6,4},{8,10},{10,8},{12,14},{14,12},{1,3},{3,1},... | collective-permute-start | bytes 516104 | tf_op jit(solution)/shard_map/ppermute | solution.py:729
  612.3 1.3 copy-start.2
  618.3 8.3 %copy-start.4 = (bf16[512,1024]{1,0:T(8,128)(2,1)S(1)}, bf16[512,1024]{1,0:T(8,128)(2,1)}, u32[]{:S(2)}) copy-start(bf16[512,1024]{1,0:T(8,128)(2,1)} %get-tuple-element.75) | copy-start | bytes 3145732
  618.3 8.3 %copy-start.5 = (bf16[512,1024]{1,0:T(8,128)(2,1)S(1)}, bf16[512,1024]{1,0:T(8,128)(2,1)}, u32[]{:S(2)}) copy-start(bf16[512,1024]{1,0:T(8,128)(2,1)} %get-tuple-element.74) | copy-start | bytes 3145732
  618.3 5.8 collective-permute-start.3
  624.1 9.7 %collective-permute-start.4 = (f32[42,1024]{1,0:T(8,128)S(1)}, f32[42,1024]{1,0:T(8,128)S(1)}, u32[]{:S(2)}, u32[]{:S(2)}) collective-permute-start(f32[42,1024]{1,0:T(8,128)S(1)} %add.33), channel_id=1, source_target_pairs={{0,8},{2,10},{4,12},{6,14},{8,0},{10,2},{12,4},{14,6},{1,9},{3,11}... | collective-permute-start | bytes 516104 | tf_op jit(solution)/shard_map/ppermute | solution.py:729
  626.6 2.3 copy-start.11
  626.6 3.2 copy-start.10
  626.6 4.0 copy-start.6
  628.9 2.8 copy-start.7
  628.9 2.8 copy-start.8
  628.9 2.8 copy-start.9
  631.7 4.8 copy-start
  633.0 4.5 copy-start.1

commit v6 on v5

--- a/solution.py
+++ b/solution.py
@@ -77,9 +77,9 @@
 def nn(left,right):
     return jnp.dot(left,right,preferred_element_type=jnp.float32)
 
-def block_mask(first, block, limit):
-    rows=lax.broadcasted_iota(jnp.int32,(BLOCK,SPAN),0)
-    cols=lax.broadcasted_iota(jnp.int32,(BLOCK,SPAN),1)
+def block_mask(first, block, limit, lines=BLOCK):
+    rows=lax.broadcasted_iota(jnp.int32,(lines,SPAN),0)%BLOCK
+    cols=lax.broadcasted_iota(jnp.int32,(lines,SPAN),1)
     offset=cols-rows
     place=first+block*BLOCK+cols-LEFT
     return (offset>=0)&(offset<WIN)&(place>=0)&(place<limit)
@@ -282,6 +282,24 @@
                     self.got(steps, dx, dy, 1, 3, index)
         for copy in self.started:
             copy.wait_send()
+
+
+def stack_heads(values):
+    zero = jnp.zeros((BLOCK, LANES), jnp.bfloat16)
+    return jnp.concatenate([jnp.where(head_lanes(head), values, zero) for head in range(2)], 0)
+
+
+def roll_halves(values, shift):
+    halves = [values[:BLOCK], values[BLOCK:]]
+    rolled = [pltpu.roll(half, shift, 1, stride=1, stride_axis=0) for half in halves]
+    return jnp.concatenate(rolled, 0)
+
+
+def stacked_probs(query, keys, table, mask):
+    relative = roll_halves(nt(query, table), 0)
+    raw = jnp.where(mask, (nt(query, keys) + relative) * HEAD_DIM**-0.5, NEGATIVE)
+    expo = jnp.exp(raw - jnp.max(raw, -1, keepdims=True))
+    return expo * (1.0 / jnp.sum(expo, -1, keepdims=True))
 
 
 class Ticker:
@@ -379,31 +397,38 @@
     row_blocks(resid.shape[0], 64, body)
 
 
-def module_forward(ticker, weights, entry, hidden, total, helds, saved, sems, chunks):
+def module_forward(ticker, weights, entry, hidden, total, helds, saved, sems, ready):
     width = total.shape[1]
-    total[...] = jnp.zeros_like(total)
+    chunks = hidden.shape[0]
     stores = []
     for chunk in range(chunks):
         before = helds[chunk % 2]
         if chunk > 1:
             stores[chunk - 2].wait()
-        w_in = weights.take()
+        w_in = weights[0].take()
 
         def body(cols):
             value = nn(entry[...], w_in[:, cols])
             before[:, cols] = value.astype(jnp.bfloat16)
-            hidden[:, cols] = (value * jax.nn.sigmoid(value)).astype(jnp.bfloat16)
+            hidden[chunk, :, cols] = (value * jax.nn.sigmoid(value)).astype(jnp.bfloat16)
 
         row_blocks(width, 256, body)
         target = saved.at[:, pl.ds(chunk * width, width)]
         stores.append(fetch(before, target, sems.at[chunk]))
+        if ready == 2 or chunk % 2:
+            ticker.advance()
+    total[...] = jnp.zeros_like(total)
+    ticker.until(ready)
+    weights = weights[1]()
+    for chunk in range(chunks):
         w_out = weights.take()
 
         def gather(cols):
-            total[:, cols] += nn(hidden[...], w_out[:, cols])
+            total[:, cols] += nn(hidden[chunk], w_out[:, cols])
 
         row_blocks(width, 256, gather)
-        ticker.advance()
+        if chunk % 2:
+            ticker.advance()
     for store in stores[-2:]:
         store.wait()
 
@@ -459,12 +484,10 @@
     def stream(*weights):
         return Stream(spaces, slot_sems, [lambda slot, ref=ref: [(ref, slot)] for ref in weights])
 
-    def module_stream(w_in, w_out):
-        parts = []
-        for chunk in range(chunks):
-            here = pl.ds(chunk * width, width)
-            parts += [w_in.at[0, :, here], w_out.at[0, here]]
-        return stream(*parts)
+    def module_streams(w_in, w_out):
+        heres = [pl.ds(chunk * width, width) for chunk in range(chunks)]
+        first = stream(*[w_in.at[0, :, here] for here in heres])
+        return (first, lambda: stream(*[w_out.at[0, here] for here in heres]))
 
     for _ in range(5):
         ticker.advance()
@@ -488,10 +511,9 @@
     row_blocks(rows, 64, widen)
     norm_rows(resid, gains[pl.ds(0, 1), :], entry)
     ticker.until(1)
-    ticker.until(2)
     pair = (held_a, held_b)
-    weights = module_stream(outs[1], outs[2])
-    module_forward(ticker, weights, entry, hidden, total, pair, u0, saved_sems, chunks)
+    weights = module_streams(outs[1], outs[2])
+    module_forward(ticker, weights, entry, hidden, total, pair, u0, saved_sems, 2)
     join_rows(resid, total, 0.5, squares, 1)
     stored = fetch(resid, x1, local.at[0])
     norm_rows(resid, gains[pl.ds(1, 1), :], entry)
@@ -527,7 +549,6 @@
     for edge in edges:
         edge.wait()
     table = table_ref[...]
-    zero = jnp.zeros((BLOCK, LANES), jnp.bfloat16)
     for pair_at in range(width // LANES):
         lanes = pl.ds(pair_at * LANES, LANES)
 
@@ -535,13 +556,11 @@
             here = pl.ds(pl.multiple_of(block * BLOCK, BLOCK), BLOCK)
             near = pl.ds(pl.multiple_of(block * BLOCK, BLOCK), SPAN)
             key, value = (k_ref[0, near, lanes], v_ref[0, near, lanes])
-            mask = block_mask(first_ref[0], block, limit)
-            both = []
-            for head in range(2):
-                query = jnp.where(head_lanes(head), q_ref[here, lanes], zero)
-                probs = block_probs(query, key, table, mask)
-                both.append(nn(probs.astype(jnp.bfloat16), value))
-            mixed[here, lanes] = jnp.where(head_lanes(0), both[0], both[1]).astype(jnp.bfloat16)
+            mask = block_mask(first_ref[0], block, limit, 2 * BLOCK)
+            probs = stacked_probs(stack_heads(q_ref[here, lanes]), key, table, mask)
+            both = nn(probs.astype(jnp.bfloat16), value)
+            both = jnp.where(head_lanes(0), both[:BLOCK], both[BLOCK:])
+            mixed[here, lanes] = both.astype(jnp.bfloat16)
             return carry
 
         lax.fori_loop(0, rows // BLOCK, attend_block, 0)
@@ -554,6 +573,7 @@
         )
     ]
     ticker.until(4)
+    ticker.advance()
     product_rows(mixed, stream(outs[4].at[0]).take(), total)
     stored.wait()
     join_rows(resid, total, 1.0, squares, 2)
@@ -571,6 +591,7 @@
         opened = (value * jax.nn.sigmoid(gate)).astype(jnp.bfloat16)
         glu[pl.ds(32, rows), cols] = opened.astype(jnp.float32)
 
+    ticker.advance()
     row_blocks(width, 256, open_columns)
     halo = pltpu.make_async_remote_copy(
         src_ref=glu.at[pl.ds(rows, 32)],
@@ -593,6 +614,7 @@
     kept = fetch(total, summed, local.at[7])
     swish_rows(total, gains[pl.ds(3, 1), :], entry)
     ticker.until(6)
+    ticker.advance()
     conv = glu.at[pl.ds(0, rows)]
     product_rows(entry, stream(outs[6].at[0]).take(), conv)
     stored.wait()
@@ -603,9 +625,8 @@
     for keep in keeps:
         keep.wait()
     ticker.until(7)
-    ticker.until(8)
-    weights = module_stream(outs[7], outs[8])
-    module_forward(ticker, weights, entry, hidden, total, pair, u1, saved_sems, chunks)
+    weights = module_streams(outs[7], outs[8])
+    module_forward(ticker, weights, entry, hidden, total, pair, u1, saved_sems, 8)
     stored.wait()
     join_rows(resid, total, 0.5, squares, 4)
     stored = fetch(resid, x4, local.at[0])
@@ -705,7 +726,11 @@
             pltpu.VMEM((lines, width), jnp.bfloat16),
             pltpu.VMEM((lines, width), jnp.float32),
         ]
-        + [pltpu.VMEM((rows, width), jnp.bfloat16)] * 5
+        + [
+            pltpu.VMEM((rows, width), jnp.bfloat16),
+            pltpu.VMEM((inner // width, rows, width), jnp.bfloat16),
+        ]
+        + [pltpu.VMEM((rows, width), jnp.bfloat16)] * 3
         + [
             pltpu.VMEM((1, ext, width), jnp.bfloat16),
             pltpu.VMEM((1, ext, width), jnp.bfloat16),
@@ -1241,17 +1266,20 @@
 
 def back_kernel(settings, *refs):
     count, clips, rows, limit = settings
-    first_ref, table_ref, gains, taps = refs[:4]
+    first_ref, table_ref, gains, taps, squares = refs[:5]
+    refs = refs[1:]
     cot, x4, x3, x2, x1, x0, u1, u0, joined, summed = refs[4:14]
     mixed, query, keys, values, c_in, c_out, a_out, qkv = refs[14:22]
     second_in, second_out, w_in, w_out = refs[22:26]
-    grad_x, gain_sums, dt_ref, tap_sums = refs[26:30]
+    grad_x, tally = refs[26:28]
+    refs = refs[:26] + (None, None) + refs[26:]
     to_second_out, to_second_in, to_conv_out, to_conv_in = refs[30:34]
     to_attn, to_q, to_k, to_v, to_out, to_in, kept = refs[34:41]
     refs = refs[41:]
     resid, total_ext, resid_in, low, entry, mixed_grad, q_ref, dq_ref = refs[:8]
     k_ref, v_ref, dk_ref, dv_ref, later, earlier, dk_sum, dv_sum, slots = refs[8:17]
-    local, slot_sems, saved_sems, halo_sems = refs[17:21]
+    local, slot_sems, saved_sems, halo_sems, arrivals, tally_sems, dt_ref = refs[17:24]
+    gain_sums, tap_sums = (tally.at[pl.ds(0, 8)], tally.at[pl.ds(8, 32)])
     width = resid.shape[1]
     total = total_ext.at[pl.ds(0, rows)]
     groups = lax.axis_size("group")
@@ -1259,7 +1287,7 @@
     span = lax.axis_size("seq")
     chunks = w_out.shape[1]
     reduce_greet()
-    pool = Pool(part, width, count, kept, refs[21:])
+    pool = Pool(part, width, count, kept, refs[24:])
     pump = pool.pump
     copies = module_copies(second_in, second_out, groups)
     copies += [lambda slot: [(c_out, slot)]]
@@ -1347,10 +1375,9 @@
     for load in loads[1:]:
         load.wait()
     table = table_ref[...]
-    zero = jnp.zeros((BLOCK, LANES), jnp.bfloat16)
-    across = lax.broadcasted_iota(jnp.int32, (BLOCK, BLOCK), 0)
-    across = across + lax.broadcasted_iota(jnp.int32, (BLOCK, BLOCK), 1)
-    flip = (across == BLOCK - 1).astype(jnp.float32).astype(jnp.bfloat16)
+    across = lax.broadcasted_iota(jnp.int32, (2 * BLOCK, 2 * BLOCK), 0)
+    across = across + lax.broadcasted_iota(jnp.int32, (2 * BLOCK, 2 * BLOCK), 1)
+    flip = (across == 2 * BLOCK - 1).astype(jnp.float32).astype(jnp.bfloat16)
     dt_ref[...] = jnp.zeros_like(dt_ref)
     blocks = rows // BLOCK
     for pair in range(width // LANES):
@@ -1364,25 +1391,23 @@
             near = pl.ds(pl.multiple_of(block * BLOCK, BLOCK), SPAN)
             key = k_ref[clip, near, lanes]
             value = v_ref[clip, near, lanes]
-            mask = block_mask(first_ref[0], block, limit)
-            grad_query = []
-            for head in range(2):
-                q = jnp.where(head_lanes(head), q_ref[here, lanes], zero)
-                g = jnp.where(head_lanes(head), mixed_grad[here, lanes], zero)
-                probs = block_probs(q, key, table, mask)
-                grad_probs = nt(g, value)
-                grad_raw = probs * (grad_probs - jnp.sum(probs * grad_probs, -1, keepdims=True))
-                grad_raw = grad_raw.astype(jnp.bfloat16)
-                turned = pltpu.roll(
-                    nn(flip, grad_raw), SPAN - BLOCK + 1, 1, stride=1, stride_axis=0
-                )
-                unskewed = nn(flip, turned.astype(jnp.bfloat16)).astype(jnp.bfloat16)
-                dv_sum[clip, near, :] += tn(probs.astype(jnp.bfloat16), g)
-                dk_sum[clip, near, :] += tn(grad_raw, q)
-                dt_ref[...] += tn(unskewed, q)
-                grad_query.append(nn(grad_raw, key) + nn(unskewed, table))
-            both = jnp.where(head_lanes(0), grad_query[0], grad_query[1])
-            dq_ref[here, lanes] = (both * HEAD_DIM**-0.5).astype(jnp.bfloat16)
+            mask = block_mask(first_ref[0], block, limit, 2 * BLOCK)
+            q = stack_heads(q_ref[here, lanes])
+            g = stack_heads(mixed_grad[here, lanes])
+            probs = stacked_probs(q, key, table, mask)
+            grad_probs = nt(g, value)
+            grad_raw = probs * (grad_probs - jnp.sum(probs * grad_probs, -1, keepdims=True))
+            grad_raw = grad_raw.astype(jnp.bfloat16)
+            dv_sum[clip, near, :] += tn(probs.astype(jnp.bfloat16), g)
+            dk_sum[clip, near, :] += tn(grad_raw, q)
+            turned = roll_halves(nn(flip, grad_raw), SPAN - BLOCK + 1).astype(jnp.bfloat16)
+            dt_ref[...] += tn(turned, nn(flip, q).astype(jnp.bfloat16))
+            relative = nn(turned, table)
+            relative = jnp.where(head_lanes(0), relative[BLOCK:], relative[:BLOCK])
+            relative = nn(flip[:BLOCK, BLOCK:], relative.astype(jnp.bfloat16))
+            direct = nn(grad_raw, key)
+            direct = jnp.where(head_lanes(0), direct[:BLOCK], direct[BLOCK:])
+            dq_ref[here, lanes] = ((direct + relative) * HEAD_DIM**-0.5).astype(jnp.bfloat16)
             return carry
 
         lax.fori_loop(0, clips * blocks, attend_block, 0, unroll=2)
@@ -1448,8 +1473,38 @@
     cast_rows(resid, low)
     store = pltpu.make_async_copy(low, grad_x, local.at[1])
     store.start()
+    for block in range(10):
+        spot = pl.ds(40 + block // 8 * 8, 8)
+        tally[spot, pl.ds(block % 8 * LANES, LANES)] = dt_ref[pl.ds(block * 8, 8), :]
+    tally[pl.ds(48, 8), pl.ds(2 * LANES, width - 2 * LANES)] = jnp.zeros(
+        (8, width - 2 * LANES), jnp.float32
+    )
+    tally[pl.ds(56, 8), :] = squares[...]
+    for turn, peer in enumerate(partners()):
+        copy = pltpu.make_async_remote_copy(
+            src_ref=tally,
+            dst_ref=arrivals.at[turn],
+            send_sem=tally_sems.at[0, turn],
+            recv_sem=tally_sems.at[1, turn],
+            device_id=peer,
+            device_id_type=MESH,
+        )
+        copy.start()
+        pool.pump()
+        copy.wait()
+        tally[...] += arrivals[turn]
     pool.drain()
     store.wait()
+
+
+def partners():
+    group = lax.axis_index("group")
+    peers = [{"replica": 1 - lax.axis_index("replica")}, {"seq": 1 - lax.axis_index("seq")}]
+    bit = 1
+    while bit < lax.axis_size("group"):
+        peers.append({"group": group + bit * (1 - 2 * (group // bit % 2))})
+        bit *= 2
+    return peers
 
 
 def reduce_greet():
@@ -1459,7 +1514,7 @@
     greet(deep + [across, twin] + [{"seq": (seq + steps) % span} for steps in range(1, span)])
 
 
-def back(cot, resids, saved, kept, table, gains, taps, weights, rows):
+def back(cot, resids, saved, kept, table, gains, taps, squares, weights, rows):
     joined, summed, u1, u0 = saved
     query, keys, values, mixed = kept
     c_in, c_out, a_out, qkv, second_in, second_out, w_in, w_out = weights
@@ -1474,6 +1529,7 @@
     vmem = pl.BlockSpec(memory_space=pltpu.VMEM)
     low = lambda *shape: jax.ShapeDtypeStruct(shape, jnp.bfloat16)
     wide = lambda *shape: jax.ShapeDtypeStruct(shape, jnp.float32)
+    turns = 2 + (groups - 1).bit_length()
     holds = [pltpu.VMEM((rows + more, width), jnp.float32) for more in (0, 32, 0)]
     holds += [pltpu.VMEM((rows, width), jnp.bfloat16)] * 5
     holds += [pltpu.VMEM((clips, ext, width), jnp.bfloat16)] * 4
@@ -1487,15 +1543,18 @@
         pltpu.SemaphoreType.DMA((3, groups)),
         pltpu.SemaphoreType.DMA((2, groups)),
         pltpu.SemaphoreType.DMA((2, 5)),
+        pltpu.VMEM((turns, 64, width), jnp.float32),
+        pltpu.SemaphoreType.DMA((2, turns)),
+        pltpu.VMEM((SPAN, LANES), jnp.float32),
     ]
     grad_out = low(chunks * part, width)
     grad_in = low(part, chunks * width)
     by_chunk = lambda weight: weight.reshape(groups, chunks, part, width)
     results = pl.pallas_call(
         functools.partial(back_kernel, (count, clips, rows, limit)),
-        in_specs=[pl.BlockSpec(memory_space=pltpu.SMEM)] + [vmem] * 3 + [hbm] * 22,
-        out_specs=[hbm] + [vmem] * 3 + [hbm] * 11,
-        out_shape=[low(rows, width), wide(8, width), wide(SPAN, LANES), wide(32, width)]
+        in_specs=[pl.BlockSpec(memory_space=pltpu.SMEM)] + [vmem] * 4 + [hbm] * 22,
+        out_specs=[hbm, vmem] + [hbm] * 11,
+        out_shape=[low(rows, width), wide(64, width)]
         + [grad_out, grad_in, low(part, width), low(part, 2 * width)]
         + [low(part, width)] * 4
         + [grad_out, grad_in, low(count, groups // 2, 2, part, width)],
@@ -1509,6 +1568,7 @@
         wide_table(table),
         gains,
         taps,
+        squares,
         cot,
         *resids,
         u1,
@@ -1528,9 +1588,11 @@
         w_in,
         by_chunk(w_out),
     )
-    grad_x, gain_sums, dt, tap_sums = results[:4]
+    grad_x, tally = results[:2]
+    tables = tally[40:56].reshape(2, 8, width // LANES, LANES).transpose(0, 2, 1, 3)
+    dt = tables.reshape(-1, LANES)
     dt = (dt[:WIN, :HEAD_DIM] + dt[:WIN, HEAD_DIM:]) * HEAD_DIM**-0.5
-    return grad_x, gain_sums, dt, tap_sums, results[4:]
+    return grad_x, tally, dt, results[2:]
 
 
 def unmix(grad, groups):
@@ -1716,8 +1778,7 @@
     proj, a_out, c_in, c_out = (gathered[3], gathered[4][0], gathered[5][0], gathered[6][0])
     if quick:
         result, squares, x1, x2, x3, x4, u0, u1, query, keys, values, mixed, joined, summed = saved
-        squares = jnp.sum(squares[:5], 1)
-        grad, gain_sums, grad_table, grad_taps, shares = back(
+        grad, totals, total_table, shares = back(
             cotangent.reshape(flat_rows, width),
             (x4, x3, x2, x1, flat),
             (joined, summed, u1, u0),
@@ -1725,11 +1786,12 @@
             rel_table,
             small[:8].astype(jnp.float32),
             jnp.pad(depth.astype(jnp.float32), ((0, 32 - taps), (0, 0))),
+            squares,
             (c_in, c_out, a_out, proj, f_in[1], f_out[1], f_in[0], f_out[0]),
             rows,
         )
-        gain_grads = gain_sums[:norms]
-        grad_taps = grad_taps[:taps]
+        sums = jnp.sum(totals[56:61], 1)
+        totals = jnp.concatenate([totals[:norms], totals[8 : 8 + taps]], 0)
         groups = lax.axis_size("group")
         grad_in_first, grad_in_second = (unmix(shares[9], groups), unmix(shares[1], groups))
         grad_out_first, grad_out_second = (shares[8], shares[0])
@@ -1793,19 +1855,22 @@
                 grad_gain_final,
             ]
         )
-    loose = jnp.concatenate([grad_table.reshape(-1), squares])
-    lines = -(-loose.shape[0] // width)
-    loose = jnp.pad(loose, (0, lines * width - loose.shape[0])).reshape(lines, width)
-    totals = butterfly(jnp.concatenate([gain_grads, grad_taps, loose], 0))
+        loose = jnp.concatenate([grad_table.reshape(-1), squares])
+        lines = -(-loose.shape[0] // width)
+        loose = jnp.pad(loose, (0, lines * width - loose.shape[0])).reshape(lines, width)
+        totals = butterfly(jnp.concatenate([gain_grads, grad_taps, loose], 0))
+        loose = totals[norms + taps :].reshape(-1)
+        totals = totals[: norms + taps]
+        table_size = rel_table.shape[0] * rel_table.shape[1]
+        total_table = loose[:table_size].reshape(rel_table.shape)
+        sums = loose[table_size : table_size + 5]
     owned = lax.dynamic_slice_in_dim(
-        totals[: norms + taps], lax.axis_index("group") * gains.shape[1], gains.shape[1], 1
-    )
-    loose = totals[norms + taps :].reshape(-1)
-    table_size = rel_table.shape[0] * rel_table.shape[1]
+        totals, lax.axis_index("group") * gains.shape[1], gains.shape[1], 1
+    )
     count = (
         flat_rows * width * lax.axis_size("seq") * lax.axis_size("group") * lax.axis_size("replica")
     )
-    stats = jnp.sqrt(loose[table_size : table_size + 5] / count)
+    stats = jnp.sqrt(sums / count)
     return (
         result.astype(jnp.bfloat16).reshape(shape),
         grad.astype(jnp.bfloat16).reshape(shape),
@@ -1817,7 +1882,7 @@
         grad_conv_out.astype(jnp.float32),
         owned[norms:],
         owned[:norms],
-        loose[:table_size].reshape(rel_table.shape),
+        total_table,
         stats,
     )
 

time: 649 us -> 638 us (0.983)
  waiting for transfers between devices: 12.1 us -> 0 us
  starting transfers between devices: 7.68 us -> 0 us
    ppermute x5 -> x0, waiting for transfers between devices: 12.1 us -> none  [swap(): lax.ppermute(value, axis, [(i, i ^ bit) for i in range(lax.axis_size(axis...]
    ppermute x5 -> x0, starting transfers between devices: 7.68 us -> none  [swap(): lax.ppermute(value, axis, [(i, i ^ bit) for i in range(lax.axis_size(axis...]
  transfers between devices with their start and end apart: 5 -> 0, of which waited for: 5 -> 0; matrix products, arithmetic and copies ran while one was open for 2% -> 0% of each run, Pallas kernels for 0% -> 0%
where the time goes in v6:
time: 638 us; the launch traced here: 625 us
  Pallas kernels  595 us (93%)
  other arithmetic  15.2 us (2%)
  local copies, waits for them, and re-layouts  14.3 us (2%)
    pallas_call x1, Pallas kernels, back(): pl.pallas_call(functools.partial(back_kernel, (count, clips, rows, limit)...  337 us
    pallas_call x1, Pallas kernels, forward(): pl.pallas_call(functools.partial(forward_kernel, settings), in_specs=[pl....  258 us

profile of v6, /device:TPU:0, one launch (start us, length us, event | category | flops | bytes accessed | tf_op | source)
XLA Modules:
  0.0 625.1 jit_solution(7547788717342240725)
XLA Ops:
  0.7 1.3 fusion.5.refs_3_
  2.0 0.7 pad.15
  2.7 0.7 copy.28.refs_1_
  3.4 257.8 %forward.1 = (bf16[1,384,128]{2,1,0:T(8,128)(2,1)}, bf16[1,1024,4096]{2,1,0:T(8,128)(2,1)}, bf16[1,4096,1024]{2,1,0:T(8,128)(2,1)}, bf16[3,1024,1024]{2,1,0:T(8,...) custom-call(s32[1]{0:T(128)} %bitcast.refs_0_, ...), custom_call_target="tpu_custom_call" | custom-call | tf_op jit(solution)/shard_map/forward/pallas_call | solution.py:711
  261.2 0.9 copy.40
  262.8 0.7 pad_convert_fusion.refs_3_
  263.5 336.8 %back.1 = (bf16[512,1024]{1,0:T(8,128)(2,1)}, f32[64,1024]{1,0:T(8,128)}, bf16[512,1024]{1,0:T(8,128)(2,1)}, bf16[128,4096]{1,0:T(8,128)(2,1)}, bf16[128,1024]{1...) custom-call(s32[1]{0:T(128)} %bitcast.refs_0_, ...), custom_call_target="tpu_custom_call" | custom-call | tf_op jit(solution)/shard_map/back/pallas_call | solution.py:1553
  600.3 1.5 copy.36
  602.2 0.8 stack_reshape.6
  603.1 0.9 slice_reduce_fusion
  604.5 0.8 slice.34
  605.2 0.8 slice.38
  606.1 0.9 slice.35
  607.2 0.7 copy.33
  609.1 1.8 convert_element_type.40
  610.9 0.8 convert_element_type.42
  612.4 0.8 stack_reshape.7
  613.2 2.1 convert_element_type.41
  615.3 2.3 maximum_convert_fusion.2
  617.6 2.3 maximum_convert_fusion
  620.0 2.3 maximum_convert_fusion.1
  622.3 1.0 copy.44
  623.3 0.6 copy-done.1
  623.9 1.0 copy.45
  (27 shorter events, 3.7 us)
Async XLA Ops:
  602.2 8.6 %copy-start.6 = (bf16[128,1024]{1,0:T(8,128)(2,1)S(1)}, bf16[128,1024]{1,0:T(8,128)(2,1)}, u32[]{:S(2)}) copy-start(bf16[128,1024]{1,0:T(8,128)(2,1)} %get-tuple-element.80) | copy-start | bytes 786436
  602.2 9.5 %copy-start.2 = (bf16[128,4096]{1,0:T(8,128)(2,1)S(1)}, bf16[128,4096]{1,0:T(8,128)(2,1)}, u32[]{:S(2)}) copy-start(bf16[128,4096]{1,0:T(8,128)(2,1)} %get-tuple-element.72) | copy-start | bytes 3145732
  612.4 3.0 copy-start.5
  617.6 2.3 copy-start.3
  617.6 2.4 copy-start.4
  620.0 2.3 copy-start
  622.3 1.6 copy-start.1

commit v7 on v6

--- a/solution.py
+++ b/solution.py
@@ -394,7 +394,7 @@
         resid[rows, :] += scale * value
         squares[pl.ds(line, 1), :] += jnp.sum(value * value, 0, keepdims=True)
 
-    row_blocks(resid.shape[0], 64, body)
+    row_blocks(resid.shape[0], 128, body)
 
 
 def module_forward(ticker, weights, entry, hidden, total, helds, saved, sems, ready):
@@ -459,7 +459,7 @@
         middle = normal * gain
         target[rows, :] = (middle * jax.nn.sigmoid(middle)).astype(jnp.bfloat16)
 
-    row_blocks(source.shape[0], 64, body)
+    row_blocks(source.shape[0], 128, body)
 
 
 def forward_kernel(settings, *refs):
@@ -508,7 +508,7 @@
     def widen(at):
         resid[at, :] = entry[at, :].astype(jnp.float32)
 
-    row_blocks(rows, 64, widen)
+    row_blocks(rows, 128, widen)
     norm_rows(resid, gains[pl.ds(0, 1), :], entry)
     ticker.until(1)
     pair = (held_a, held_b)
@@ -635,7 +635,7 @@
     def tally(at):
         squares[pl.ds(0, 1), :] += jnp.sum(resid[at, :] * resid[at, :], 0, keepdims=True)
 
-    row_blocks(rows, 64, tally)
+    row_blocks(rows, 128, tally)
     norm_rows(resid, gains[pl.ds(5, 1), :], entry)
     last = fetch(entry, out, local.at[1])
     ticker.finish()
@@ -1061,7 +1061,7 @@
         normal, _ = norm_parts(source[rows, :].astype(jnp.float32))
         target[rows, :] = (normal * gain).astype(target.dtype)
 
-    row_blocks(source.shape[0], 64, body)
+    row_blocks(source.shape[0], 128, body)
 
 
 def norm_back_rows(source, gain, grads, resid, sums, line):
@@ -1078,14 +1078,14 @@
         )
         sums[pl.ds(line, 1), :] += jnp.sum(grad * normal, 0, keepdims=True)
 
-    row_blocks(source.shape[0], 64, body)
+    row_blocks(source.shape[0], 128, body)
 
 
 def cast_rows(source, target, scale=1.0):
     def body(rows):
         target[rows, :] = (source[rows, :] * scale).astype(jnp.bfloat16)
 
-    row_blocks(source.shape[0], 64, body)
+    row_blocks(source.shape[0], 128, body)
 
 
 def transposed_rows(left, right, target, size=256):
@@ -1227,7 +1227,7 @@
         )
         sums[pl.ds(line, 1), :] += jnp.sum(grad * normal, 0, keepdims=True)
 
-    row_blocks(source.shape[0], 64, body)
+    row_blocks(source.shape[0], 128, body)
 
 
 def depthwise_back(grads, taps, value, gate, grad_value, grad_gate, tap_sums, pump):
@@ -1314,7 +1314,7 @@
     def widen(at):
         total[at, :] = low[at, :].astype(jnp.float32)
 
-    row_blocks(rows, 64, widen)
+    row_blocks(rows, 128, widen)
     norm_back_rows(resid_in, gains[pl.ds(5, 1), :], total, resid, gain_sums, 5)
     load = fetch(x3, resid_in, local.at[0])
     cast_rows(resid, low, 0.5)

time: 638 us -> 633 us (level)
  no operation moved by 1% of the time
where the time goes in v7:
time: 633 us; the launch traced here: 623 us
  Pallas kernels  592 us (94%)
  other arithmetic  15.2 us (2%)
  local copies, waits for them, and re-layouts  14.3 us (2%)
    pallas_call x1, Pallas kernels, back(): pl.pallas_call(functools.partial(back_kernel, (count, clips, rows, limit)...  337 us
    pallas_call x1, Pallas kernels, forward(): pl.pallas_call(functools.partial(forward_kernel, settings), in_specs=[pl....  256 us

profile of v7, /device:TPU:0, one launch (start us, length us, event | category | flops | bytes accessed | tf_op | source)
XLA Modules:
  0.0 623.0 jit_solution(5812915857371562114)
XLA Ops:
  0.7 1.3 fusion.5.refs_3_
  2.0 0.7 pad.15
  2.7 0.7 copy.28.refs_1_
  3.4 255.5 %forward.1 = (bf16[1,384,128]{2,1,0:T(8,128)(2,1)}, bf16[1,1024,4096]{2,1,0:T(8,128)(2,1)}, bf16[1,4096,1024]{2,1,0:T(8,128)(2,1)}, bf16[3,1024,1024]{2,1,0:T(8,...) custom-call(s32[1]{0:T(128)} %bitcast.refs_0_, ...), custom_call_target="tpu_custom_call" | custom-call | tf_op jit(solution)/shard_map/forward/pallas_call | solution.py:711
  258.9 0.9 copy.40
  260.5 0.7 pad_convert_fusion.refs_3_
  261.2 336.9 %back.1 = (bf16[512,1024]{1,0:T(8,128)(2,1)}, f32[64,1024]{1,0:T(8,128)}, bf16[512,1024]{1,0:T(8,128)(2,1)}, bf16[128,4096]{1,0:T(8,128)(2,1)}, bf16[128,1024]{1...) custom-call(s32[1]{0:T(128)} %bitcast.refs_0_, ...), custom_call_target="tpu_custom_call" | custom-call | tf_op jit(solution)/shard_map/back/pallas_call | solution.py:1553
  598.2 1.5 copy.36
  600.1 0.8 stack_reshape.6
  600.9 0.9 slice_reduce_fusion
  602.3 0.8 slice.34
  603.1 0.8 slice.38
  603.9 0.9 slice.35
  605.0 0.7 copy.33
  606.9 1.8 convert_element_type.40
  608.7 0.8 convert_element_type.42
  610.2 0.8 stack_reshape.7
  611.1 2.1 convert_element_type.41
  613.2 2.3 maximum_convert_fusion.2
  615.5 2.3 maximum_convert_fusion
  617.9 2.3 maximum_convert_fusion.1
  620.2 1.0 copy.44
  621.1 0.6 copy-done.1
  621.8 1.0 copy.45
  (27 shorter events, 3.7 us)
Async XLA Ops:
  600.0 8.6 %copy-start.6 = (bf16[128,1024]{1,0:T(8,128)(2,1)S(1)}, bf16[128,1024]{1,0:T(8,128)(2,1)}, u32[]{:S(2)}) copy-start(bf16[128,1024]{1,0:T(8,128)(2,1)} %get-tuple-element.80) | copy-start | bytes 786436
  600.1 9.5 %copy-start.2 = (bf16[128,4096]{1,0:T(8,128)(2,1)S(1)}, bf16[128,4096]{1,0:T(8,128)(2,1)}, u32[]{:S(2)}) copy-start(bf16[128,4096]{1,0:T(8,128)(2,1)} %get-tuple-element.72) | copy-start | bytes 3145732
  610.2 3.0 copy-start.5
  615.5 2.3 copy-start.3
  615.5 2.4 copy-start.4
  617.9 2.3 copy-start
  620.2 1.6 copy-start.1
